TPU v7x, 32 devices: a whole 2x2x4 slice. The times are simulated.
32 devices in a mesh: shard: 4 (over z), ctx: 8 (over y, x, core).
Axes of the slice: x: 2, y: 2, z: 4, core: 2. Of those that a mesh axis runs over, the one named last changes fastest.
Arguments:
- tokens: bfloat16 [8, 1024, 512], P('shard', 'ctx'), may hold values from -6 to 6
- lengths: int32 [8], P('shard'), may hold values from 256 to 1024, as said below
- expert_picks: int32 [8, 1024, 8], P('shard', 'ctx'), may hold values from 0 to 23, all different within a row
- first_gain: float32 [512], P('shard'), may hold values from 0.5 to 1.5
- first_bias: float32 [512], P('shard'), may hold values from -0.625 to 0.625
- kv_weight: float32 [512, 128], P('shard'), may hold values from -0.25 to 0.25
- query_weight: float32 [512, 1536], P('shard'), may hold values from -0.25 to 0.25
- router_weight: float32 [512, 24], P('shard'), may hold values from -0.125 to 0.125
- output_weight: float32 [1536, 512], P('shard'), may hold values from -16 to 16
- second_gain: float32 [512], P('shard'), may hold values from 0.5 to 1.5
- second_bias: float32 [512], P('shard'), may hold values from -0.625 to 0.625
- inner_weight: float32 [512, 2048], P('shard'), may hold values from -0.25 to 0.25
- inner_bias: float32 [2048], P('shard'), may hold values from -1.25 to 1.25
- outer_weight: float32 [2048, 512], P('shard'), may hold values from -0.125 to 0.125
- outer_bias: float32 [512], P('shard'), may hold values from -1.25 to 1.25
- cotangent: bfloat16 [8, 1024, 512], P('shard', 'ctx'), may hold values from -6 to 6
Outputs:
- layer_out: bfloat16 [8, 1024, 512], P('shard', 'ctx')
- input_grad: float32 [8, 1024, 512], P('shard', 'ctx')
- first_gain_grad: float32 [512], P('shard')
- first_bias_grad: float32 [512], P('shard')
- kv_weight_grad: float32 [512, 128], P('shard')
- query_weight_grad: float32 [512, 1536], P('shard')
- router_weight_grad: float32 [512, 24], P('shard')
- output_weight_grad: float32 [1536, 512], P('shard')
- second_gain_grad: float32 [512], P('shard')
- second_bias_grad: float32 [512], P('shard')
- inner_weight_grad: float32 [512, 2048], P('shard')
- inner_bias_grad: float32 [2048], P('shard')
- outer_weight_grad: float32 [2048, 512], P('shard')
- outer_bias_grad: float32 [512], P('shard')
Inputs may be any that keep to these rules, and one draw needn't show every extreme that they name: `lengths`: of the 2 slots at each index of shard, one has length exactly 1024. `expert_picks`: each token names 8 different experts.
All inputs are finite; a program needn't handle non-finite values.
Results may differ from a plain program's by a relative error of at most 0.019.
Values may be sent and summed in bfloat16 or wider, within the bound.
A program may use at most 128 MiB of HBM per device.

v0:
```python
import jax
import jax.numpy as jnp
from jax import lax
from jax.sharding import PartitionSpec as P

HS = 64
E = 24
TOP = 8


NORM_EPS = 1e-05
PRECISE = lax.Precision.HIGHEST
NEG_LARGE = -1e30


def layer_norm(inputs, gain_vec, bias_vec):
    row_mean = jnp.mean(inputs, axis=-1, keepdims=True)
    centered = inputs - row_mean
    row_var = jnp.mean(centered * centered, axis=-1, keepdims=True)
    return centered * lax.rsqrt(row_var + NORM_EPS) * gain_vec + bias_vec


def gelu_tanh(inputs):
    return jax.nn.gelu(inputs, approximate=True)


def gate_softmax(inputs):
    return jax.nn.softmax(inputs, axis=-1)


def row_dot(left, right):
    return lax.dot_general(
        left, right, (((1,), (1,)), ((), ())), preferred_element_type=jnp.float32
    )


def col_dot(left, right):
    return lax.dot_general(
        left, right, (((0,), (0,)), ((), ())), preferred_element_type=jnp.float32
    )


def on_device(
    tokens,
    lengths,
    expert_picks,
    first_gain,
    first_bias,
    kv_weight,
    query_weight,
    router_weight,
    output_weight,
    second_gain,
    second_bias,
    inner_weight,
    inner_bias,
    outer_weight,
    outer_bias,
    cotangent,
):
    gathered = (
        lax.all_gather(first_gain.astype(jnp.bfloat16), "shard", axis=0, tiled=True),
        lax.all_gather(first_bias.astype(jnp.bfloat16), "shard", axis=0, tiled=True),
        lax.all_gather(kv_weight.astype(jnp.bfloat16), "shard", axis=0, tiled=True),
        lax.all_gather(query_weight.astype(jnp.bfloat16), "shard", axis=0, tiled=True),
        lax.all_gather(router_weight.astype(jnp.bfloat16), "shard", axis=0, tiled=True),
        lax.all_gather(output_weight.astype(jnp.bfloat16), "shard", axis=0, tiled=True),
        lax.all_gather(second_gain.astype(jnp.bfloat16), "shard", axis=0, tiled=True),
        lax.all_gather(second_bias.astype(jnp.bfloat16), "shard", axis=0, tiled=True),
        lax.all_gather(inner_weight.astype(jnp.bfloat16), "shard", axis=0, tiled=True),
        lax.all_gather(inner_bias.astype(jnp.bfloat16), "shard", axis=0, tiled=True),
        lax.all_gather(outer_weight.astype(jnp.bfloat16), "shard", axis=0, tiled=True),
        lax.all_gather(outer_bias.astype(jnp.bfloat16), "shard", axis=0, tiled=True),
    )
    (
        gain_one,
        bias_one,
        kv_low,
        query_low,
        router_low,
        output_low,
        gain_two,
        bias_two,
        inner_low,
        inner_bias_low,
        outer_low,
        outer_bias_low,
    ) = gathered
    gain_one = gain_one.astype(jnp.float32)
    bias_one = bias_one.astype(jnp.float32)
    gain_two = gain_two.astype(jnp.float32)
    bias_two = bias_two.astype(jnp.float32)
    inner_shift = inner_bias_low.astype(jnp.float32)
    outer_shift = outer_bias_low.astype(jnp.float32)
    slots_here, seg_rows, model_width = tokens.shape
    token_count = slots_here * seg_rows
    ctx_count = lax.axis_size("ctx")
    ctx_index = lax.axis_index("ctx")
    half_rows = seg_rows // 2
    slot_span = seg_rows * ctx_count
    half_count = half_rows * TOP
    offsets = jnp.arange(seg_rows, dtype=jnp.int32)
    token_pos = jnp.where(
        offsets < half_rows,
        ctx_index * half_rows + offsets,
        slot_span - (ctx_index + 2) * half_rows + offsets,
    )
    valid = (token_pos[None, :] < lengths[:, None]).astype(jnp.float32).reshape(token_count, 1)
    half_pos = jnp.repeat(token_pos, TOP).reshape(2, half_count)
    scale = HS ** (-0.5)

    def slot_blocks(key_val):
        slot_len = key_val.shape[0]
        block_len = min(512, slot_len)
        block_count = slot_len // block_len
        return (
            key_val.reshape(block_count, block_len, 2 * HS),
            jnp.arange(block_count, dtype=jnp.int32) * block_len,
        )

    def block_scores(query_rows, row_pos, key_block, key_begin, length):
        raw_scores = row_dot(query_rows, key_block[:, :HS]) * scale
        key_pos = key_begin + jnp.arange(key_block.shape[0], dtype=jnp.int32)
        allowed = (key_pos[None, :] <= row_pos[:, None]) & (key_pos[None, :] < length)
        return jnp.where(allowed, raw_scores, -jnp.inf)

    def forward_half(operands, key_blocks, begins, length):
        query_rows, row_pos = operands
        row_count = query_rows.shape[0]

        def stat_step(running, block_ops):
            key_block, key_begin = block_ops
            run_max, run_sum = running
            scores = block_scores(query_rows, row_pos, key_block, key_begin, length)
            new_max = jnp.maximum(run_max, jnp.max(scores, axis=1))
            new_sum = run_sum * jnp.exp(run_max - new_max) + jnp.sum(
                jnp.exp(scores - new_max[:, None]), axis=1
            )
            return ((new_max, new_sum), None)

        start_state = (
            jnp.full((row_count,), NEG_LARGE, jnp.float32),
            jnp.zeros((row_count,), jnp.float32),
        )
        (run_max, run_sum), unused = lax.scan(stat_step, start_state, (key_blocks, begins))
        positive = run_sum > 0.0
        log_total = jnp.where(positive, run_max + jnp.log(jnp.where(positive, run_sum, 1.0)), 0.0)

        def value_step(running, block_ops):
            key_block, key_begin = block_ops
            acc_main, acc_full = running
            scores = block_scores(query_rows, row_pos, key_block, key_begin, length)
            attn_prob = jnp.exp(scores - log_total[:, None])
            prob_low = attn_prob.astype(jnp.bfloat16)
            prob_rest = (attn_prob - prob_low.astype(jnp.float32)).astype(jnp.bfloat16)
            value_rows = key_block[:, HS:]
            part_main = jnp.dot(prob_low, value_rows, preferred_element_type=jnp.float32)
            part_rest = jnp.dot(prob_rest, value_rows, preferred_element_type=jnp.float32)
            return ((acc_main + part_main, acc_full + part_main + part_rest), None)

        zero_rows = jnp.zeros((row_count, HS), jnp.float32)
        (head_main, head_full), unused = lax.scan(
            value_step, (zero_rows, zero_rows), (key_blocks, begins)
        )
        return (head_main, head_full, log_total)

    def forward_slot(operands):
        query_halves, key_val, length = operands
        key_blocks, begins = slot_blocks(key_val)

        def forward_one_half(half_ops):
            return forward_half(half_ops, key_blocks, begins, length)

        return lax.map(forward_one_half, (query_halves, half_pos))

    def backward_half(operands, key_blocks, begins, length):
        query_rows, row_pos, log_total, grad_rows, row_delta = operands
        row_count = query_rows.shape[0]

        def grad_step(running, block_ops):
            key_block, key_begin = block_ops
            scores = block_scores(query_rows, row_pos, key_block, key_begin, length)
            attn_prob = jnp.exp(scores - log_total[:, None])
            prob_low = attn_prob.astype(jnp.bfloat16)
            key_rows = key_block[:, :HS]
            value_rows = key_block[:, HS:]
            grad_value = col_dot(prob_low, grad_rows)
            grad_prob = row_dot(grad_rows, value_rows)
            grad_score = (attn_prob * (grad_prob - row_delta[:, None])).astype(jnp.bfloat16)
            grad_query = jnp.dot(grad_score, key_rows, preferred_element_type=jnp.float32) * scale
            grad_key = col_dot(grad_score, query_rows) * scale
            part_kv = jnp.concatenate((grad_key, grad_value), axis=1)
            return (running + grad_query, part_kv)

        return lax.scan(grad_step, jnp.zeros((row_count, HS), jnp.float32), (key_blocks, begins))

    def backward_slot(operands):
        query_halves, key_val, length, log_halves, grad_halves, delta_halves = operands
        key_blocks, begins = slot_blocks(key_val)

        def backward_one_half(half_ops):
            return backward_half(half_ops, key_blocks, begins, length)

        grad_query, kv_parts = lax.map(
            backward_one_half, (query_halves, half_pos, log_halves, grad_halves, delta_halves)
        )
        return (grad_query, jnp.sum(kv_parts, axis=0).reshape(key_val.shape[0], 2 * HS))

    flat_in = tokens.reshape(token_count, model_width).astype(jnp.float32)
    normed_low = layer_norm(flat_in, gain_one, bias_one).astype(jnp.bfloat16)
    keyval_low = jnp.dot(normed_low, kv_low, preferred_element_type=jnp.float32).astype(
        jnp.bfloat16
    )
    query_all = (
        jnp.dot(normed_low, query_low, preferred_element_type=jnp.float32)
        .astype(jnp.bfloat16)
        .reshape(token_count, E, HS)
    )
    match = (
        expert_picks.reshape(token_count, TOP)[:, :, None]
        == jnp.arange(E, dtype=jnp.int32)[None, None, :]
    )
    one_hot_low = match.astype(jnp.bfloat16)
    one_hot = match.astype(jnp.float32)
    queries = jnp.einsum(
        "tje,ted->tjd", one_hot_low, query_all, preferred_element_type=jnp.float32
    ).astype(jnp.bfloat16)
    logits = jnp.dot(normed_low, router_low, preferred_element_type=jnp.float32)
    picked = jnp.einsum("tje,te->tj", one_hot, logits, precision=PRECISE)
    gate_probs = gate_softmax(picked)
    gathered_kv = lax.all_gather(
        keyval_low.reshape(slots_here, seg_rows, 2 * HS), "ctx", axis=1, tiled=True
    )
    dealt_kv = gathered_kv.reshape(slots_here, ctx_count, 2, half_rows, 2 * HS)
    keyval_all = jnp.concatenate((dealt_kv[:, :, 0], dealt_kv[:, ::-1, 1]), axis=1).reshape(
        slots_here, slot_span, 2 * HS
    )
    query_slots = queries.reshape(slots_here, 2, half_count, HS)
    head_main, head_full, log_total = lax.map(forward_slot, (query_slots, keyval_all, lengths))
    head_out = head_main.reshape(token_count, TOP, HS)
    mixed = jnp.einsum(
        "tje,tjd->ted", one_hot, gate_probs[:, :, None] * head_out, precision=PRECISE
    )
    mixed_low = mixed.reshape(token_count, E * HS).astype(jnp.bfloat16)
    residual = flat_in + jnp.dot(mixed_low, output_low, preferred_element_type=jnp.float32)
    normed_two_low = layer_norm(residual, gain_two, bias_two).astype(jnp.bfloat16)
    hidden = jnp.dot(normed_two_low, inner_low, preferred_element_type=jnp.float32) + inner_shift
    act_low = gelu_tanh(hidden).astype(jnp.bfloat16)
    final_sum = (
        residual + jnp.dot(act_low, outer_low, preferred_element_type=jnp.float32) + outer_shift
    )
    layer_out = (final_sum * valid).astype(jnp.bfloat16).reshape(tokens.shape)
    grad_final = cotangent.reshape(token_count, model_width).astype(jnp.float32) * valid
    grad_final_low = grad_final.astype(jnp.bfloat16)
    outer_grad = col_dot(act_low, grad_final_low)
    outer_bias_grad = jnp.sum(grad_final, axis=0)
    grad_act = row_dot(grad_final_low, outer_low)
    unused, gelu_pull = jax.vjp(gelu_tanh, hidden)
    grad_hidden_low = gelu_pull(grad_act)[0].astype(jnp.bfloat16)
    inner_grad = col_dot(normed_two_low, grad_hidden_low)
    inner_bias_grad = jnp.sum(grad_hidden_low.astype(jnp.float32), axis=0)
    grad_normed_two = row_dot(grad_hidden_low, inner_low)
    unused, norm_two_pull = jax.vjp(layer_norm, residual, gain_two, bias_two)
    grad_resid_part, second_gain_grad, second_bias_grad = norm_two_pull(grad_normed_two)
    grad_residual = grad_final + grad_resid_part
    grad_branch_low = grad_residual.astype(jnp.bfloat16)
    output_grad = col_dot(mixed_low, grad_branch_low)
    grad_mixed = row_dot(grad_branch_low, output_low).reshape(token_count, E, HS)
    grad_select = jnp.einsum("tje,ted->tjd", one_hot, grad_mixed, precision=PRECISE)
    grad_head_low = (gate_probs[:, :, None] * grad_select).astype(jnp.bfloat16)
    grad_gates = jnp.sum(grad_select * head_out, axis=-1)
    unused, gate_pull = jax.vjp(gate_softmax, picked)
    grad_picked = gate_pull(grad_gates)[0]
    grad_logits_low = jnp.einsum("tje,tj->te", one_hot, grad_picked, precision=PRECISE).astype(
        jnp.bfloat16
    )
    row_delta = jnp.sum(
        grad_head_low.astype(jnp.float32) * head_full.reshape(token_count, TOP, HS), axis=-1
    )
    grad_head_slots = grad_head_low.reshape(slots_here, 2, half_count, HS)
    grad_query_slots, grad_kv_slots = lax.map(
        backward_slot,
        (
            query_slots,
            keyval_all,
            lengths,
            log_total,
            grad_head_slots,
            row_delta.reshape(slots_here, 2, half_count),
        ),
    )
    natural_kv = grad_kv_slots.reshape(slots_here, 2 * ctx_count, half_rows, 2 * HS)
    dealt_grad = jnp.stack(
        (natural_kv[:, :ctx_count], natural_kv[:, ctx_count:][:, ::-1]), axis=2
    ).reshape(slots_here, slot_span, 2 * HS)
    grad_kv_sum = lax.psum_scatter(
        dealt_grad.astype(jnp.bfloat16), "ctx", scatter_dimension=1, tiled=True
    ).astype(jnp.float32)
    grad_kv_low = grad_kv_sum.reshape(token_count, 2 * HS).astype(jnp.bfloat16)
    grad_query_low = grad_query_slots.reshape(token_count, TOP, HS).astype(jnp.bfloat16)
    grad_query_all = jnp.einsum(
        "tje,tjd->ted", one_hot_low, grad_query_low, preferred_element_type=jnp.float32
    )
    grad_query_all = grad_query_all.astype(jnp.bfloat16).reshape(token_count, E * HS)
    query_grad = col_dot(normed_low, grad_query_all)
    kv_grad = col_dot(normed_low, grad_kv_low)
    router_grad = col_dot(normed_low, grad_logits_low)
    grad_normed = (
        row_dot(grad_query_all, query_low)
        + row_dot(grad_kv_low, kv_low)
        + row_dot(grad_logits_low, router_low)
    )
    unused, norm_one_pull = jax.vjp(layer_norm, flat_in, gain_one, bias_one)
    grad_in_part, first_gain_grad, first_bias_grad = norm_one_pull(grad_normed)
    input_grad = (grad_residual + grad_in_part).reshape(tokens.shape)
    shares = (
        lax.psum_scatter(
            first_gain_grad.astype(jnp.bfloat16), "shard", scatter_dimension=0, tiled=True
        ).astype(jnp.float32),
        lax.psum_scatter(
            first_bias_grad.astype(jnp.bfloat16), "shard", scatter_dimension=0, tiled=True
        ).astype(jnp.float32),
        lax.psum_scatter(
            kv_grad.astype(jnp.bfloat16), "shard", scatter_dimension=0, tiled=True
        ).astype(jnp.float32),
        lax.psum_scatter(
            query_grad.astype(jnp.bfloat16), "shard", scatter_dimension=0, tiled=True
        ).astype(jnp.float32),
        lax.psum_scatter(
            router_grad.astype(jnp.bfloat16), "shard", scatter_dimension=0, tiled=True
        ).astype(jnp.float32),
        lax.psum_scatter(
            output_grad.astype(jnp.bfloat16), "shard", scatter_dimension=0, tiled=True
        ).astype(jnp.float32),
        lax.psum_scatter(
            second_gain_grad.astype(jnp.bfloat16), "shard", scatter_dimension=0, tiled=True
        ).astype(jnp.float32),
        lax.psum_scatter(
            second_bias_grad.astype(jnp.bfloat16), "shard", scatter_dimension=0, tiled=True
        ).astype(jnp.float32),
        lax.psum_scatter(
            inner_grad.astype(jnp.bfloat16), "shard", scatter_dimension=0, tiled=True
        ).astype(jnp.float32),
        lax.psum_scatter(
            inner_bias_grad.astype(jnp.bfloat16), "shard", scatter_dimension=0, tiled=True
        ).astype(jnp.float32),
        lax.psum_scatter(
            outer_grad.astype(jnp.bfloat16), "shard", scatter_dimension=0, tiled=True
        ).astype(jnp.float32),
        lax.psum_scatter(
            outer_bias_grad.astype(jnp.bfloat16), "shard", scatter_dimension=0, tiled=True
        ).astype(jnp.float32),
    )
    totals = (
        lax.psum(shares[0].astype(jnp.bfloat16), "ctx").astype(jnp.float32),
        lax.psum(shares[1].astype(jnp.bfloat16), "ctx").astype(jnp.float32),
        lax.psum(shares[2].astype(jnp.bfloat16), "ctx").astype(jnp.float32),
        lax.psum(shares[3].astype(jnp.bfloat16), "ctx").astype(jnp.float32),
        lax.psum(shares[4].astype(jnp.bfloat16), "ctx").astype(jnp.float32),
        lax.psum(shares[5].astype(jnp.bfloat16), "ctx").astype(jnp.float32),
        lax.psum(shares[6].astype(jnp.bfloat16), "ctx").astype(jnp.float32),
        lax.psum(shares[7].astype(jnp.bfloat16), "ctx").astype(jnp.float32),
        lax.psum(shares[8].astype(jnp.bfloat16), "ctx").astype(jnp.float32),
        lax.psum(shares[9].astype(jnp.bfloat16), "ctx").astype(jnp.float32),
        lax.psum(shares[10].astype(jnp.bfloat16), "ctx").astype(jnp.float32),
        lax.psum(shares[11].astype(jnp.bfloat16), "ctx").astype(jnp.float32),
    )
    return (
        layer_out,
        input_grad,
        totals[0],
        totals[1],
        totals[2],
        totals[3],
        totals[4],
        totals[5],
        totals[6],
        totals[7],
        totals[8],
        totals[9],
        totals[10],
        totals[11],
    )


def solution(mesh):
    return jax.shard_map(
        on_device,
        mesh=mesh,
        in_specs=(
            P("shard", "ctx", None),
            P("shard"),
            P("shard", "ctx", None),
            P("shard"),
            P("shard"),
            P("shard", None),
            P("shard", None),
            P("shard", None),
            P("shard", None),
            P("shard"),
            P("shard"),
            P("shard", None),
            P("shard"),
            P("shard", None),
            P("shard"),
            P("shard", "ctx", None),
        ),
        out_specs=(
            P("shard", "ctx", None),
            P("shard", "ctx", None),
            P("shard"),
            P("shard"),
            P("shard", None),
            P("shard", None),
            P("shard", None),
            P("shard", None),
            P("shard"),
            P("shard"),
            P("shard", None),
            P("shard"),
            P("shard", None),
            P("shard"),
        ),
        check_vma=False,
    )
```

profile of v0, /device:TPU:0, one launch (start us, length us, event | category | flops | bytes accessed | tf_op | source)
XLA Modules:
  0.0 623.1 jit_solution(18068863298309178075)
XLA Ops:
  13.5 12.5 %all-gather.1 = bf16[4,1,128]{2,1,0:T(2,128)(2,1)S(1)} all-gather(bf16[1,1,128]{2,1,0:T(2,128)(2,1)S(1)} %convert_bitcast_fusion.3), channel_id=1, replica_groups=mesh['shard'=4,'ctx'=8] {'shard'}, dimensions={0}, use_global_device_ids=true | all-gather | bytes 1280 | tf_op jit(solution)/shard_map/all_gather | solution.py:63
  34.3 12.2 %all_gather.41 = bf16[512,24]{0,1:T(8,128)(2,1)S(1)} all-gather(bf16[128,24]{0,1:T(8,128)(2,1)S(1)} %convert_element_type.278), channel_id=1, replica_groups=mesh['shard'=4,'ctx'=8] {'shard'}, dimensions={0}, use_global_device_ids=true | all-gather | bytes 30720 | tf_op jit(solution)/shard_map/all_gather | solution.py:66
  50.0 13.4 %all_gather.43 = bf16[512,128]{1,0:T(8,128)(2,1)S(1)} all-gather(bf16[128,128]{1,0:T(8,128)(2,1)S(1)} %convert_element_type.282), channel_id=1, replica_groups=mesh['shard'=4,'ctx'=8] {'shard'}, dimensions={0}, use_global_device_ids=true | all-gather | bytes 163840 | tf_op jit(solution)/shard_map/all_gather | solution.py:64
  64.1 9.9 %all_gather.44 = bf16[2,1024,128]{2,1,0:T(8,128)(2,1)S(1)} all-gather(bf16[2,128,128]{2,1,0:T(8,128)(2,1)S(1)} %bitcast.337), channel_id=1, replica_groups=mesh['shard'=4,'ctx'=8] {'ctx'}, dimensions={1}, use_global_device_ids=true | all-gather | bytes 589824 | tf_op jit(solution)/shard_map/all_gather | solution.py:231
  74.1 12.1 %all-gather.4 = bf16[4,1,512]{2,1,0:T(2,128)(2,1)S(1)} all-gather(bf16[1,1,512]{2,1,0:T(2,128)(2,1)S(1)} %reshape.326), channel_id=1, replica_groups=mesh['shard'=4,'ctx'=8] {'shard'}, dimensions={0}, use_global_device_ids=true | all-gather | bytes 5120 | tf_op jit(solution)/shard_map/all_gather | solution.py:71
  95.2 9.4 %all-gather.2 = bf16[4,1,128]{2,1,0:T(2,128)(2,1)S(1)} all-gather(bf16[1,1,128]{2,1,0:T(2,128)(2,1)S(1)} %convert_bitcast_fusion.2), channel_id=1, replica_groups=mesh['shard'=4,'ctx'=8] {'shard'}, dimensions={0}, use_global_device_ids=true | all-gather | bytes 1280 | tf_op jit(solution)/shard_map/all_gather | solution.py:68
  116.3 80.9 %while.107 = (s32[]{:T(128)}, f32[2,2,512,64]{2,3,1,0:T(8,128)}, f32[2,2,512,64]{2,3,1,0:T(8,128)}, f32[2,2,512]{2,1,0:T(2,128)}, bf16[2,2,512,64]{3,2,1,0:T(8,1...) while((s32[]{:T(128)}, f32[2,2,512,64]{2,3,1,0:T(8,128)}, ...), condition=%wide.region_13.14_spmd.clone, body=%wide.region_4.13_spmd.clone.sunk | while | flops 138845696 | bytes 9811446 | solution.py:239
  119.0 35.7 %while.110 = (s32[]{:T(128)}, f32[2,512,64]{1,2,0:T(8,128)S(1)}, f32[2,512,64]{1,2,0:T(8,128)S(1)}, f32[2,512]{1,0:T(2,128)}, bf16[2,512,64]{2,1,0:T(8,128)(2,1)...) while((s32[]{:T(128)}, f32[2,512,64]{1,2,0:T(8,128)S(1)}, ...), condition=%wide.region_12.12_spmd.clone.clone, body=%wide.region_5.11_spmd.clone.clone.sunk | while | flops 138845696 | bytes 7955141 | solution.py:174
  159.4 35.6 %while.110 = (s32[]{:T(128)}, f32[2,512,64]{1,2,0:T(8,128)S(1)}, f32[2,512,64]{1,2,0:T(8,128)S(1)}, f32[2,512]{1,0:T(2,128)}, bf16[2,512,64]{2,1,0:T(8,128)(2,1)...) while((s32[]{:T(128)}, f32[2,512,64]{1,2,0:T(8,128)S(1)}, ...), condition=%wide.region_12.12_spmd.clone.clone, body=%wide.region_5.11_spmd.clone.clone.sunk | while | flops 138845696 | bytes 7955141 | solution.py:174
  232.7 68.0 %while.109 = (s32[]{:T(128)}, bf16[2,2,512,64]{2,3,1,0:T(8,128)(2,1)}, bf16[2,1024,128]{2,1,0:T(8,128)(2,1)}, bf16[2,2,512,64]{3,2,1,0:T(8,128)(2,1)S(1)}, f32[2...) while((s32[]{:T(128)}, ...), condition=%wide.region_25.26_spmd.clone, body=%wide.region_19.25_spmd.clone.sunk | while | flops 170460672 | bytes 24629792 | solution.py:281
  237.5 26.1 %while.111 = (s32[]{:T(128)}, bf16[2,512,64]{1,2,0:T(8,128)(2,1)S(1)}, f32[2,2,512,128]{2,3,1,0:T(8,128)}, bf16[2,512,64]{2,1,0:T(8,128)(2,1)S(1)}, s32[2,512]{1...) while((s32[]{:T(128)}, ...), condition=%wide.region_23.23_spmd.clone, body=%wide.region_20.22_spmd.clone.sunk | while | flops 170329600 | bytes 8281544 | solution.py:204
  239.4 10.3 %while.112 = (s32[]{:T(128)}, f32[512,64]{0,1:T(8,128)S(1)}, f32[2,512,128]{1,2,0:T(8,128)S(1)}, s32[2]{0:T(128)}, s32[512]{0:T(512)S(1)}, /*index=5*/s32[]{:T(1...) while((s32[]{:T(128)}, f32[512,64]{0,1:T(8,128)S(1)}, ...), condition=%wide.region_22.21_spmd.clone, body=%wide.region_21.20_spmd.clone.sunk | while | flops 170329600 | bytes 6696111 | solution.py:195
  252.5 10.3 %while.112 = (s32[]{:T(128)}, f32[512,64]{0,1:T(8,128)S(1)}, f32[2,512,128]{1,2,0:T(8,128)S(1)}, s32[2]{0:T(128)}, s32[512]{0:T(512)S(1)}, /*index=5*/s32[]{:T(1...) while((s32[]{:T(128)}, f32[512,64]{0,1:T(8,128)S(1)}, ...), condition=%wide.region_22.21_spmd.clone, body=%wide.region_21.20_spmd.clone.sunk | while | flops 170329600 | bytes 6696111 | solution.py:195
  271.5 26.1 %while.111 = (s32[]{:T(128)}, bf16[2,512,64]{1,2,0:T(8,128)(2,1)S(1)}, f32[2,2,512,128]{2,3,1,0:T(8,128)}, bf16[2,512,64]{2,1,0:T(8,128)(2,1)S(1)}, s32[2,512]{1...) while((s32[]{:T(128)}, ...), condition=%wide.region_23.23_spmd.clone, body=%wide.region_20.22_spmd.clone.sunk | while | flops 170329600 | bytes 8281544 | solution.py:204
  273.4 10.3 %while.112 = (s32[]{:T(128)}, f32[512,64]{0,1:T(8,128)S(1)}, f32[2,512,128]{1,2,0:T(8,128)S(1)}, s32[2]{0:T(128)}, s32[512]{0:T(512)S(1)}, /*index=5*/s32[]{:T(1...) while((s32[]{:T(128)}, f32[512,64]{0,1:T(8,128)S(1)}, ...), condition=%wide.region_22.21_spmd.clone, body=%wide.region_21.20_spmd.clone.sunk | while | flops 170329600 | bytes 6696111 | solution.py:195
  286.5 10.3 %while.112 = (s32[]{:T(128)}, f32[512,64]{0,1:T(8,128)S(1)}, f32[2,512,128]{1,2,0:T(8,128)S(1)}, s32[2]{0:T(128)}, s32[512]{0:T(512)S(1)}, /*index=5*/s32[]{:T(1...) while((s32[]{:T(128)}, f32[512,64]{0,1:T(8,128)S(1)}, ...), condition=%wide.region_22.21_spmd.clone, body=%wide.region_21.20_spmd.clone.sunk | while | flops 170329600 | bytes 6696111 | solution.py:195
  344.7 18.0 %reduce-scatter.22.cloned.1.call-done = bf16[128,24]{1,0:T(8,128)(2,1)} async-done(((bf16[512,24]{1,0:T(8,128)(2,1)}), bf16[128,24]{1,0:T(8,128)(2,1)}) %reduce-scatter.22.cloned.1.call-update) | async-done | bytes 6160
  363.9 34.7 %reduce-scatter.14.cloned.1.call-done = bf16[128,1536]{1,0:T(8,128)(2,1)} async-done(((bf16[512,1536]{1,0:T(8,128)(2,1)}), bf16[128,1536]{1,0:T(8,128)(2,1)}) %reduce-scatter.14.cloned.1.call-update) | async-done | bytes 393232 | tf_op jit(solution)/shard_map/reduce_scatter | solution.py:326
  398.6 36.6 %reduce-scatter.16.cloned.1.call-done = bf16[384,512]{1,0:T(8,128)(2,1)} async-done(((bf16[1536,512]{1,0:T(8,128)(2,1)}), bf16[384,512]{1,0:T(8,128)(2,1)}) %reduce-scatter.16.cloned.1.call-update) | async-done | bytes 393232 | tf_op jit(solution)/shard_map/reduce_scatter | solution.py:332
  435.2 45.2 %reduce-scatter.18.cloned.1.call-done = bf16[128,2048]{1,0:T(8,128)(2,1)} async-done(((bf16[512,2048]{1,0:T(8,128)(2,1)}), bf16[128,2048]{1,0:T(8,128)(2,1)}) %reduce-scatter.18.cloned.1.call-update) | async-done | bytes 524304 | tf_op jit(solution)/shard_map/reduce_scatter | solution.py:341
  480.3 45.5 %reduce-scatter.20.cloned.1.call-done = bf16[512,512]{1,0:T(8,128)(2,1)} async-done(((bf16[2048,512]{1,0:T(8,128)(2,1)}), bf16[512,512]{1,0:T(8,128)(2,1)}) %reduce-scatter.20.cloned.1.call-update) | async-done | bytes 524304 | tf_op jit(solution)/shard_map/reduce_scatter | solution.py:347
  526.6 10.2 %all-reduce.8 = (bf16[512]{0:T(512)(128)(2,1)S(1)}, bf16[512]{0:T(512)(128)(2,1)S(1)}, bf16[512]{0:T(512)(128)(2,1)S(1)}, bf16[512]{0:T(512)(128)(2,1)S(1)}, bf1...) all-reduce(bf16[512]{0:T(512)(128)(2,1)S(1)} %get-tuple-element.637, ...), channel_id=3, replica_groups=mesh['shard'=4,'ctx'=8] {'shard'}, use_global_device_ids=true, to_apply=%region_32.33.clone | all-reduce | flops 4608 | bytes 18432
  547.1 23.8 %all-reduce.6 = (bf16[128]{0:T(256)(128)(2,1)S(1)}, bf16[128]{0:T(256)(128)(2,1)S(1)}, bf16[128,128]{1,0:T(8,128)(2,1)S(1)}, bf16[128,24]{0,1:T(8,128)(2,1)S(1)}...) all-reduce(bf16[128]{0:T(256)(128)(2,1)S(1)} %dynamic-slice.1, ...), channel_id=1, replica_groups=mesh['shard'=4,'ctx'=8] {'ctx'}, use_global_device_ids=true, to_apply=%region_33.34 | all-reduce | flops 20608 | bytes 82432 | tf_op jit(solution)/shard_map/psum | solution.py:355
  575.3 34.8 %all-reduce.11.cloned.1.call-done = (bf16[128,1536]{1,0:T(8,128)(2,1)}, bf16[384,512]{1,0:T(8,128)(2,1)}, bf16[128,2048]{1,0:T(8,128)(2,1)}, bf16[512,512]{1,0:T(8,128)(2,1)}) async-done(((bf16[128,1536]{1,0:T(8,128)(2,1)}, bf16[384,512]{1,0:T(8,128)(2,1)}, bf16[128,2048]{1,0:T(8,128)(2,1)}, bf16[512,512]{1,0:T(8,128)(2,1)}), (bf16[128,1536]{1,0:T(8,128)(2,1)}, bf16[384,512]{1,0:T(8,128)(2,1)}, ...) | async-done | bytes 1835024 | tf_op jit(solution)/shard_map/psum | solution.py:358
  (703 shorter events, 349.2 us)
Async XLA Ops:
  7.2 101.1 %all-gather.11.cloned.1.call-start = ((), (), s32[]{:S(2)}) async-start(), calls=%async_computation.7 | async-start | bytes 1966080 | tf_op jit(solution)/shard_map/all_gather | solution.py:65
  9.3 199.6 %all-gather.13.cloned.1.call-start = ((), (), s32[]{:S(2)}) async-start(), calls=%async_computation.8 | async-start | bytes 1966080 | tf_op jit(solution)/shard_map/all_gather | solution.py:67
  10.2 201.1 %all-gather.17.cloned.1.call-start = ((), (), s32[]{:S(2)}) async-start(), calls=%async_computation.10 | async-start | bytes 2621440 | tf_op jit(solution)/shard_map/all_gather | solution.py:72
  11.2 203.9 %all-gather.15.cloned.1.call-start = ((), (), s32[]{:S(2)}) async-start(), calls=%async_computation.9 | async-start | bytes 2621440 | tf_op jit(solution)/shard_map/all_gather | solution.py:70
  12.1 328.6 %reduce-scatter.10.cloned.1.call-start = ((), (), s32[]{:S(2)}) async-start(), calls=%async_computation.11 | async-start | bytes 589824 | tf_op jit(solution)/shard_map/reduce_scatter | solution.py:296
  34.2 78.2 %copy-start.30 = (s32[256,8]{1,0:T(8,128)}, s32[256,8]{1,0:T(8,128)S(1)}, u32[]{:S(2)}) copy-start(s32[256,8]{1,0:T(8,128)S(1)} %copy.65) | copy-start | bytes 24580
  308.9 53.9 %reduce-scatter.22.cloned.1.call-start = ((), (), s32[]{:S(2)}) async-start(), calls=%async_computation.17 | async-start | bytes 163840
  311.4 87.1 %reduce-scatter.14.cloned.1.call-start = ((), (), s32[]{:S(2)}) async-start(), calls=%async_computation.13 | async-start | bytes 1966080 | tf_op jit(solution)/shard_map/reduce_scatter | solution.py:326
  313.4 121.7 %reduce-scatter.16.cloned.1.call-start = ((), (), s32[]{:S(2)}) async-start(), calls=%async_computation.14 | async-start | bytes 1966080 | tf_op jit(solution)/shard_map/reduce_scatter | solution.py:332
  315.3 165.0 %reduce-scatter.18.cloned.1.call-start = ((), (), s32[]{:S(2)}) async-start(), calls=%async_computation.15 | async-start | bytes 2621440 | tf_op jit(solution)/shard_map/reduce_scatter | solution.py:341
  318.9 206.9 %reduce-scatter.20.cloned.1.call-start = ((), (), s32[]{:S(2)}) async-start(), calls=%async_computation.16 | async-start | bytes 2621440 | tf_op jit(solution)/shard_map/reduce_scatter | solution.py:347
  322.9 224.2 %reduce-scatter.12.cloned.1.call-start = ((), (), s32[]{:S(2)}) async-start(), calls=%async_computation.12 | async-start | bytes 163840 | tf_op jit(solution)/shard_map/reduce_scatter | solution.py:323
  342.6 267.5 %all-reduce.11.cloned.1.call-start = ((), (), s32[]{:S(2)}) async-start(), calls=%async_computation.18 | async-start | bytes 3670016 | tf_op jit(solution)/shard_map/psum | solution.py:358
  344.7 181.1 %copy-start.4 = (bf16[2,128,512]{2,1,0:T(8,128)(2,1)S(1)}, bf16[2,128,512]{2,1,0:T(8,128)(2,1)}, u32[]{:S(2)}) copy-start(bf16[2,128,512]{2,1,0:T(8,128)(2,1)} %param.30) | copy-start | bytes 786436
  344.7 181.1 %copy-start.48 = (bf16[512,24]{0,1:T(8,128)(2,1)S(1)}, bf16[512,24]{0,1:T(8,128)(2,1)}, u32[]{:S(2)}) copy-start(bf16[512,24]{0,1:T(8,128)(2,1)} %copy-done.47) | copy-start | bytes 73732
  344.7 181.1 %copy-start.54 = (f32[4,1,128]{2,1,0:T(1,128)S(1)}, f32[4,1,128]{2,1,0:T(1,128)}, u32[]{:S(2)}) copy-start(f32[4,1,128]{2,1,0:T(1,128)} %copy-done.53) | copy-start | bytes 6148
  344.7 181.1 %copy-start.59 = (f32[256]{0:T(256)S(1)}, f32[256]{0:T(256)}, u32[]{:S(2)}) copy-start(f32[256]{0:T(256)} %copy-done.58) | copy-start | bytes 3076
  363.6 162.6 %copy-start.67 = (f32[2,128]{1,0:T(2,128)S(1)}, f32[2,128]{1,0:T(2,128)}, u32[]{:S(2)}) copy-start(f32[2,128]{1,0:T(2,128)} %copy-done.66) | copy-start | bytes 3076
  363.6 162.6 %copy-start.63 = (f32[256]{0:T(256)S(1)}, f32[256]{0:T(256)}, u32[]{:S(2)}) copy-start(f32[256]{0:T(256)} %copy-done.62) | copy-start | bytes 3076
  363.8 162.7 %copy-start.84 = (bf16[2048]{0:T(1024)(128)(2,1)S(1)}, bf16[2048]{0:T(1024)(128)(2,1)}, u32[]{:S(2)}) copy-start(bf16[2048]{0:T(1024)(128)(2,1)} %get-tuple-element.788) | copy-start | bytes 12292
  363.9 162.7 %copy-start.86 = (bf16[512]{0:T(512)(128)(2,1)S(1)}, bf16[512]{0:T(512)(128)(2,1)}, u32[]{:S(2)}) copy-start(bf16[512]{0:T(512)(128)(2,1)} %get-tuple-element.635) | copy-start | bytes 3076
  363.9 162.7 %copy-start.87 = (bf16[512]{0:T(512)(128)(2,1)S(1)}, bf16[512]{0:T(512)(128)(2,1)}, u32[]{:S(2)}) copy-start(bf16[512]{0:T(512)(128)(2,1)} %get-tuple-element.639) | copy-start | bytes 3076
  363.9 173.3 %copy-start.17 = (f32[256,512]{1,0:T(8,128)S(1)}, f32[256,512]{1,0:T(8,128)}, u32[]{:S(2)}) copy-start(f32[256,512]{1,0:T(8,128)} %copy-done.16) | copy-start | bytes 1572868
  363.9 173.3 %copy-start.75 = (f32[256]{0:T(256)S(1)}, f32[256]{0:T(256)}, u32[]{:S(2)}) copy-start(f32[256]{0:T(256)} %copy-done.74) | copy-start | bytes 3076
  (99 other events, 909.5 us)
Sparse Core Ops, SparseCore 0:
  10.2 40.5 all-gather.10
  52.4 36.2 all-gather.12
  90.2 44.8 all-gather.16
  136.5 44.4 all-gather.14
  309.0 31.7 reduce-scatter.9
  343.5 19.1 reduce-scatter.21
  365.0 33.4 reduce-scatter.13
  400.9 34.2 reduce-scatter.15
  437.5 42.8 reduce-scatter.17
  482.6 43.1 reduce-scatter.19
  528.6 18.4 reduce-scatter.11
  551.1 58.9 all-reduce.10
where the time goes:
time: 626 us; the launch traced here: 623 us
  waiting for transfers between devices  227 us (36%)
  blocking collectives  127 us (20%)
  local copies, waits for them, and re-layouts  89.1 us (14%)
  matrix products  80.6 us (13%)
  other arithmetic  79.8 us (13%)
  between operations  16.7 us (3%)
    reduce_scatter x1, waiting for transfers between devices, on_device(): lax.psum_scatter(outer_grad.astype(jnp.bfloat16), 'shard', scatter_dimens...  45.5 us
    reduce_scatter x1, waiting for transfers between devices, on_device(): lax.psum_scatter(inner_grad.astype(jnp.bfloat16), 'shard', scatter_dimens...  45.2 us
    reduce_scatter x1, waiting for transfers between devices, on_device(): lax.psum_scatter(output_grad.astype(jnp.bfloat16), 'shard', scatter_dimen...  36.6 us
    dynamic_slice x32, local copies, waits for them, and re-layouts, on_device(): lax.map(forward_slot, (query_slots, keyval_all, lengths))  35.3 us
    psum x1, waiting for transfers between devices, on_device(): lax.psum(shares[3].astype(jnp.bfloat16), 'ctx').astype(jnp.float32)  34.8 us
    reduce_scatter x1, waiting for transfers between devices, on_device(): lax.psum_scatter(query_grad.astype(jnp.bfloat16), 'shard', scatter_dimens...  34.7 us
    lt x24, other arithmetic, block_scores(): key_pos[None, :] < length  30.2 us
    psum x1, blocking collectives, on_device(): lax.psum(shares[0].astype(jnp.bfloat16), 'ctx').astype(jnp.float32)  23.8 us
  transfers between devices with their start and end apart: 12, of which 8 were waited for; matrix products, arithmetic and copies ran while one was open for 23% of the time, Pallas kernels for 0%

commit v1 on v0

v1 whole, which is shorter than its diff:
```python
import functools

import jax
import jax.numpy as jnp
from jax import lax
from jax.experimental import pallas as pl
from jax.experimental.pallas import tpu as pltpu
from jax.sharding import PartitionSpec as P

HS = 64
E = 24
TOP = 8
NORM_EPS = 1e-05
NEG_LARGE = -1e30
BF16 = jnp.bfloat16
F32 = jnp.float32
PANEL = 512
VMEM_BYTES = 63 * 1024 * 1024
GELU_C = 0.7978845608028654
GELU_A = 0.044715


def dot(left, right):
    return jnp.dot(left, right, preferred_element_type=F32)


def dot_t(left, right):
    return lax.dot_general(left, right, (((1,), (1,)), ((), ())), preferred_element_type=F32)


class Net:
    def __init__(self, shards, ctxs, group, send_sem, recv_sem):
        self.shards, self.ctxs, self.group = shards, ctxs, group
        self.pairs = group // 2
        self.groups = ctxs // group
        self.z = lax.axis_index("shard")
        self.i = lax.axis_index("ctx")
        self.core = self.i % 2
        self.chip = (self.i % group) // 2
        self.grp = self.i // group
        self.mine = self.core * self.pairs + self.chip
        self.send_sem, self.recv_sem = send_sem, recv_sem
        self.used = 0
        self.sent = []

    def far(self, step):
        return (self.z + step) % self.shards

    def src(self, step):
        return (self.z + self.shards - step) % self.shards

    def chip_to(self, step):
        return (self.chip + step) % self.pairs

    def chip_from(self, step):
        return (self.chip + self.pairs - step) % self.pairs

    def same_core(self, chip):
        return self.grp * self.group + chip * 2 + self.core

    def sibling(self):
        return self.i + 1 - 2 * self.core

    def slot(self):
        self.used += 1
        return self.used - 1

    def copy(self, src, dst, slot, z, i):
        return pltpu.make_async_remote_copy(
            src_ref=src,
            dst_ref=dst,
            send_sem=self.send_sem.at[slot],
            recv_sem=self.recv_sem.at[slot],
            device_id={"shard": z, "ctx": i},
            device_id_type=pl.DeviceIdType.MESH,
        )

    def send(self, src, dst, z, i):
        slot = self.slot()
        one = self.copy(src, dst, slot, z, i)
        one.start()
        self.sent.append(one)
        return slot

    def wait(self, slot, dst):
        self.copy(dst, dst, slot, self.z, self.i).wait_recv()

    def finish(self):
        for one in self.sent:
            one.wait_send()
        self.sent = []

    def greet(self):
        barrier = pltpu.get_barrier_semaphore()
        count = 0
        for step in range(1, self.ctxs):
            peer = (self.i + step) % self.ctxs
            pl.semaphore_signal(
                barrier,
                inc=1,
                device_id={"shard": self.z, "ctx": peer},
                device_id_type=pl.DeviceIdType.MESH,
            )
            count += 1
        for step in range(1, self.shards):
            pl.semaphore_signal(
                barrier,
                inc=1,
                device_id={"shard": self.far(step), "ctx": self.i},
                device_id_type=pl.DeviceIdType.MESH,
            )
            count += 1
        pl.semaphore_wait(barrier, count)


class Gather:
    def __init__(self, net, buf):
        self.net, self.buf = net, buf
        self.rows = buf.shape[1]
        self.piece = self.rows // net.group
        self.half = self.rows // 2

    def part(self, z, core, chip):
        first = pl.multiple_of((core * self.net.pairs + chip) * self.piece, self.piece)
        return self.buf.at[z, pl.ds(first, self.piece)]

    def core_part(self, z, core):
        return self.buf.at[z, pl.ds(pl.multiple_of(core * self.half, self.half), self.half)]

    def start(self):
        net = self.net
        own = self.part(net.z, net.core, net.chip)
        self.z_slots = [net.send(own, own, net.far(k), net.i) for k in range(1, net.shards)]

    def spread(self):
        net = self.net
        self.p_slots = []
        for k in range(1, net.shards):
            piece = self.part(net.src(k), net.core, net.chip)
            net.wait(self.z_slots[k - 1], piece)
            self.p_slots.append(
                [
                    net.send(piece, piece, net.z, net.same_core(net.chip_to(q)))
                    for q in range(1, net.pairs)
                ]
            )

    def share(self):
        net = self.net
        self.c_slots = []
        for k in range(1, net.shards):
            for q in range(1, net.pairs):
                net.wait(self.p_slots[k - 1][q - 1], self.part(net.src(k), net.core, net.chip_from(q)))
            block = self.core_part(net.src(k), net.core)
            self.c_slots.append(net.send(block, block, net.z, net.sibling()))

    def finish(self):
        net = self.net
        for k in range(1, net.shards):
            net.wait(self.c_slots[k - 1], self.core_part(net.src(k), 1 - net.core))


class Reduce:
    def __init__(self, net, grad, from_core, from_chip, from_group, from_far, out):
        self.net, self.grad = net, grad
        self.from_core, self.from_chip, self.from_group, self.from_far = (
            from_core,
            from_chip,
            from_group,
            from_far,
        )
        self.out = out
        self.rows, self.width = grad.shape[1], grad.shape[2]
        self.piece = self.rows // net.group
        self.half = self.rows // 2

    def first(self, core, chip):
        return pl.multiple_of((core * self.net.pairs + chip) * self.piece, self.piece)

    def core_rows(self, core):
        return pl.ds(pl.multiple_of(core * self.half, self.half), self.half)

    def start(self):
        net = self.net
        self.c_slot = net.send(
            self.grad.at[:, self.core_rows(1 - net.core)], self.from_core, net.z, net.sibling()
        )

    def add_core(self):
        net = self.net
        net.wait(self.c_slot, self.from_core)
        lines = 16
        base = pl.multiple_of(net.core * self.half, self.half)

        def one(step, carry):
            at = pl.multiple_of(step * lines, lines)
            rows = pl.ds(pl.multiple_of(base + at, lines), lines)
            for z in range(net.shards):
                self.grad[z, rows] = (
                    self.grad[z, rows].astype(F32)
                    + self.from_core[z, pl.ds(at, lines)].astype(F32)
                ).astype(BF16)
            return carry

        lax.fori_loop(0, self.half // lines, one, 0)
        self.p_slots = [
            net.send(
                self.grad.at[:, pl.ds(self.first(net.core, net.chip_to(q)), self.piece)],
                self.from_chip.at[q - 1],
                net.z,
                net.same_core(net.chip_to(q)),
            )
            for q in range(1, net.pairs)
        ]

    def total(self, parts):
        net = self.net
        lines = 16
        base = self.first(net.core, net.chip)

        def one(step, carry):
            at = pl.multiple_of(step * lines, lines)
            rows = pl.ds(pl.multiple_of(base + at, lines), lines)
            for z in range(net.shards):
                value = self.grad[z, rows].astype(F32)
                for part in range(parts.shape[0]):
                    value = value + parts[part, z, pl.ds(at, lines)].astype(F32)
                self.grad[z, rows] = value.astype(BF16)
            return carry

        lax.fori_loop(0, self.piece // lines, one, 0)

    def add_chip(self):
        net = self.net
        for q in range(1, net.pairs):
            net.wait(self.p_slots[q - 1], self.from_chip.at[q - 1])
        self.total(self.from_chip)
        own = pl.ds(self.first(net.core, net.chip), self.piece)
        step, at = 1, 0
        while step < net.groups:
            peer = net.i + net.group * step * (1 - 2 * ((net.grp // step) % 2))
            slot = net.send(self.grad.at[:, own], self.from_group.at[at], net.z, peer)
            net.wait(slot, self.from_group.at[at])
            net.sent.pop().wait_send()
            self.total(self.from_group.at[at : at + 1])
            step, at = step * 2, at + 1
        self.z_slots = [
            net.send(self.grad.at[net.far(k), own], self.from_far.at[k - 1], net.far(k), net.i)
            for k in range(1, net.shards)
        ]

    def add_far(self):
        net = self.net
        for k in range(1, net.shards):
            net.wait(self.z_slots[k - 1], self.from_far.at[k - 1])
        own = pl.ds(self.first(net.core, net.chip), self.piece)
        value = self.grad[net.z, own].astype(F32)
        for k in range(1, net.shards):
            value = value + self.from_far[k - 1].astype(F32)
        self.out[own, :] = value.astype(BF16)
        piece = self.out.at[own]
        self.o_slots = [
            net.send(piece, piece, net.z, net.same_core(net.chip_to(q))) for q in range(1, net.pairs)
        ]

    def share(self):
        net = self.net
        for q in range(1, net.pairs):
            net.wait(
                self.o_slots[q - 1],
                self.out.at[pl.ds(self.first(net.core, net.chip_from(q)), self.piece)],
            )
        block = self.out.at[self.core_rows(net.core)]
        self.s_slot = net.send(block, block, net.z, net.sibling())

    def finish(self):
        net = self.net
        net.wait(self.s_slot, self.out.at[self.core_rows(1 - net.core)])


def layer_kernel(
    shards,
    ctxs,
    group,
    len_ref,
    x_ref,
    cot_ref,
    picks_ref,
    g1_ref,
    b1_ref,
    g2_ref,
    b2_ref,
    bo_ref,
    bi_ref,
    wq_hbm,
    wkv_hbm,
    wr_hbm,
    wo_hbm,
    wi_hbm,
    wout_hbm,
    out_ref,
    gin_ref,
    two_out,
    q_out,
    kv_out,
    vec_out,
    wq_st,
    wkv_st,
    wr_st,
    wi_st,
    stage,
    w1,
    w2,
    vecs,
    normed,
    normed_t,
    q_t,
    sel_a,
    heads_t,
    small,
    kvall,
    kvt,
    qpad,
    ghpad,
    hrow,
    linv,
    ebuf,
    dkv,
    from_kv,
    mixed_t,
    xhat2,
    n2,
    n2_t,
    gfin_low,
    biases,
    g_t,
    two_g,
    two_core,
    two_chip,
    two_group,
    two_far,
    qg,
    qg_core,
    qg_chip,
    qg_group,
    qg_far,
    kg,
    kg_core,
    kg_chip,
    kg_group,
    kg_far,
    vec_g,
    vec_near,
    vec_far,
    local_sem,
    send_sem,
    recv_sem,
):
    net = Net(shards, ctxs, group, send_sem, recv_sem)
    z, c = net.z, net.i
    tokens, width = x_ref.shape
    seg = tokens // 2
    half = seg // 2
    blocks = 2 * ctxs
    ws = width // shards
    wos = E * HS // shards
    fs = wout_hbm.shape[0]
    off_out = wos
    off_in = wos + fs
    scale = HS ** (-0.5)
    panels = 4
    chunks = fs * shards // PANEL
    per_chunk = PANEL // fs

    wo_st, wout_st = stage.at[0:wos], stage.at[wos : wos + fs]
    resid, acc_a, acc_b = (stage.at[k * tokens : (k + 1) * tokens] for k in range(3))
    loads = []
    for at, (src, dst) in enumerate(
        (
            (wq_hbm, wq_st),
            (wkv_hbm, wkv_st),
            (wr_hbm, wr_st),
            (wo_hbm, wo_st),
            (wi_hbm, wi_st),
            (wout_hbm, wout_st),
        )
    ):
        one = pltpu.make_async_copy(src, dst, local_sem.at[at])
        one.start()
        loads.append(one)

    own_vec = vecs.at[z]
    own_vec[...] = jnp.zeros(own_vec.shape, F32)
    for row, ref in enumerate((g1_ref, b1_ref, g2_ref, b2_ref, bo_ref, bi_ref)):
        own_vec[row : row + 1, 0 : ref.shape[1]] = ref[...].astype(BF16).astype(F32)
    for one in loads[:3]:
        one.wait()
    w1[z, :, 0 : E * HS] = wq_st[...].astype(BF16)
    w1[z, :, E * HS : E * HS + 2 * HS] = wkv_st[...].astype(BF16)
    w1[z, :, E * HS + 2 * HS :] = jnp.zeros((ws, 128), BF16)
    w1[z, :, E * HS + 2 * HS : E * HS + 2 * HS + E] = wr_st[...].astype(BF16)

    net.greet()
    first_gather = Gather(net, w1)
    first_gather.start()
    vec_slots = [net.send(own_vec, own_vec, net.far(k), net.i) for k in range(1, shards)]
    for one in loads[3:]:
        one.wait()
    w2[z, 0:wos] = wo_st[...].astype(BF16)
    w2[z, off_out : off_out + fs] = wout_st[...].astype(BF16)
    for panel in range(panels):
        w2[z, off_in + panel * ws : off_in + (panel + 1) * ws] = wi_st[
            :, panel * PANEL : (panel + 1) * PANEL
        ].astype(BF16)
    second_gather = Gather(net, w2)
    second_gather.start()

    x = x_ref[...].astype(F32)
    mean1 = jnp.mean(x, axis=1, keepdims=True)
    cen = x - mean1
    small[0, :, 0:1] = lax.rsqrt(jnp.mean(cen * cen, axis=1, keepdims=True) + NORM_EPS)
    small[0, :, 2:3] = mean1

    def first_hat():
        return (x_ref[...].astype(F32) - small[0, :, 2:3]) * small[0, :, 0:1]

    first_gather.spread()
    for k in range(1, shards):
        net.wait(vec_slots[k - 1], vecs.at[net.src(k)])

    def whole(row, part):
        return jnp.concatenate([vecs[s, row : row + 1, 0:part] for s in range(shards)], axis=1)

    gain1, bias1 = whole(0, ws), whole(1, ws)
    gain2, bias2, bias_out = whole(2, ws), whole(3, ws), whole(4, ws)
    bias_in = whole(5, fs)
    for chunk in range(chunks):
        biases[chunk : chunk + 1, :] = bias_in[:, chunk * PANEL : (chunk + 1) * PANEL]
    norm_value = first_hat() * gain1 + bias1
    normed[...] = norm_value.astype(BF16)
    normed_t[...] = norm_value.T.astype(BF16)
    first_gather.share()
    first_gather.finish()

    def w1_tile(first, size):
        return w1[:, :, first : first + size].reshape(width, size)

    kvr = dot(normed[...], w1_tile(E * HS, 256))
    kv_own = kvr[:, 0 : 2 * HS].astype(BF16)
    for h in range(2):
        block = c if h == 0 else blocks - 1 - c
        for s in range(2):
            kvall[block, s] = kv_own[s * seg + h * half : s * seg + (h + 1) * half]
    kv_slots = []
    for step in range(1, ctxs):
        peer = (c + step) % ctxs
        pair = []
        for h in range(2):
            ref = kvall.at[c if h == 0 else blocks - 1 - c]
            pair.append(net.send(ref, ref, z, peer))
        kv_slots.append(pair)
    kv_sent = net.sent[-2 * (ctxs - 1) :]
    del net.sent[-2 * (ctxs - 1) :]

    second_gather.spread()

    logits_t = kvr[:, 2 * HS : 2 * HS + 128].T
    eye = (
        lax.broadcasted_iota(jnp.int32, (TOP, TOP), 0)
        == lax.broadcasted_iota(jnp.int32, (TOP, TOP), 1)
    ).astype(F32)
    picks = dot_t(eye, picks_ref[...].astype(F32))
    small_p = jnp.full((TOP, tokens), 0.0, F32)
    for e in range(E):
        small_p = jnp.where(picks == float(e), logits_t[e : e + 1, :], small_p)
    top = jnp.max(small_p, axis=0, keepdims=True)
    gexp = jnp.exp(small_p - top)
    gates = gexp / jnp.sum(gexp, axis=0, keepdims=True)
    small[1, 0:TOP, 0:tokens] = gates
    small[1, TOP : 2 * TOP, 0:tokens] = picks

    def query_tile(n, carry):
        cols = pl.ds(pl.multiple_of(n * 256, 256), 256)
        value = dot(normed[...], w1[:, :, cols].reshape(width, 256))
        value = value.astype(BF16).astype(F32).T
        for k in range(4):
            q_t[n * 4 + k] = value[k * HS : (k + 1) * HS]
        return carry

    lax.fori_loop(0, E * HS // 256, query_tile, 0)

    def choose(src, store):
        def one(j, carry):
            pick = small[1, pl.ds(TOP + j, 1), 0:tokens]
            value = jnp.zeros((HS, tokens), F32)
            for e in range(E):
                value = jnp.where(pick == float(e), src[e], value)
            store(j, value)
            return carry

        lax.fori_loop(0, TOP, one, 0)

    def spread_back(src, store):
        def one(e, carry):
            value = jnp.zeros((HS, tokens), F32)
            for j in range(TOP):
                pick = small[1, TOP + j : TOP + j + 1, 0:tokens]
                value = jnp.where(pick == e.astype(F32), src[j], value)
            store(e, value)
            return carry

        lax.fori_loop(0, E, one, 0)

    low_lane = lax.broadcasted_iota(jnp.int32, (HS, 2 * half), 1) < half

    def swap(one, two):
        return (
            jnp.where(low_lane, one, pltpu.roll(two, half, 1)),
            jnp.where(low_lane, pltpu.roll(one, half, 1), two),
        )

    def store_query(j, value):
        sel_a[j] = value * scale

    choose(q_t, store_query)
    for s in range(2):
        for pair in range(TOP // 2):
            halves = swap(
                sel_a[2 * pair, :, s * seg : (s + 1) * seg],
                sel_a[2 * pair + 1, :, s * seg : (s + 1) * seg],
            )
            for h in range(2):
                qpad[2 * s + h, 0:HS, pair * 128 : (pair + 1) * 128] = halves[h].astype(BF16)
    for sh in range(4):
        qpad[sh, HS:, :] = jnp.zeros((HS, TOP * half), BF16)
        ghpad[sh, 0:HS, :] = jnp.zeros((HS, TOP * half), BF16)

    for step in range(1, ctxs):
        source = (c + ctxs - step) % ctxs
        net.wait(kv_slots[step - 1][0], kvall.at[source])
        net.wait(kv_slots[step - 1][1], kvall.at[blocks - 1 - source])

    def turn(block, carry):
        both = kvall[block].reshape(2 * half, 2 * HS)
        kvt[block] = both.astype(F32).T.astype(BF16)
        dkv[block] = jnp.zeros((2, half, 2 * HS), F32)
        return carry

    lax.fori_loop(0, blocks, turn, 0)

    lanes = TOP * half
    offset = lax.broadcasted_iota(jnp.int32, (1, lanes), 1) % half
    key_row = lax.broadcasted_iota(jnp.int32, (half, lanes), 0)

    def place(h):
        if h == 0:
            return c, c + 1, blocks - c
        return blocks - 1 - c, blocks - c, 0

    def fold(value, op):
        parts = [value[8 * k : 8 * k + 8] for k in range(half // 8)]
        while len(parts) > 1:
            parts = [op(parts[k], parts[k + 1]) for k in range(0, len(parts), 2)]
        return parts[0]

    def masked(block, s, sh, limit):
        scores = dot(kvall[block, s], qpad[sh])
        return jnp.where(key_row <= limit - block * half, scores, NEG_LARGE)

    for s in range(2):
        length = len_ref[s]
        for h in range(2):
            sh = 2 * s + h
            position, count, base = place(h)
            limit = jnp.minimum(position * half + offset, length - 1)

            def score_step(block, top, s=s, sh=sh, limit=limit):
                return jnp.maximum(top, fold(masked(block, s, sh, limit), jnp.maximum))

            top = lax.fori_loop(0, count, score_step, jnp.full((8, lanes), NEG_LARGE, F32))
            top = jnp.max(top, axis=0, keepdims=True)
            acc_a[0:HS, :] = jnp.zeros((HS, lanes), F32)

            def value_step(block, total, s=s, sh=sh, limit=limit, top=top, base=base):
                expd = jnp.exp(masked(block, s, sh, limit) - top)
                low = expd.astype(BF16)
                ebuf[s, base + block] = low
                acc_a[0:HS, :] += dot(kvt[block, HS:, s * half : (s + 1) * half], low)
                return total + fold(expd, jnp.add)

            total = lax.fori_loop(0, count, value_step, jnp.zeros((8, lanes), F32))
            inverse = 1.0 / jnp.sum(total, axis=0, keepdims=True)
            linv[sh] = jnp.broadcast_to(inverse, (8, lanes))
            hrow[sh] = acc_a[0:HS, :] * inverse
    second_gather.share()

    for s in range(2):
        for pair in range(TOP // 2):
            both = swap(
                hrow[2 * s, :, pair * 128 : (pair + 1) * 128],
                hrow[2 * s + 1, :, pair * 128 : (pair + 1) * 128],
            )
            for k in range(2):
                heads_t[2 * pair + k, :, s * seg : (s + 1) * seg] = both[k]
    for j in range(TOP):
        sel_a[j] = heads_t[j] * small[1, j : j + 1, 0:tokens]

    def store_mixed(e, value):
        mixed_t[e] = value.astype(BF16)

    spread_back(sel_a, store_mixed)
    second_gather.finish()

    experts = E // shards
    acc_a[...] = x_ref[...].astype(F32)

    def project(s, carry):
        part = mixed_t[pl.ds(s * experts, experts)].reshape(wos, tokens)
        acc_a[...] += dot(part.astype(F32).T.astype(BF16), w2[s, 0:wos])
        return carry

    lax.fori_loop(0, shards, project, 0)
    residual = acc_a[...]
    resid[...] = residual
    cen = residual - jnp.mean(residual, axis=1, keepdims=True)
    rstd2 = lax.rsqrt(jnp.mean(cen * cen, axis=1, keepdims=True) + NORM_EPS)
    small[0, :, 1:2] = rstd2
    cen = cen * rstd2
    xhat2[...] = cen
    cen = cen * gain2 + bias2
    n2[...] = cen.astype(BF16)
    n2_t[...] = cen.T.astype(BF16)

    row = lax.broadcasted_iota(jnp.int32, (tokens, 1), 0)
    inner_row = row % seg
    pos = jnp.where(
        inner_row < half, c * half + inner_row, blocks * half - (c + 2) * half + inner_row
    )
    valid = (pos < jnp.where(row < seg, len_ref[0], len_ref[1])).astype(F32)
    gfin_low[...] = (cot_ref[...].astype(F32) * valid).astype(BF16)
    acc_a[...] = jnp.zeros((tokens, width), F32)
    acc_b[...] = jnp.zeros((tokens, width), F32)
    vec_g[...] = jnp.zeros(vec_g.shape, F32)

    def feed(f, carry):
        rows_in = pl.ds(pl.multiple_of(off_in + f * ws, 16), ws)
        w_in = w2[:, rows_in].reshape(width, PANEL)
        w_out = w2[pl.ds(f * per_chunk, per_chunk), off_out : off_out + fs].reshape(PANEL, width)
        hidden = dot(n2[...], w_in) + biases[pl.ds(f, 1), :]
        square = hidden * hidden
        tanh = jnp.tanh(GELU_C * hidden * (1.0 + GELU_A * square))
        act = (0.5 * hidden * (1.0 + tanh)).astype(BF16)
        slope = 0.5 * (1.0 + tanh) + 0.5 * GELU_C * hidden * (1.0 - tanh * tanh) * (
            1.0 + 3.0 * GELU_A * square
        )
        gfin = gfin_low[...]
        acc_a[...] += dot(act, w_out)
        grad_hidden = (slope * dot_t(gfin, w_out)).astype(BF16)
        vec_g[pl.ds(5 + f, 1), :] = jnp.sum(grad_hidden.astype(F32), axis=0, keepdims=True)
        grad_outer = dot(act.astype(F32).T.astype(BF16), gfin).astype(BF16)
        two_g[pl.ds(f * per_chunk, per_chunk), off_out : off_out + fs] = grad_outer.reshape(
            per_chunk, fs, width
        )
        grad_inner = dot(n2_t[...], grad_hidden).astype(BF16)
        two_g[:, rows_in] = grad_inner.reshape(shards, ws, PANEL)
        acc_b[...] += dot_t(grad_hidden, w_in)
        return carry

    lax.fori_loop(0, chunks, feed, 0)
    out_ref[...] = (valid * (resid[...] + acc_a[...] + bias_out)).astype(BF16)
    gfin = cot_ref[...].astype(F32) * valid
    vec_g[4:5, :] = jnp.sum(gfin, axis=0, keepdims=True)
    grad_n2 = acc_b[...]
    vec_g[3:4, :] = jnp.sum(grad_n2, axis=0, keepdims=True)
    vec_g[2:3, :] = jnp.sum(grad_n2 * xhat2[...], axis=0, keepdims=True)
    grad_hat = grad_n2 * gain2
    grad_hat = grad_hat - jnp.mean(grad_hat, axis=1, keepdims=True)
    grad_hat = grad_hat - xhat2[...] * jnp.mean(grad_hat * xhat2[...], axis=1, keepdims=True)
    grad_residual = gfin + grad_hat * small[0, :, 1:2]
    resid[...] = grad_residual
    n2[...] = grad_residual.astype(BF16)

    def branch(s, carry):
        part = mixed_t[pl.ds(s * experts, experts)].reshape(wos, tokens)
        two_g[s, 0:wos] = dot(part, n2[...]).astype(BF16)
        grad = dot_t(w2[s, 0:wos], n2[...])
        q_t[pl.ds(s * experts, experts)] = grad.reshape(experts, HS, tokens)
        return carry

    lax.fori_loop(0, shards, branch, 0)
    two = Reduce(net, two_g, two_core, two_chip, two_group, two_far, two_out)
    two.start()

    def store_head_grad(j, value):
        sel_a[j] = value * small[1, pl.ds(j, 1), 0:tokens]
        small[1, pl.ds(2 * TOP + j, 1), 0:tokens] = jnp.sum(
            value * heads_t[j], axis=0, keepdims=True
        )

    choose(q_t, store_head_grad)
    gates = small[1, 0:TOP, 0:tokens]
    grad_gates = small[1, 2 * TOP : 3 * TOP, 0:tokens]
    grad_picked = gates * (grad_gates - jnp.sum(gates * grad_gates, axis=0, keepdims=True))
    picks = small[1, TOP : 2 * TOP, 0:tokens]
    g_t[E * HS + 2 * HS :, :] = jnp.zeros((128, tokens), BF16)
    grad_logits = [
        jnp.sum(jnp.where(picks == float(e), grad_picked, 0.0), axis=0, keepdims=True)
        for e in range(E)
    ]
    grad_logits += [jnp.zeros((1, tokens), F32)] * (32 - E)
    g_t[E * HS + 2 * HS : E * HS + 2 * HS + 32, :] = jnp.concatenate(grad_logits, axis=0).astype(
        BF16
    )
    for s in range(2):
        for pair in range(TOP // 2):
            halves = swap(
                sel_a[2 * pair, :, s * seg : (s + 1) * seg],
                sel_a[2 * pair + 1, :, s * seg : (s + 1) * seg],
            )
            at = pair * 128
            for h in range(2):
                sh = 2 * s + h
                grad = (halves[h] * linv[sh, 0:1, at : at + 128]).astype(BF16)
                ghpad[sh, HS:, at : at + 128] = grad
                linv[sh, 1:2, at : at + 128] = jnp.sum(
                    grad.astype(F32) * hrow[sh, :, at : at + 128], axis=0, keepdims=True
                )
    two.add_core()

    for s in range(2):
        for h in range(2):
            sh = 2 * s + h
            position, count, base = place(h)
            delta = linv[sh, 1:2, :]
            acc_a[0:HS, :] = jnp.zeros((HS, lanes), F32)

            def grad_step(block, carry, s=s, sh=sh, base=base, delta=delta):
                expd = ebuf[s, base + block]
                grad_prob = dot(kvall[block, s], ghpad[sh])
                grad_score = (expd.astype(F32) * (grad_prob - delta)).astype(BF16)
                dkv[block, s] += dot_t(expd, ghpad[sh]) + dot_t(grad_score, qpad[sh])
                acc_a[0:HS, :] += dot(kvt[block, 0:HS, s * half : (s + 1) * half], grad_score)
                return carry

            lax.fori_loop(0, count, grad_step, 0)
            hrow[sh] = acc_a[0:HS, :] * scale

    for one in kv_sent:
        one.wait_send()

    def lower(block, carry):
        kvall[block] = dkv[block].astype(BF16)
        return carry

    lax.fori_loop(0, blocks, lower, 0)
    dkv_slots = []
    for step in range(1, ctxs):
        peer = (c + step) % ctxs
        pair = []
        for h in range(2):
            ref = kvall.at[peer if h == 0 else blocks - 1 - peer]
            pair.append(net.send(ref, from_kv.at[step - 1, h], z, peer))
        dkv_slots.append(pair)

    for s in range(2):
        for pair in range(TOP // 2):
            both = swap(
                hrow[2 * s, :, pair * 128 : (pair + 1) * 128],
                hrow[2 * s + 1, :, pair * 128 : (pair + 1) * 128],
            )
            for k in range(2):
                q_t[2 * pair + k, :, s * seg : (s + 1) * seg] = both[k]

    def store_grad_query(e, value):
        g_t[pl.ds(pl.multiple_of(e * HS, HS), HS), :] = value.astype(BF16)

    spread_back(q_t, store_grad_query)

    def query_grad(n, carry):
        at = pl.ds(pl.multiple_of(n * 256, 256), 256)
        grad = dot_t(normed_t[...], g_t[at, :]).astype(BF16)
        qg[:, :, at] = grad.reshape(shards, ws, 256)
        return carry

    lax.fori_loop(0, E * HS // 256, query_grad, 0)
    first_q = Reduce(net, qg, qg_core, qg_chip, qg_group, qg_far, q_out)
    first_q.start()
    two.add_chip()

    heads_t[...] = jnp.zeros(heads_t.shape, F32)

    def norm_grad(n, carry):
        at = pl.ds(pl.multiple_of(n * 256, 256), 256)
        part = dot(w1[:, :, at].reshape(width, 256), g_t[at, :])
        heads_t[...] += part.reshape(heads_t.shape)
        return carry

    lax.fori_loop(0, E * HS // 256, norm_grad, 0)
    first_q.add_core()

    for step in range(1, ctxs):
        for h in range(2):
            net.wait(dkv_slots[step - 1][h], from_kv.at[step - 1, h])
    for h in range(2):
        block = c if h == 0 else blocks - 1 - c
        value = dkv[block]
        for step in range(1, ctxs):
            value = value + from_kv[step - 1, h].astype(F32)
        for s in range(2):
            acc_a[s * seg + h * half : s * seg + (h + 1) * half, 0:128] = value[s]
    g_t[E * HS : E * HS + 2 * HS, :] = acc_a[:, 0:128].T.astype(BF16)
    tail = g_t[E * HS :, :]
    kg[...] = dot_t(normed_t[...], tail).astype(BF16).reshape(shards, ws, 256)
    first_kv = Reduce(net, kg, kg_core, kg_chip, kg_group, kg_far, kv_out)
    first_kv.start()
    part = heads_t[...].reshape(width, tokens) + dot(w1_tile(E * HS, 256), tail)
    grad_normed = part.T
    vec_g[1:2, :] = jnp.sum(grad_normed, axis=0, keepdims=True)
    hat = first_hat()
    vec_g[0:1, :] = jnp.sum(grad_normed * hat, axis=0, keepdims=True)
    vec_slots = []
    for step in range(1, ctxs):
        vec_slots.append(net.send(vec_g, vec_near.at[step - 1], z, (c + step) % ctxs))
    vec_sent = net.sent[-(ctxs - 1) :]
    del net.sent[-(ctxs - 1) :]
    grad_hat = grad_normed * gain1
    grad_hat = grad_hat - jnp.mean(grad_hat, axis=1, keepdims=True)
    grad_hat = grad_hat - hat * jnp.mean(grad_hat * hat, axis=1, keepdims=True)
    gin_ref[...] = resid[...] + grad_hat * small[0, :, 0:1]

    two.add_far()
    first_kv.add_core()
    for step in range(1, ctxs):
        net.wait(vec_slots[step - 1], vec_near.at[step - 1])
    for one in vec_sent:
        one.wait_send()
    value = vec_g[...]
    for step in range(1, ctxs):
        value = value + vec_near[step - 1]
    vec_g[...] = value
    far_slots = [
        net.send(vec_g, vec_far.at[k - 1], net.far(k), net.i) for k in range(1, shards)
    ]
    first_q.add_chip()
    two.share()
    first_kv.add_chip()
    for k in range(1, shards):
        net.wait(far_slots[k - 1], vec_far.at[k - 1])
    value = vec_g[...]
    for k in range(1, shards):
        value = value + vec_far[k - 1]
    first_kv.add_far()
    first_q.add_far()
    vec_out[...] = jnp.zeros(vec_out.shape, F32)
    for at in range(5):
        part = jnp.zeros((1, ws), F32)
        for s in range(shards):
            part = jnp.where(z == s, value[at : at + 1, s * ws : (s + 1) * ws], part)
        vec_out[at : at + 1, 0:ws] = part
    part = jnp.zeros((1, fs), F32)
    for s in range(shards):
        first = (s % per_chunk) * fs
        line = 5 + s // per_chunk
        part = jnp.where(z == s, value[line : line + 1, first : first + fs], part)
    vec_out[5:6, 0:fs] = part
    first_kv.share()
    first_q.share()
    two.finish()
    first_kv.finish()
    first_q.finish()
    net.finish()


def unpack_kernel(
    ws,
    wos,
    fs,
    out_in,
    gin_in,
    two_in,
    q_in,
    kv_in,
    vec_in,
    out_ref,
    gin_ref,
    g1_ref,
    b1_ref,
    kv_ref,
    q_ref,
    r_ref,
    wo_ref,
    g2_ref,
    b2_ref,
    wi_ref,
    bi_ref,
    wout_ref,
    bo_ref,
):
    out_ref[...] = out_in[...]
    gin_ref[...] = gin_in[...]
    for row, ref in enumerate((g1_ref, b1_ref, g2_ref, b2_ref, bo_ref, bi_ref)):
        ref[...] = vec_in[row : row + 1, 0 : ref.shape[1]]
    q_ref[...] = q_in[...].astype(F32)
    kv_ref[...] = kv_in[:, 0 : 2 * HS].astype(F32)
    r_ref[...] = kv_in[:, 2 * HS : 2 * HS + E].astype(F32)
    wo_ref[...] = two_in[0:wos].astype(F32)
    wout_ref[...] = two_in[wos : wos + fs].astype(F32)
    for panel in range(4):
        first = wos + fs + panel * ws
        wi_ref[:, panel * PANEL : (panel + 1) * PANEL] = two_in[first : first + ws].astype(F32)


def on_device(
    shards,
    ctxs,
    tokens,
    lengths,
    expert_picks,
    first_gain,
    first_bias,
    kv_weight,
    query_weight,
    router_weight,
    output_weight,
    second_gain,
    second_bias,
    inner_weight,
    inner_bias,
    outer_weight,
    outer_bias,
    cotangent,
):
    slots, seg, width = tokens.shape
    count = slots * seg
    half = seg // 2
    blocks = 2 * ctxs
    lanes = TOP * half
    ws = width // shards
    wos = output_weight.shape[0]
    fs = outer_weight.shape[0]
    group = min(ctxs, ws // 16)
    pairs, groups = group // 2, ctxs // group
    rounds = groups.bit_length() - 1
    rows_two = wos + fs + 4 * ws
    wide_one = E * HS + 256

    vmem = pl.BlockSpec(memory_space=pltpu.VMEM)
    smem = pl.BlockSpec(memory_space=pltpu.SMEM)
    anywhere = pl.BlockSpec(memory_space=pl.ANY)

    def reduce_scratch(rows, wide):
        piece = rows // group
        return [
            pltpu.VMEM((shards, rows, wide), BF16),
            pltpu.VMEM((shards, rows // 2, wide), BF16),
            pltpu.VMEM((max(pairs - 1, 1), shards, piece, wide), BF16),
            pltpu.VMEM((rounds, shards, piece, wide), BF16)
            if rounds
            else pltpu.VMEM((16, 128), BF16),
            pltpu.VMEM((shards - 1, piece, wide), BF16),
        ]

    copies = (
        2 * (shards - 1) * (pairs + 1)
        + (shards - 1)
        + 4 * (ctxs - 1)
        + 3 * (2 + 2 * (pairs - 1) + rounds + shards - 1)
        + (ctxs - 1)
        + (shards - 1)
    )
    scratch = [
        pltpu.VMEM(query_weight.shape, F32),
        pltpu.VMEM(kv_weight.shape, F32),
        pltpu.VMEM(router_weight.shape, F32),
        pltpu.VMEM(inner_weight.shape, F32),
        pltpu.VMEM((max(wos + fs, 3 * count), width), F32),
        pltpu.VMEM((shards, ws, wide_one), BF16),
        pltpu.VMEM((shards, rows_two, PANEL), BF16),
        pltpu.VMEM((shards, 8, fs), F32),
        pltpu.VMEM((count, width), BF16),
        pltpu.VMEM((width, count), BF16),
        pltpu.VMEM((E, HS, count), F32),
        pltpu.VMEM((TOP, HS, count), F32),
        pltpu.VMEM((TOP, HS, count), F32),
        pltpu.VMEM((2, count, count), F32),
        pltpu.VMEM((blocks, slots, half, 2 * HS), BF16),
        pltpu.VMEM((blocks, 2 * HS, slots * half), BF16),
        pltpu.VMEM((4, 2 * HS, lanes), BF16),
        pltpu.VMEM((4, 2 * HS, lanes), BF16),
        pltpu.VMEM((4, HS, lanes), F32),
        pltpu.VMEM((4, 8, lanes), F32),
        pltpu.VMEM((slots, blocks + 1, half, lanes), BF16),
        pltpu.VMEM((blocks, slots, half, 2 * HS), F32),
        pltpu.VMEM((ctxs - 1, 2, slots, half, 2 * HS), BF16),
        pltpu.VMEM((E, HS, count), BF16),
        pltpu.VMEM((count, width), F32),
        pltpu.VMEM((count, width), BF16),
        pltpu.VMEM((width, count), BF16),
        pltpu.VMEM((count, width), BF16),
        pltpu.VMEM((8, PANEL), F32),
        pltpu.VMEM((wide_one, count), BF16),
        *reduce_scratch(rows_two, PANEL),
        *reduce_scratch(ws, E * HS),
        *reduce_scratch(ws, 256),
        pltpu.VMEM((16, width), F32),
        pltpu.VMEM((ctxs - 1, 16, width), F32),
        pltpu.VMEM((shards - 1, 16, width), F32),
        pltpu.SemaphoreType.DMA((6,)),
        pltpu.SemaphoreType.DMA((copies,)),
        pltpu.SemaphoreType.DMA((copies,)),
    ]
    results = pl.pallas_call(
        functools.partial(layer_kernel, shards, ctxs, group),
        out_shape=(
            jax.ShapeDtypeStruct((count, width), BF16),
            jax.ShapeDtypeStruct((count, width), F32),
            jax.ShapeDtypeStruct((rows_two, PANEL), BF16),
            jax.ShapeDtypeStruct((ws, E * HS), BF16),
            jax.ShapeDtypeStruct((ws, 256), BF16),
            jax.ShapeDtypeStruct((8, fs), F32),
        ),
        in_specs=[smem] + [vmem] * 9 + [anywhere] * 6,
        out_specs=tuple([vmem] * 6),
        scratch_shapes=scratch,
        compiler_params=pltpu.CompilerParams(
            collective_id=0, has_side_effects=True, vmem_limit_bytes=VMEM_BYTES
        ),
        name="layer",
    )(
        lengths,
        tokens.reshape(count, width),
        cotangent.reshape(count, width),
        expert_picks.reshape(count, TOP),
        first_gain.reshape(1, ws),
        first_bias.reshape(1, ws),
        second_gain.reshape(1, ws),
        second_bias.reshape(1, ws),
        outer_bias.reshape(1, ws),
        inner_bias.reshape(1, fs),
        query_weight,
        kv_weight,
        router_weight,
        output_weight,
        inner_weight,
        outer_weight,
    )
    vec_shape = jax.ShapeDtypeStruct((1, ws), F32)
    final = pl.pallas_call(
        functools.partial(unpack_kernel, ws, wos, fs),
        out_shape=(
            jax.ShapeDtypeStruct((count, width), BF16),
            jax.ShapeDtypeStruct((count, width), F32),
            vec_shape,
            vec_shape,
            jax.ShapeDtypeStruct(kv_weight.shape, F32),
            jax.ShapeDtypeStruct(query_weight.shape, F32),
            jax.ShapeDtypeStruct(router_weight.shape, F32),
            jax.ShapeDtypeStruct(output_weight.shape, F32),
            vec_shape,
            vec_shape,
            jax.ShapeDtypeStruct(inner_weight.shape, F32),
            jax.ShapeDtypeStruct((1, fs), F32),
            jax.ShapeDtypeStruct(outer_weight.shape, F32),
            vec_shape,
        ),
        in_specs=[vmem] * 6,
        out_specs=tuple([vmem] * 14),
        name="unpack",
    )(*results)
    shapes = (
        tokens.shape,
        tokens.shape,
        first_gain.shape,
        first_bias.shape,
        kv_weight.shape,
        query_weight.shape,
        router_weight.shape,
        output_weight.shape,
        second_gain.shape,
        second_bias.shape,
        inner_weight.shape,
        inner_bias.shape,
        outer_weight.shape,
        outer_bias.shape,
    )
    return tuple(value.reshape(shape) for value, shape in zip(final, shapes))


def solution(mesh):
    rows = P("shard", "ctx", None)
    vec, mat = P("shard"), P("shard", None)
    return jax.shard_map(
        functools.partial(on_device, mesh.shape["shard"], mesh.shape["ctx"]),
        mesh=mesh,
        in_specs=(
            rows,
            vec,
            rows,
            vec,
            vec,
            mat,
            mat,
            mat,
            mat,
            vec,
            vec,
            mat,
            vec,
            mat,
            vec,
            rows,
        ),
        out_specs=(
            rows,
            rows,
            vec,
            vec,
            mat,
            mat,
            mat,
            mat,
            vec,
            vec,
            mat,
            vec,
            mat,
            vec,
        ),
        check_vma=False,
    )
```

time: 626 us -> 160 us (0.26)
  waiting for transfers between devices: 227 us -> 0 us
  Pallas kernels: 0 us -> 154 us
  blocking collectives: 127 us -> 0 us
  local copies, waits for them, and re-layouts: 89.1 us -> 4.43 us
  matrix products: 80.6 us -> 0 us
  other arithmetic: 79.8 us -> 0 us
  between operations: 16.7 us -> 0.65 us
    reduce_scatter x6 -> x0, waiting for transfers between devices: 174 us -> none  [the longest x1 45.5 us: on_device(): lax.psum_scatter(outer_grad.astype(jnp.bfloat16), 'shard', scatter_dimens...]
    pallas_call x0 -> x2, Pallas kernels: none -> 154 us  [the longest x1 150 us: on_device(): pl.pallas_call(functools.partial(layer_kernel, shards, ctxs, group), out_...]
    all_gather x9 -> x0, blocking collectives: 93.2 us -> none  [the longest x1 13.4 us: on_device(): lax.all_gather(kv_weight.astype(jnp.bfloat16), 'shard', axis=0, tiled=True)]
    dot_general x96 -> x0, matrix products: 80.6 us -> none  [the longest x38 21.7 us: row_dot(): lax.dot_general(left, right, (((1,), (1,)), ((), ())), preferred_element_...]
    dynamic_slice x44 -> x0, local copies, waits for them, and re-layouts: 43.6 us -> none  [the longest x32 35.3 us: on_device(): lax.map(forward_slot, (query_slots, keyval_all, lengths))]
    psum x1 -> x0, waiting for transfers between devices: 34.8 us -> none  [on_device(): lax.psum(shares[3].astype(jnp.bfloat16), 'ctx').astype(jnp.float32)]
    lt x24 -> x0, other arithmetic: 30.2 us -> none  [block_scores(): key_pos[None, :] < length]
    psum x1 -> x0, blocking collectives: 23.8 us -> none  [on_device(): lax.psum(shares[0].astype(jnp.bfloat16), 'ctx').astype(jnp.float32)]
  transfers between devices with their start and end apart: 12 -> 0, of which waited for: 8 -> 0; matrix products, arithmetic and copies ran while one was open for 23% -> 0% of each run, Pallas kernels for 0% -> 0%
where the time goes in v1:
time: 160 us
  Pallas kernels  154 us (96%)
  local copies, waits for them, and re-layouts  4.43 us (3%)
    pallas_call x1, Pallas kernels, on_device(): pl.pallas_call(functools.partial(layer_kernel, shards, ctxs, group), out_...  150 us
    unnamed x3, local copies, waits for them, and re-layouts  4.43 us
    pallas_call x1, Pallas kernels, on_device(): pl.pallas_call(functools.partial(unpack_kernel, ws, wos, fs), out_shape=(...  3.96 us

profile of v1, /device:TPU:0, one launch (start us, length us, event | category | flops | bytes accessed | tf_op | source)
XLA Modules:
  0.0 159.5 jit_solution(10478074988966631982)
XLA Ops:
  0.6 1.4 copy.31.wr_hbm
  2.1 1.5 copy.30
  3.6 150.5 %layer.1 = (bf16[256,512]{1,0:T(8,128)(2,1)}, f32[256,512]{1,0:T(8,128)}, bf16[1408,512]{1,0:T(8,128)(2,1)}, bf16[128,1536]{1,0:T(8,128)(2,1)}, bf16[128,256]{1,0:T(8,128)(2,1)}, /*index=5*/f32[8,512]{1,0:T(8,128)}) custom-call(s32[2]{0:T(128)} %len_ref.1, bf16[256,512]{1,0:T(8,128)(2,1)} %bitcast.18, bf16[256,512]{1,0:T(8,128)(2,1)} %bitcast.19, ...), custom_call_target="tpu_custom_call" | custom-call | tf_op jit(solution)/shard_map/layer/pallas_call | solution.py:1012
  154.1 4.0 %unpack.1 = (bf16[256,512]{1,0:T(8,128)(2,1)}, f32[256,512]{1,0:T(8,128)}, f32[1,128]{1,0:T(1,128)}, f32[1,128]{1,0:T(1,128)}, f32[128,128]{1,0:T(8,128)}, /*ind...) custom-call(bf16[256,512]{1,0:T(8,128)(2,1)} %get-tuple-element.34.o, ...), custom_call_target="tpu_custom_call" | custom-call | tf_op jit(solution)/shard_map/unpack/pallas_call | solution.py:1048
  158.0 1.5 copy.32

commit v2 on v1

v2 whole, which is shorter than its diff:
```python
import functools

import jax
import jax.numpy as jnp
from jax import lax
from jax.experimental import pallas as pl
from jax.experimental.pallas import tpu as pltpu
from jax.sharding import PartitionSpec as P

HS = 64
E = 24
TOP = 8
NORM_EPS = 1e-05
NEG_LARGE = -1e30
BF16 = jnp.bfloat16
F32 = jnp.float32
PANEL = 512
UNIT = 128
GELU_C = 0.7978845608028654
GELU_A = 0.044715
MESH = pl.DeviceIdType.MESH


def dot(left, right):
    return jnp.dot(left, right, preferred_element_type=F32)


def dot_t(left, right):
    return lax.dot_general(left, right, (((1,), (1,)), ((), ())), preferred_element_type=F32)


def many(first, size, step):
    return pl.ds(pl.multiple_of(first, step), size)


class Net:
    def __init__(self, shards, ctxs, group, send_sem, recv_sem):
        self.shards, self.ctxs, self.group = shards, ctxs, group
        self.pairs = group // 2
        self.groups = ctxs // group
        self.dims = self.pairs.bit_length() - 1
        self.z = lax.axis_index("shard")
        self.i = lax.axis_index("ctx")
        self.core = self.i % 2
        self.chip = (self.i % group) // 2
        self.grp = self.i // group
        self.send_sem, self.recv_sem = send_sem, recv_sem
        self.used = 0
        self.sent = []
        flip_low = self.chip + 1 - 2 * (self.chip % 2)
        if self.dims == 2:
            flip_high = self.chip + 2 - 4 * (self.chip // 2)
            self.chip_a = self.core * flip_high + (1 - self.core) * flip_low
            self.chip_b = self.core * flip_low + (1 - self.core) * flip_high
            self.chip_ab = self.pairs - 1 - self.chip
        elif self.dims == 1:
            self.chip_b = flip_low

    def far(self, step):
        return (self.z + step) % self.shards

    def src(self, step):
        return (self.z + self.shards - step) % self.shards

    def peer(self, chip):
        return self.grp * self.group + chip * 2 + self.core

    def sibling(self):
        return self.i + 1 - 2 * self.core

    def copy(self, src, dst, slot, z, i):
        return pltpu.make_async_remote_copy(
            src_ref=src,
            dst_ref=dst,
            send_sem=self.send_sem.at[slot],
            recv_sem=self.recv_sem.at[slot],
            device_id={"shard": z, "ctx": i},
            device_id_type=MESH,
        )

    def send(self, src, dst, z, i):
        slot = self.used
        self.used += 1
        one = self.copy(src, dst, slot, z, i)
        one.start()
        self.sent.append(one)
        return slot

    def wait(self, slot, dst):
        self.copy(dst, dst, slot, self.z, self.i).wait_recv()

    def finish(self):
        for one in self.sent:
            one.wait_send()
        self.sent = []

    def greet(self):
        barrier = pltpu.get_barrier_semaphore()
        for step in range(1, self.ctxs):
            pl.semaphore_signal(
                barrier,
                inc=1,
                device_id={"shard": self.z, "ctx": (self.i + step) % self.ctxs},
                device_id_type=MESH,
            )
        for step in range(1, self.shards):
            pl.semaphore_signal(
                barrier,
                inc=1,
                device_id={"shard": self.far(step), "ctx": self.i},
                device_id_type=MESH,
            )

    def greeted(self):
        pl.semaphore_wait(pltpu.get_barrier_semaphore(), self.ctxs + self.shards - 2)


class Spread:
    def __init__(self, net, ref):
        self.net, self.ref = net, ref
        self.piece = ref.shape[0] // net.group
        self.half = ref.shape[0] // 2

    def part(self, chip):
        first = (self.net.core * self.net.pairs + chip) * self.piece
        return self.ref.at[many(first, self.piece, self.piece)]

    def block(self, core):
        return self.ref.at[many(core * self.half, self.half, self.half)]

    def begin(self):
        net = self.net
        own = self.part(net.chip)
        if net.dims == 2:
            self.to_a = net.send(own, own, net.z, net.peer(net.chip_a))
        if net.dims:
            self.to_b = net.send(own, own, net.z, net.peer(net.chip_b))

    def pass_on(self):
        net = self.net
        if net.dims == 2:
            got = self.part(net.chip_a)
            net.wait(self.to_a, got)
            self.on = net.send(got, got, net.z, net.peer(net.chip_b))

    def share(self):
        net = self.net
        if net.dims:
            net.wait(self.to_b, self.part(net.chip_b))
        if net.dims == 2:
            net.wait(self.on, self.part(net.chip_ab))
        block = self.block(net.core)
        self.to_core = net.send(block, block, net.z, net.sibling())

    def end(self):
        self.net.wait(self.to_core, self.block(1 - self.net.core))


class Gather:
    def __init__(self, net, buf):
        self.net, self.buf = net, buf
        self.spreads = [Spread(net, buf.at[net.src(k)]) for k in range(1, net.shards)]

    def start(self):
        net = self.net
        own = Spread(net, self.buf.at[net.z]).part(net.chip)
        self.slots = [net.send(own, own, net.far(k), net.i) for k in range(1, net.shards)]

    def begin(self):
        for slot, spread in zip(self.slots, self.spreads):
            self.net.wait(slot, spread.part(self.net.chip))
            spread.begin()

    def pass_on(self):
        for spread in self.spreads:
            spread.pass_on()

    def share(self):
        for spread in self.spreads:
            spread.share()

    def end(self):
        for spread in self.spreads:
            spread.end()


class CoreGather:
    def __init__(self, net, buf):
        self.net, self.buf = net, buf
        self.spreads = [Spread(net, buf.at[net.src(k)]) for k in range(1, net.shards)]

    def start(self):
        net = self.net
        own = Spread(net, self.buf.at[net.z]).block(net.core)
        self.slots = [net.send(own, own, net.far(k), net.i) for k in range(1, net.shards)]

    def share(self):
        net = self.net
        for slot, spread in zip(self.slots, self.spreads):
            block = spread.block(net.core)
            net.wait(slot, block)
            spread.to_core = net.send(block, block, net.z, net.sibling())

    def end(self):
        for spread in self.spreads:
            spread.end()


class Reduce:
    def __init__(
        self, net, grad, from_core, from_a, from_b, from_group, from_far, out, far_first, store
    ):
        self.net, self.grad, self.out, self.far_first = net, grad, out, far_first
        self.store = store
        self.from_core, self.from_a, self.from_b = from_core, from_a, from_b
        self.from_group, self.from_far = from_group, from_far
        self.piece = grad.shape[1] // net.group
        self.half = grad.shape[1] // 2
        self.spread = Spread(net, out)
        near = [self.take_a, self.take_b] if net.dims == 2 else [self.take_b]
        steps = [self.take_far] + near if far_first else near + [self.take_far]
        self.steps = [self.start, self.take_core] + steps
        self.steps[-1] = functools.partial(self.last, self.steps[-1])
        if net.dims == 2:
            self.steps.append(self.spread.pass_on)
        self.steps += [self.spread.share, self.finish]
        self.stage = 0

    def advance(self, times=1):
        for _ in range(times):
            if self.stage < len(self.steps):
                self.steps[self.stage]()
                self.stage += 1

    def last(self, step):
        step()
        self.spread.begin()

    def finish(self):
        self.spread.end()
        self.store.start()

    def first(self, chip):
        return (self.net.core * self.net.pairs + chip) * self.piece

    def rows(self, chip):
        return many(self.first(chip), self.piece, self.piece)

    def planes(self, after_far):
        if after_far:
            return [(self.net.z, 0)]
        return [(s, s) for s in range(self.net.shards)]

    def add(self, first, count, planes, parts):
        lines = 16

        def one(step, carry):
            at = pl.multiple_of(step * lines, lines)
            rows = many(first + at, lines, lines)
            for here, there in planes:
                value = self.grad[here, rows].astype(F32)
                for part in parts:
                    value = value + part[there, pl.ds(at, lines)].astype(F32)
                self.grad[here, rows] = value.astype(BF16)
            return carry

        lax.fori_loop(0, count // lines, one, 0)

    def cut(self, rows, after_far):
        if after_far:
            return self.grad.at[pl.ds(self.net.z, 1), rows]
        return self.grad.at[:, rows]

    def start(self):
        net = self.net
        away = many((1 - net.core) * self.half, self.half, self.half)
        self.to_core = net.send(self.grad.at[:, away], self.from_core, net.z, net.sibling())

    def take_core(self):
        net = self.net
        net.wait(self.to_core, self.from_core)
        self.add(net.core * self.half, self.half, self.planes(False), [self.from_core])
        if self.far_first:
            own = many(net.core * self.half, self.half, self.half)
            self.send_far(own)
        else:
            self.send_near(False)

    def send_near(self, after_far):
        net = self.net
        if net.dims == 2:
            self.to_a = [
                net.send(
                    self.cut(self.rows(chip), after_far),
                    self.from_a.at[k],
                    net.z,
                    net.peer(net.chip_a),
                )
                for k, chip in enumerate((net.chip_a, net.chip_ab))
            ]
        elif net.dims == 1:
            self.send_b(after_far)

    def send_b(self, after_far):
        net = self.net
        self.to_b = net.send(
            self.cut(self.rows(net.chip_b), after_far), self.from_b, net.z, net.peer(net.chip_b)
        )

    def take_a(self):
        net = self.net
        for k, chip in ((1, net.chip_b), (0, net.chip)):
            net.wait(self.to_a[k], self.from_a.at[k])
            self.add(self.first(chip), self.piece, self.planes(self.far_first), [self.from_a.at[k]])
            if k:
                self.send_b(self.far_first)

    def take_b(self):
        net = self.net
        if net.dims:
            net.wait(self.to_b, self.from_b)
            self.add(
                self.first(net.chip), self.piece, self.planes(self.far_first), [self.from_b]
            )
        own = self.rows(net.chip)
        step, at = 1, 0
        while step < net.groups:
            peer = net.i + net.group * step * (1 - 2 * ((net.grp // step) % 2))
            slot = net.send(self.cut(own, self.far_first), self.from_group.at[at], net.z, peer)
            net.wait(slot, self.from_group.at[at])
            net.sent.pop().wait_send()
            self.add(
                self.first(net.chip),
                self.piece,
                self.planes(self.far_first),
                [self.from_group.at[at]],
            )
            step, at = step * 2, at + 1
        if self.far_first:
            self.out[own, :] = self.grad[net.z, own]
        else:
            self.send_far(own)

    def send_far(self, own):
        net = self.net
        self.own = own
        self.to_far = [
            net.send(
                self.grad.at[pl.ds(net.far(k), 1), own],
                self.from_far.at[pl.ds(k - 1, 1)],
                net.far(k),
                net.i,
            )
            for k in range(1, net.shards)
        ]

    def take_far(self):
        net = self.net
        for k in range(1, net.shards):
            net.wait(self.to_far[k - 1], self.from_far.at[pl.ds(k - 1, 1)])
        parts = [self.from_far.at[pl.ds(k, 1)] for k in range(net.shards - 1)]
        if self.far_first:
            self.add(net.core * self.half, self.half, self.planes(True), parts)
            self.send_near(True)
        else:
            self.add(self.first(net.chip), self.piece, self.planes(True), parts)
            self.out[self.own, :] = self.grad[net.z, self.own]


def reduce_scratch(shards, group, rounds, rows, wide, far_first, lead=()):
    pairs = group // 2
    piece, half = rows // group, rows // 2
    far_rows = half if far_first else piece
    planes = 1 if far_first else shards
    tiny = (*lead, 1, 16, 128)
    return [
        pltpu.VMEM((*lead, shards, rows, wide), BF16),
        pltpu.VMEM((*lead, shards, half, wide), BF16),
        pltpu.VMEM((*lead, 2, planes, piece, wide) if pairs == 4 else tiny, BF16),
        pltpu.VMEM((*lead, planes, piece, wide), BF16),
        pltpu.VMEM((*lead, rounds, planes, piece, wide) if rounds else tiny, BF16),
        pltpu.VMEM((*lead, shards - 1, far_rows, wide), BF16),
    ]


def reduce_copies(shards, group, rounds):
    pairs = group // 2
    near = {1: 0, 2: 1, 4: 3}[pairs]
    return 2 * (near + 1) + rounds + shards - 1


def layer_kernel(
    shards,
    ctxs,
    group,
    chunk_far,
    len_ref,
    x_hbm,
    cot_hbm,
    picks_hbm,
    g1_hbm,
    b1_hbm,
    g2_hbm,
    b2_hbm,
    bo_hbm,
    bi_hbm,
    wq_hbm,
    wkv_hbm,
    wr_hbm,
    wo_hbm,
    wi_hbm,
    wout_hbm,
    out_hbm,
    gin_hbm,
    chunk_hbm,
    wo_hbm_out,
    q_hbm,
    kv_hbm,
    x_ref,
    cot_ref,
    picks_ref,
    g1_ref,
    b1_ref,
    g2_ref,
    b2_ref,
    bo_ref,
    bi_ref,
    wq_st,
    wkv_st,
    wr_st,
    wi_st,
    stage,
    wk,
    wq,
    wo,
    wc,
    vecs,
    normed,
    normed_t,
    q_t,
    sel_a,
    heads_t,
    small,
    kvall,
    kvt,
    pads,
    hrow,
    linv,
    ebuf,
    dkv,
    from_sib,
    from_kv,
    mixed_t,
    xhat2,
    n2,
    n2_t,
    gfin_low,
    biases,
    g_t,
    gc,
    gc_core,
    gc_a,
    gc_b,
    gc_group,
    gc_far,
    go,
    go_core,
    go_a,
    go_b,
    go_group,
    go_far,
    gq,
    gq_core,
    gq_a,
    gq_b,
    gq_group,
    gq_far,
    gk,
    gk_core,
    gk_a,
    gk_b,
    gk_group,
    gk_far,
    out_ref,
    gin_ref,
    chunk_out,
    wo_out,
    q_out,
    kv_out,
    vec_g,
    local_sem,
    send_sem,
    recv_sem,
):
    net = Net(shards, ctxs, group, send_sem, recv_sem)
    z, c = net.z, net.i
    tokens, width = x_ref.shape
    seg = tokens // 2
    half = seg // 2
    blocks = 2 * ctxs
    ws = width // shards
    wos = wo.shape[1]
    fs = wout_hbm.shape[0]
    scale = HS ** (-0.5)
    chunks = fs // UNIT
    panels = shards * UNIT // PANEL
    per_panel = PANEL // UNIT
    lanes = TOP * half
    wide = E * HS
    vec_line = E
    bias_line = vec_line + 5
    per_unit = UNIT // ws
    near_steps = ctxs // 2

    def local(src, dst, at):
        return pltpu.make_async_copy(src, dst, local_sem.at[at])

    net.greet()
    wo_st, wout_st = stage.at[0:wos], stage.at[wos : wos + fs]
    resid, acc_a, acc_b = (stage.at[k * tokens : (k + 1) * tokens] for k in range(3))
    loads = {}
    for at, (src, dst) in enumerate(
        (
            (wkv_hbm, wkv_st),
            (wr_hbm, wr_st),
            (wq_hbm, wq_st),
            (g1_hbm, g1_ref),
            (b1_hbm, b1_ref),
            (g2_hbm, g2_ref),
            (b2_hbm, b2_ref),
            (bo_hbm, bo_ref),
            (bi_hbm, bi_ref),
            (x_hbm, x_ref),
            (picks_hbm, picks_ref),
            (wo_hbm, wo_st),
            (wi_hbm, wi_st),
            (wout_hbm, wout_st),
            (cot_hbm, cot_ref),
        )
    ):
        loads[id(dst)] = local(src, dst, at)
        loads[id(dst)].start()
    loads[id(wkv_st)].wait()
    loads[id(wr_st)].wait()
    wk[z, :, 0 : 2 * HS] = wkv_st[...].astype(BF16)
    padded = jnp.concatenate([wr_st[...], jnp.zeros((128 - E, ws), F32)], axis=0)
    wk[z, :, 2 * HS :] = padded.T.astype(BF16)
    own_vec = vecs.at[z]
    own_vec[...] = jnp.zeros(own_vec.shape, F32)
    for row, ref in enumerate((g1_ref, b1_ref, g2_ref, b2_ref, bo_ref, bi_ref)):
        loads[id(ref)].wait()
        own_vec[row : row + 1, 0 : ref.shape[1]] = ref[...].astype(BF16).astype(F32)
    net.greeted()
    gather_k, gather_q, gather_o = CoreGather(net, wk), Gather(net, wq), Gather(net, wo)
    gather_c = [Gather(net, wc.at[k]) for k in range(chunks)]
    gather_k.start()
    vec_slots = [net.send(own_vec, own_vec, net.far(k), net.i) for k in range(1, shards)]
    loads[id(wq_st)].wait()
    wq[z] = wq_st[...].astype(BF16)
    gather_q.start()

    loads[id(x_ref)].wait()
    x = x_ref[...].astype(F32)
    mean1 = jnp.mean(x, axis=1, keepdims=True)
    cen = x - mean1
    small[0, :, 0:1] = lax.rsqrt(jnp.mean(cen * cen, axis=1, keepdims=True) + NORM_EPS)
    small[0, :, 2:3] = mean1

    def first_hat():
        return (x_ref[...].astype(F32) - small[0, :, 2:3]) * small[0, :, 0:1]

    for ref in (wo_st, wi_st, wout_st):
        loads[id(ref)].wait()
    wo[z] = wo_st[...].astype(BF16)
    for k in range(chunks):
        wc[k, z, 0:UNIT] = wout_st[k * UNIT : (k + 1) * UNIT].astype(BF16)
        for s in range(shards):
            first = UNIT + (s // per_panel) * ws
            at = (s % per_panel) * UNIT
            wc[k, z, first : first + ws, at : at + UNIT] = wi_st[
                :, s * fs + k * UNIT : s * fs + (k + 1) * UNIT
            ].astype(BF16)
    gather_k.share()
    for k in range(1, shards):
        net.wait(vec_slots[k - 1], vecs.at[net.src(k)])

    def whole(row):
        return jnp.concatenate([vecs[s, row : row + 1, 0:ws] for s in range(shards)], axis=1)

    gain1, bias1, gain2, bias2, bias_out = (whole(row) for row in range(5))
    for k in range(chunks):
        for p in range(panels):
            biases[k * panels + p : k * panels + p + 1, :] = jnp.concatenate(
                [
                    vecs[s, 5:6, k * UNIT : (k + 1) * UNIT]
                    for s in range(p * per_panel, (p + 1) * per_panel)
                ],
                axis=1,
            )
    norm_value = first_hat() * gain1 + bias1
    normed[...] = norm_value.astype(BF16)
    normed_t[...] = norm_value.T.astype(BF16)
    gather_k.end()

    kvr = dot(normed[...], wk[...].reshape(width, 256))
    kv_own = kvr[:, 0 : 2 * HS].astype(BF16)

    def at_block(ref, block):
        return ref.at[block // 2, :, block % 2]

    def my_block(h):
        return c if h == 0 else blocks - 1 - c

    def core_blocks(ref, core):
        return ref.at[0:near_steps, :, core], ref.at[near_steps:ctxs, :, 1 - core]

    for h in range(2):
        block = my_block(h)
        for s in range(2):
            first = s * seg + h * half
            kvall[block // 2, s, block % 2] = kv_own[first : first + half]
    kv_first = len(net.sent)
    kv_slots = []
    for step in range(1, near_steps):
        kv_slots.append(
            [
                net.send(at_block(kvall, block), at_block(kvall, block), z, (c + 2 * step) % ctxs)
                for block in (c, blocks - 1 - c)
            ]
        )
    kv_sent = net.sent[kv_first:]
    del net.sent[kv_first:]
    gather_q.begin()
    gather_o.start()
    logits_t = kvr[:, 2 * HS : 2 * HS + 128].T
    loads[id(picks_ref)].wait()
    picks = jnp.concatenate([picks_ref[0], picks_ref[1]], axis=1).astype(F32)
    picked = jnp.zeros((TOP, tokens), F32)
    for e in range(E):
        picked = jnp.where(picks == float(e), logits_t[e : e + 1, :], picked)
    top = jnp.max(picked, axis=0, keepdims=True)
    gexp = jnp.exp(picked - top)
    small[1, 0:TOP, 0:tokens] = gexp / jnp.sum(gexp, axis=0, keepdims=True)
    small[1, TOP : 2 * TOP, 0:tokens] = picks
    for step in range(1, near_steps):
        source = (c + ctxs - 2 * step) % ctxs
        for slot, block in zip(kv_slots[step - 1], (source, blocks - 1 - source)):
            net.wait(slot, at_block(kvall, block))
    kv_cross = [net.send(part, part, z, net.sibling()) for part in core_blocks(kvall, net.core)]
    kv_sent += net.sent[-2:]
    del net.sent[-2:]
    gather_q.pass_on()
    gather_c[0].start()
    for slot, part in zip(kv_cross, core_blocks(kvall, 1 - net.core)):
        net.wait(slot, part)

    def turn(step, carry):
        for s in range(2):
            keys = kvall[step, s].reshape(2 * half, 2 * HS)
            kvt[step, s] = keys.astype(F32).T.astype(BF16)
            dkv[step, s] = jnp.zeros((2 * half, 2 * HS), F32)
        return carry

    lax.fori_loop(0, ctxs, turn, 0)
    gather_q.share()
    gather_o.begin()
    if chunks > 1:
        gather_c[1].start()
    gather_q.end()

    def query_tile(n, carry):
        cols = many(n * 256, 256, 256)
        value = dot(normed[...], wq[:, :, cols].reshape(width, 256))
        value = value.astype(BF16).astype(F32).T
        for k in range(4):
            q_t[n * 4 + k] = value[k * HS : (k + 1) * HS]
        return carry

    lax.fori_loop(0, wide // 256, query_tile, 0)

    def choose(src, store):
        def one(j, carry):
            pick = small[1, pl.ds(TOP + j, 1), 0:tokens]
            value = jnp.zeros((HS, tokens), F32)
            for e in range(E):
                value = jnp.where(pick == float(e), src[e], value)
            store(j, value)
            return carry

        lax.fori_loop(0, TOP, one, 0)

    def spread_back(src, store):
        def one(e, carry):
            value = jnp.zeros((HS, tokens), F32)
            for j in range(TOP):
                pick = small[1, TOP + j : TOP + j + 1, 0:tokens]
                value = jnp.where(pick == e.astype(F32), src[j], value)
            store(e, value)
            return carry

        lax.fori_loop(0, E, one, 0)

    low_lane = lax.broadcasted_iota(jnp.int32, (HS, 2 * half), 1) < half

    def swap(one, two):
        return (
            jnp.where(low_lane, one, pltpu.roll(two, half, 1)),
            jnp.where(low_lane, pltpu.roll(one, half, 1), two),
        )

    def store_query(j, value):
        sel_a[j] = value * scale

    def serve(*calls):
        for k, call in calls:
            if k < chunks:
                getattr(gather_c[k], call)()

    gather_o.pass_on()
    serve((0, "begin"), (2, "start"))
    choose(q_t, store_query)
    for s in range(2):
        for pair in range(TOP // 2):
            halves = swap(
                sel_a[2 * pair, :, s * seg : (s + 1) * seg],
                sel_a[2 * pair + 1, :, s * seg : (s + 1) * seg],
            )
            for h in range(2):
                pads[2 * s + h, 0:HS, pair * 128 : (pair + 1) * 128] = halves[h].astype(BF16)
    for sh in range(4):
        pads[sh, HS:, 0:lanes] = jnp.zeros((HS, lanes), BF16)
        pads[sh, 0:HS, lanes:] = jnp.zeros((HS, lanes), BF16)

    gather_o.share()
    serve((0, "pass_on"), (1, "begin"), (3, "start"))

    offset = lax.broadcasted_iota(jnp.int32, (1, lanes), 1) % half
    key_row = lax.broadcasted_iota(jnp.int32, (2 * half, lanes), 0)

    def place(h):
        if h == 1:
            return (blocks - c + 1) // 2, 0
        return (c + 2) // 2, (blocks - c + 1) // 2

    def fold(value, op):
        parts = [value[8 * k : 8 * k + 8] for k in range(value.shape[0] // 8)]
        while len(parts) > 1:
            parts = [op(parts[k], parts[k + 1]) for k in range(0, len(parts), 2)]
        return parts[0]

    def keys_of(step, s):
        return kvall[step, s].reshape(2 * half, 2 * HS)

    def attend(h):
        count, base = place(h)
        limits = [
            jnp.minimum(my_block(h) * half + offset, len_ref[s] - 1) for s in range(2)
        ]

        def masked(step, s):
            scores = dot(keys_of(step, s), pads[2 * s + h, :, 0:lanes])
            return jnp.where(key_row <= limits[s] - step * 2 * half, scores, NEG_LARGE)

        def score_step(step, tops):
            return tuple(
                jnp.maximum(tops[s], fold(masked(step, s), jnp.maximum)) for s in range(2)
            )

        start = jnp.full((8, lanes), NEG_LARGE, F32)
        tops = lax.fori_loop(0, count, score_step, (start, start))
        tops = [jnp.max(top, axis=0, keepdims=True) for top in tops]
        if h == 1:
            serve((0, "share"), (1, "pass_on"), (2, "begin"))
        for s in range(2):
            hrow[2 * s + h] = jnp.zeros((HS, lanes), F32)

        def value_step(step, totals):
            result = []
            for s in range(2):
                expd = jnp.exp(masked(step, s) - tops[s])
                low = expd.astype(BF16)
                ebuf[s, base + step] = low
                hrow[2 * s + h] += dot(kvt[step, s, HS:], low)
                result.append(totals[s] + fold(expd, jnp.add))
            return tuple(result)

        start = jnp.zeros((8, lanes), F32)
        totals = lax.fori_loop(0, count, value_step, (start, start))
        for s in range(2):
            inverse = 1.0 / jnp.sum(totals[s], axis=0, keepdims=True)
            linv[2 * s + h] = jnp.broadcast_to(inverse, (8, lanes))
            hrow[2 * s + h] = hrow[2 * s + h] * inverse

    attend(1)
    serve((1, "share"), (2, "pass_on"), (3, "begin"))
    attend(0)
    serve((2, "share"), (3, "pass_on"))

    for s in range(2):
        for pair in range(TOP // 2):
            both = swap(
                hrow[2 * s, :, pair * 128 : (pair + 1) * 128],
                hrow[2 * s + 1, :, pair * 128 : (pair + 1) * 128],
            )
            for k in range(2):
                heads_t[2 * pair + k, :, s * seg : (s + 1) * seg] = both[k]
    for j in range(TOP):
        sel_a[j] = heads_t[j] * small[1, j : j + 1, 0:tokens]

    def store_mixed(e, value):
        mixed_t[e] = value.astype(BF16)

    spread_back(sel_a, store_mixed)
    gather_o.end()
    serve((3, "share"))

    experts = E // shards
    acc_a[...] = x_ref[...].astype(F32)

    def project(s, carry):
        part = mixed_t[pl.ds(s * experts, experts)].reshape(wos, tokens)
        acc_a[...] += dot(part.astype(F32).T.astype(BF16), wo[s])
        return carry

    lax.fori_loop(0, shards, project, 0)
    residual = acc_a[...]
    resid[...] = residual
    cen = residual - jnp.mean(residual, axis=1, keepdims=True)
    rstd2 = lax.rsqrt(jnp.mean(cen * cen, axis=1, keepdims=True) + NORM_EPS)
    small[0, :, 1:2] = rstd2
    cen = cen * rstd2
    xhat2[...] = cen
    cen = cen * gain2 + bias2
    n2[...] = cen.astype(BF16)
    n2_t[...] = cen.T.astype(BF16)

    row = lax.broadcasted_iota(jnp.int32, (tokens, 1), 0)
    inner_row = row % seg
    pos = jnp.where(
        inner_row < half, c * half + inner_row, blocks * half - (c + 2) * half + inner_row
    )
    valid = (pos < jnp.where(row < seg, len_ref[0], len_ref[1])).astype(F32)
    loads[id(cot_ref)].wait()
    gfin_low[...] = (cot_ref[...].astype(F32) * valid).astype(BF16)
    acc_a[...] = jnp.zeros((tokens, width), F32)
    acc_b[...] = jnp.zeros((tokens, width), F32)
    vec_g[...] = jnp.zeros(vec_g.shape, F32)

    def feed(k, p):
        rows_in = slice(UNIT + p * ws, UNIT + (p + 1) * ws)
        planes = slice(p * per_panel, (p + 1) * per_panel)
        w_in = wc[k, :, rows_in].reshape(width, PANEL)
        w_out = wc[k, planes, 0:UNIT].reshape(PANEL, width)
        line = k * panels + p
        hidden = dot(n2[...], w_in) + biases[line : line + 1, :]
        square = hidden * hidden
        tanh = jnp.tanh(GELU_C * hidden * (1.0 + GELU_A * square))
        act = (0.5 * hidden * (1.0 + tanh)).astype(BF16)
        slope = 0.5 * (1.0 + tanh) + 0.5 * GELU_C * hidden * (1.0 - tanh * tanh) * (
            1.0 + 3.0 * GELU_A * square
        )
        gfin = gfin_low[...]
        acc_a[...] += dot(act, w_out)
        grad_hidden = (slope * dot_t(gfin, w_out)).astype(BF16)
        total = jnp.sum(grad_hidden.astype(F32), axis=0, keepdims=True)
        for a in range(per_panel):
            for q in range(per_unit):
                at = bias_line + k * per_unit + q
                first = (p * per_panel + a) * ws
                vec_g[at : at + 1, first : first + ws] = total[
                    :, a * UNIT + q * ws : a * UNIT + (q + 1) * ws
                ]
        grad_outer = dot(act.astype(F32).T.astype(BF16), gfin).astype(BF16)
        gc[k, planes, 0:UNIT] = grad_outer.reshape(per_panel, UNIT, width)
        grad_inner = dot(n2_t[...], grad_hidden).astype(BF16)
        gc[k, :, rows_in] = grad_inner.reshape(shards, ws, PANEL)
        acc_b[...] += dot_t(grad_hidden, w_in)

    outs = [local(out_ref, out_hbm, 15), local(gin_ref, gin_hbm, 16)]

    def reduction(refs, out, hbm, at, far_first):
        store = local(out, hbm, at)
        outs.append(store)
        return Reduce(net, *refs, out, far_first, store)

    reduce_c = [
        reduction(
            [ref.at[k] for ref in (gc, gc_core, gc_a, gc_b, gc_group, gc_far)],
            chunk_out.at[k],
            chunk_hbm.at[k],
            20 + k,
            chunk_far[k],
        )
        for k in range(chunks)
    ]
    for k in range(chunks):
        gather_c[k].end()
        for p in range(panels):
            feed(k, p)
        reduce_c[k].advance()
        if k:
            reduce_c[k - 1].advance()
    out_ref[...] = (valid * (resid[...] + acc_a[...] + bias_out)).astype(BF16)
    outs[0].start()
    gfin = cot_ref[...].astype(F32) * valid
    vec_g[vec_line + 4 : vec_line + 5, :] = jnp.sum(gfin, axis=0, keepdims=True)
    grad_n2 = acc_b[...]
    vec_g[vec_line + 3 : vec_line + 4, :] = jnp.sum(grad_n2, axis=0, keepdims=True)
    vec_g[vec_line + 2 : vec_line + 3, :] = jnp.sum(grad_n2 * xhat2[...], axis=0, keepdims=True)
    grad_hat = grad_n2 * gain2
    grad_hat = grad_hat - jnp.mean(grad_hat, axis=1, keepdims=True)
    grad_hat = grad_hat - xhat2[...] * jnp.mean(grad_hat * xhat2[...], axis=1, keepdims=True)
    grad_residual = gfin + grad_hat * small[0, :, 1:2]
    resid[...] = grad_residual
    n2[...] = grad_residual.astype(BF16)
    reduce_c[chunks - 1].advance()

    def branch(s, carry):
        part = mixed_t[pl.ds(s * experts, experts)].reshape(wos, tokens)
        go[s] = dot(part, n2[...]).astype(BF16)
        grad = dot_t(wo[s], n2[...])
        q_t[pl.ds(s * experts, experts)] = grad.reshape(experts, HS, tokens)
        return carry

    lax.fori_loop(0, shards, branch, 0)
    reduce_o = reduction(
        (go, go_core, go_a, go_b, go_group, go_far), wo_out, wo_hbm_out, 17, False
    )
    reduce_o.advance()

    def store_head_grad(j, value):
        sel_a[j] = value * small[1, pl.ds(j, 1), 0:tokens]
        small[1, pl.ds(2 * TOP + j, 1), 0:tokens] = jnp.sum(
            value * heads_t[j], axis=0, keepdims=True
        )

    choose(q_t, store_head_grad)
    reduce_c[0].advance()
    gates = small[1, 0:TOP, 0:tokens]
    grad_gates = small[1, 2 * TOP : 3 * TOP, 0:tokens]
    grad_picked = gates * (grad_gates - jnp.sum(gates * grad_gates, axis=0, keepdims=True))
    picks = small[1, TOP : 2 * TOP, 0:tokens]
    g_t[wide + 2 * HS :, :] = jnp.zeros((128, tokens), BF16)
    grad_logits = [
        jnp.sum(jnp.where(picks == float(e), grad_picked, 0.0), axis=0, keepdims=True)
        for e in range(E)
    ]
    grad_logits += [jnp.zeros((1, tokens), F32)] * (32 - E)
    g_t[wide + 2 * HS : wide + 2 * HS + 32, :] = jnp.concatenate(grad_logits, axis=0).astype(BF16)
    for s in range(2):
        for pair in range(TOP // 2):
            halves = swap(
                sel_a[2 * pair, :, s * seg : (s + 1) * seg],
                sel_a[2 * pair + 1, :, s * seg : (s + 1) * seg],
            )
            at = pair * 128
            for h in range(2):
                sh = 2 * s + h
                grad = (halves[h] * linv[sh, 0:1, at : at + 128]).astype(BF16)
                pads[sh, HS:, lanes + at : lanes + at + 128] = grad
                linv[sh, 1:2, at : at + 128] = jnp.sum(
                    grad.astype(F32) * hrow[sh, :, at : at + 128], axis=0, keepdims=True
                )
    reduce_o.advance()
    reduce_c[1 % chunks].advance()

    def attend_back(h):
        count, base = place(h)
        deltas = [linv[2 * s + h, 1:2, :] for s in range(2)]
        for s in range(2):
            hrow[2 * s + h] = jnp.zeros((HS, lanes), F32)

        def grad_step(step, carry):
            for s in range(2):
                sh = 2 * s + h
                expd = ebuf[s, base + step]
                grad_prob = dot(keys_of(step, s), pads[sh, :, lanes:])
                grad_score = (expd.astype(F32) * (grad_prob - deltas[s])).astype(BF16)
                dkv[step, s] += dot_t(jnp.concatenate([grad_score, expd], axis=1), pads[sh])
                hrow[sh] += dot(kvt[step, s, 0:HS], grad_score)
            return carry

        lax.fori_loop(0, count, grad_step, 0)

    attend_back(1)
    for k in range(chunks):
        reduce_c[k].advance()
    attend_back(0)

    for one in kv_sent:
        one.wait_send()

    def lower(step, carry):
        kvall[step] = dkv[step].astype(BF16).reshape(2, 2, half, 2 * HS)
        return carry

    lax.fori_loop(0, ctxs, lower, 0)
    dkv_cross = [
        net.send(part, from_sib.at[k], z, net.sibling())
        for k, part in enumerate(core_blocks(kvall, 1 - net.core))
    ]
    for s in range(2):
        for pair in range(TOP // 2):
            both = swap(
                hrow[2 * s, :, pair * 128 : (pair + 1) * 128],
                hrow[2 * s + 1, :, pair * 128 : (pair + 1) * 128],
            )
            for k in range(2):
                q_t[2 * pair + k, :, s * seg : (s + 1) * seg] = both[k] * scale

    def store_grad_query(e, value):
        g_t[many(e * HS, HS, HS), :] = value.astype(BF16)

    spread_back(q_t, store_grad_query)

    for k in range(2):
        net.wait(dkv_cross[k], from_sib.at[k])

    def add_sibling(step, carry):
        for k, sub in enumerate((net.core, 1 - net.core)):
            at = step + k * near_steps
            rows = many(sub * half, half, half)
            for s in range(2):
                value = dkv[at, s, rows] + from_sib[k, step, s].astype(F32)
                dkv[at, s, rows] = value
                kvall[at, s, sub] = value.astype(BF16)
        return carry

    lax.fori_loop(0, near_steps, add_sibling, 0)
    dkv_slots = []
    for step in range(1, near_steps):
        peer = (c + 2 * step) % ctxs
        dkv_slots.append(
            [
                net.send(at_block(kvall, block), from_kv.at[step - 1, h], z, peer)
                for h, block in enumerate((peer, blocks - 1 - peer))
            ]
        )

    def query_grad(n, carry):
        at = many(n * 256, 256, 256)
        grad = dot_t(normed_t[...], g_t[at, :]).astype(BF16)
        gq[:, :, at] = grad.reshape(shards, ws, 256)
        return carry

    lax.fori_loop(0, wide // 256, query_grad, 0)
    reduce_q = reduction((gq, gq_core, gq_a, gq_b, gq_group, gq_far), q_out, q_hbm, 18, False)
    reduce_q.advance()
    reduce_o.advance()

    heads_t[...] = jnp.zeros(heads_t.shape, F32)

    def norm_grad(n, carry):
        at = many(n * 256, 256, 256)
        part = dot(wq[:, :, at].reshape(width, 256), g_t[at, :])
        heads_t[...] += part.reshape(heads_t.shape)
        return carry

    lax.fori_loop(0, wide // 256, norm_grad, 0)
    reduce_q.advance()
    for step in range(1, near_steps):
        for h in range(2):
            net.wait(dkv_slots[step - 1][h], from_kv.at[step - 1, h])
    for h in range(2):
        block = my_block(h)
        for s in range(2):
            value = dkv[block // 2, s, many((block % 2) * half, half, half)]
            for step in range(1, near_steps):
                value = value + from_kv[step - 1, h, s].astype(F32)
            first = s * seg + h * half
            acc_a[first : first + half, 0:128] = value
    g_t[wide : wide + 2 * HS, :] = acc_a[:, 0:128].T.astype(BF16)
    tail = g_t[wide:, :]
    part = heads_t[...].reshape(width, tokens) + dot(wk[...].reshape(width, 256), tail)
    grad_normed = part.T
    hat = first_hat()
    vec_g[vec_line : vec_line + 1, :] = jnp.sum(grad_normed * hat, axis=0, keepdims=True)
    vec_g[vec_line + 1 : vec_line + 2, :] = jnp.sum(grad_normed, axis=0, keepdims=True)
    tail_grad = dot_t(normed_t[...], tail)
    gk[:, :, 0 : 2 * HS] = tail_grad[:, 0 : 2 * HS].astype(BF16).reshape(shards, ws, 2 * HS)
    tail_grad = tail_grad[:, 2 * HS :] + vec_g[...].T
    gk[:, :, 2 * HS :] = tail_grad.astype(BF16).reshape(shards, ws, 128)
    reduce_k = reduction((gk, gk_core, gk_a, gk_b, gk_group, gk_far), kv_out, kv_hbm, 19, False)
    reduce_k.advance()
    grad_hat = grad_normed * gain1
    grad_hat = grad_hat - jnp.mean(grad_hat, axis=1, keepdims=True)
    grad_hat = grad_hat - hat * jnp.mean(grad_hat * hat, axis=1, keepdims=True)
    gin_ref[...] = resid[...] + grad_hat * small[0, :, 0:1]
    outs[1].start()

    everything = [*reduce_c, reduce_o, reduce_q, reduce_k]
    while any(one.stage < len(one.steps) for one in everything):
        for one in everything:
            one.advance()
    net.finish()
    for one in outs:
        one.wait()


def unpack_kernel(shards, *refs):
    ins, outs = refs[0:6], refs[6:20]
    in_st, out_st, sem = refs[20:26], refs[26:40], refs[40]
    loads = [pltpu.make_async_copy(a, b, sem.at[k]) for k, (a, b) in enumerate(zip(ins, in_st))]
    stores = [
        pltpu.make_async_copy(in_st[k] if k < 2 else out_st[k], outs[k], sem.at[6 + k])
        for k in range(14)
    ]
    for k in (2, 3, 4, 5, 1, 0):
        loads[k].start()
    chunk_in, wo_in, q_in, kv_in = in_st[2:]
    g1_ref, b1_ref, kv_ref, q_ref, r_ref, wo_ref, g2_ref, b2_ref = out_st[2:10]
    wi_ref, bi_ref, wout_ref, bo_ref = out_st[10:]
    ws, fs = q_ref.shape[0], wout_ref.shape[0]
    per_panel = PANEL // UNIT
    loads[2].wait()
    for k in range(chunk_in.shape[0]):
        wout_ref[k * UNIT : (k + 1) * UNIT, :] = chunk_in[k, 0:UNIT].astype(F32)
    stores[12].start()
    for k in range(chunk_in.shape[0]):
        for s in range(shards):
            first = UNIT + (s // per_panel) * ws
            at = (s % per_panel) * UNIT
            wi_ref[:, s * fs + k * UNIT : s * fs + (k + 1) * UNIT] = chunk_in[
                k, first : first + ws, at : at + UNIT
            ].astype(F32)
    stores[10].start()
    loads[3].wait()
    wo_ref[...] = wo_in[...].astype(F32)
    stores[7].start()
    loads[4].wait()
    q_ref[...] = q_in[...].astype(F32)
    stores[5].start()
    loads[5].wait()
    kv_ref[...] = kv_in[:, 0 : 2 * HS].astype(F32)
    stores[4].start()
    turned = kv_in[:, 2 * HS :].astype(F32).T
    r_ref[...] = turned[0:E]
    stores[6].start()
    for row, at, ref in (
        (0, 2, g1_ref),
        (1, 3, b1_ref),
        (2, 8, g2_ref),
        (3, 9, b2_ref),
        (4, 13, bo_ref),
    ):
        ref[...] = turned[E + row : E + row + 1]
        stores[at].start()
    for line in range(fs // ws):
        bi_ref[:, line * ws : (line + 1) * ws] = turned[E + 5 + line : E + 6 + line]
    stores[11].start()
    loads[1].wait()
    stores[1].start()
    loads[0].wait()
    stores[0].start()
    for one in stores:
        one.wait()


def on_device(
    shards,
    ctxs,
    tokens,
    lengths,
    expert_picks,
    first_gain,
    first_bias,
    kv_weight,
    query_weight,
    router_weight,
    output_weight,
    second_gain,
    second_bias,
    inner_weight,
    inner_bias,
    outer_weight,
    outer_bias,
    cotangent,
):
    slots, seg, width = tokens.shape
    count = slots * seg
    half = seg // 2
    lanes = TOP * half
    ws = width // shards
    wos = output_weight.shape[0]
    fs = outer_weight.shape[0]
    group = min(ctxs, ws // 16, 8)
    pairs, groups = group // 2, ctxs // group
    rounds = groups.bit_length() - 1
    chunks = fs // UNIT
    panels = shards * UNIT // PANEL
    chunk_rows = UNIT + panels * ws
    wide = E * HS
    chunk_far = [False] * chunks
    shapes_mid = (
        jax.ShapeDtypeStruct((count, width), BF16),
        jax.ShapeDtypeStruct((count, width), F32),
        jax.ShapeDtypeStruct((chunks, chunk_rows, PANEL), BF16),
        jax.ShapeDtypeStruct((wos, width), BF16),
        jax.ShapeDtypeStruct((ws, wide), BF16),
        jax.ShapeDtypeStruct((ws, 256), BF16),
    )

    smem = pl.BlockSpec(memory_space=pltpu.SMEM)
    anywhere = pl.BlockSpec(memory_space=pl.ANY)
    spread = {1: 0, 2: 1, 4: 3}[pairs]
    copies = (
        (3 + chunks) * (shards - 1) * (spread + 2)
        + (3 + chunks) * (reduce_copies(shards, group, rounds) + 1)
        + 4 * (ctxs // 2 - 1)
        + 4
        + (shards - 1)
    )
    scratch = [
        pltpu.VMEM((count, width), BF16),
        pltpu.VMEM((count, width), BF16),
        pltpu.VMEM((slots, TOP, seg), jnp.int32),
        *[pltpu.VMEM((1, ws), F32)] * 5,
        pltpu.VMEM((1, fs), F32),
        pltpu.VMEM(query_weight.shape, F32),
        pltpu.VMEM(kv_weight.shape, F32),
        pltpu.VMEM((E, ws), F32),
        pltpu.VMEM(inner_weight.shape, F32),
        pltpu.VMEM((max(wos + fs, 3 * count), width), F32),
        pltpu.VMEM((shards, ws, 256), BF16),
        pltpu.VMEM((shards, ws, wide), BF16),
        pltpu.VMEM((shards, wos, width), BF16),
        pltpu.VMEM((chunks, shards, chunk_rows, PANEL), BF16),
        pltpu.VMEM((shards, 8, fs), F32),
        pltpu.VMEM((count, width), BF16),
        pltpu.VMEM((width, count), BF16),
        pltpu.VMEM((E, HS, count), F32),
        pltpu.VMEM((TOP, HS, count), F32),
        pltpu.VMEM((TOP, HS, count), F32),
        pltpu.VMEM((2, count, count), F32),
        pltpu.VMEM((ctxs, slots, 2, half, 2 * HS), BF16),
        pltpu.VMEM((ctxs, slots, 2 * HS, 2 * half), BF16),
        pltpu.VMEM((4, 2 * HS, 2 * lanes), BF16),
        pltpu.VMEM((4, HS, lanes), F32),
        pltpu.VMEM((4, 8, lanes), F32),
        pltpu.VMEM((slots, ctxs + 1, 2 * half, lanes), BF16),
        pltpu.VMEM((ctxs, slots, 2 * half, 2 * HS), F32),
        pltpu.VMEM((2, ctxs // 2, slots, half, 2 * HS), BF16),
        pltpu.VMEM((ctxs // 2 - 1, 2, slots, half, 2 * HS), BF16),
        pltpu.VMEM((E, HS, count), BF16),
        pltpu.VMEM((count, width), F32),
        pltpu.VMEM((count, width), BF16),
        pltpu.VMEM((width, count), BF16),
        pltpu.VMEM((count, width), BF16),
        pltpu.VMEM((8, PANEL), F32),
        pltpu.VMEM((wide + 256, count), BF16),
        *reduce_scratch(shards, group, rounds, chunk_rows, PANEL, False, (chunks,)),
        *reduce_scratch(shards, group, rounds, wos, width, False),
        *reduce_scratch(shards, group, rounds, ws, wide, False),
        *reduce_scratch(shards, group, rounds, ws, 256, False),
        *[pltpu.VMEM(one.shape, one.dtype) for one in shapes_mid],
        pltpu.VMEM((128, width), F32),
        pltpu.SemaphoreType.DMA((20 + chunks,)),
        pltpu.SemaphoreType.DMA((copies,)),
        pltpu.SemaphoreType.DMA((copies,)),
    ]
    results = pl.pallas_call(
        functools.partial(layer_kernel, shards, ctxs, group, chunk_far),
        out_shape=shapes_mid,
        in_specs=[smem] + [anywhere] * 15,
        out_specs=tuple([anywhere] * 6),
        scratch_shapes=scratch,
        compiler_params=pltpu.CompilerParams(
            collective_id=0, has_side_effects=True, vmem_limit_bytes=63 * 1024 * 1024
        ),
        name="layer",
    )(
        lengths,
        tokens.reshape(count, width),
        cotangent.reshape(count, width),
        jnp.swapaxes(expert_picks, 1, 2),
        first_gain.reshape(1, ws),
        first_bias.reshape(1, ws),
        second_gain.reshape(1, ws),
        second_bias.reshape(1, ws),
        outer_bias.reshape(1, ws),
        inner_bias.reshape(1, fs),
        query_weight,
        kv_weight,
        router_weight.T,
        output_weight,
        inner_weight,
        outer_weight,
    )
    vec_shape = jax.ShapeDtypeStruct((1, ws), F32)
    shapes_out = (
        jax.ShapeDtypeStruct((count, width), BF16),
        jax.ShapeDtypeStruct((count, width), F32),
        vec_shape,
        vec_shape,
        jax.ShapeDtypeStruct(kv_weight.shape, F32),
        jax.ShapeDtypeStruct(query_weight.shape, F32),
        jax.ShapeDtypeStruct((E, ws), F32),
        jax.ShapeDtypeStruct(output_weight.shape, F32),
        vec_shape,
        vec_shape,
        jax.ShapeDtypeStruct(inner_weight.shape, F32),
        jax.ShapeDtypeStruct((1, fs), F32),
        jax.ShapeDtypeStruct(outer_weight.shape, F32),
        vec_shape,
    )
    final = pl.pallas_call(
        functools.partial(unpack_kernel, shards),
        out_shape=shapes_out,
        in_specs=[anywhere] * 6,
        out_specs=tuple([anywhere] * 14),
        scratch_shapes=[pltpu.VMEM(one.shape, one.dtype) for one in (*shapes_mid, *shapes_out)]
        + [pltpu.SemaphoreType.DMA((20,))],
        name="unpack",
    )(*results)
    final = list(final)
    final[6] = final[6].T
    shapes = (
        tokens.shape,
        tokens.shape,
        first_gain.shape,
        first_bias.shape,
        kv_weight.shape,
        query_weight.shape,
        router_weight.shape,
        output_weight.shape,
        second_gain.shape,
        second_bias.shape,
        inner_weight.shape,
        inner_bias.shape,
        outer_weight.shape,
        outer_bias.shape,
    )
    return tuple(value.reshape(shape) for value, shape in zip(final, shapes))


def solution(mesh):
    rows = P("shard", "ctx", None)
    vec, mat = P("shard"), P("shard", None)
    return jax.shard_map(
        functools.partial(on_device, mesh.shape["shard"], mesh.shape["ctx"]),
        mesh=mesh,
        in_specs=(
            rows,
            vec,
            rows,
            vec,
            vec,
            mat,
            mat,
            mat,
            mat,
            vec,
            vec,
            mat,
            vec,
            mat,
            vec,
            rows,
        ),
        out_specs=(
            rows,
            rows,
            vec,
            vec,
            mat,
            mat,
            mat,
            mat,
            vec,
            vec,
            mat,
            vec,
            mat,
            vec,
        ),
        check_vma=False,
    )
```

time: 160 us -> 120 us (0.75)
  Pallas kernels: 154 us -> 119 us
  local copies, waits for them, and re-layouts: 4.43 us -> 0 us
    pallas_call x2, Pallas kernels: 154 us -> 119 us  [the longest x1 115 us: on_device(): pl.pallas_call(functools.partial(layer_kernel, shards, ctxs, group, chunk...]
    unnamed x3 -> x0, local copies, waits for them, and re-layouts: 4.43 us -> none
where the time goes in v2:
time: 120 us
  Pallas kernels  119 us (99%)
    pallas_call x1, Pallas kernels, on_device(): pl.pallas_call(functools.partial(layer_kernel, shards, ctxs, group, chunk...  115 us
    pallas_call x1, Pallas kernels, on_device(): pl.pallas_call(functools.partial(unpack_kernel, shards), out_shape=shapes...  3.63 us

profile of v2, /device:TPU:0, one launch (start us, length us, event | category | flops | bytes accessed | tf_op | source)
XLA Modules:
  0.0 119.8 jit_solution(17601408923346473299)
XLA Ops:
  0.7 115.4 %layer.1 = (bf16[256,512]{1,0:T(8,128)(2,1)}, f32[256,512]{1,0:T(8,128)}, bf16[4,256,512]{2,1,0:T(8,128)(2,1)}, bf16[384,512]{1,0:T(8,128)(2,1)}, bf16[128,1536]{1,0:T(8,128)(2,1)}, /*index=5*/bf16[128,256]{1,0:T(8,128)(2,1)}) custom-call(s32[2]{0:T(128)} %len_ref.1, bf16[256,512]{1,0:T(8,128)(2,1)} %bitcast.19, bf16[256,512]{1,0:T(8,128)(2,1)} %bitcast.20, ...), custom_call_target="tpu_custom_call" | custom-call | tf_op jit(solution)/shard_map/layer/pallas_call | solution.py:1261
  116.0 3.6 %unpack.1 = (bf16[256,512]{1,0:T(8,128)(2,1)}, f32[256,512]{1,0:T(8,128)}, f32[1,128]{1,0:T(1,128)}, f32[1,128]{1,0:T(1,128)}, f32[128,128]{1,0:T(8,128)}, /*ind...) custom-call(bf16[256,512]{1,0:T(8,128)(2,1)} %get-tuple-element.34.r, ...), custom_call_target="tpu_custom_call" | custom-call | tf_op jit(solution)/shard_map/unpack/pallas_call | solution.py:1306

commit v3 on v2

--- a/solution.py
+++ b/solution.py
@@ -19,6 +19,7 @@
 GELU_C = 0.7978845608028654
 GELU_A = 0.044715
 MESH = pl.DeviceIdType.MESH
+RING = 40
 
 
 def dot(left, right):
@@ -45,8 +46,9 @@
         self.chip = (self.i % group) // 2
         self.grp = self.i // group
         self.send_sem, self.recv_sem = send_sem, recv_sem
-        self.used = 0
-        self.sent = []
+        self.arrivals = 0
+        self.starts = 0
+        self.ring = [[] for _ in range(RING)]
         flip_low = self.chip + 1 - 2 * (self.chip % 2)
         if self.dims == 2:
             flip_high = self.chip + 2 - 4 * (self.chip // 2)
@@ -68,31 +70,39 @@
     def sibling(self):
         return self.i + 1 - 2 * self.core
 
-    def copy(self, src, dst, slot, z, i):
+    def copy(self, src, dst, sent, arrived, z, i):
         return pltpu.make_async_remote_copy(
             src_ref=src,
             dst_ref=dst,
-            send_sem=self.send_sem.at[slot],
-            recv_sem=self.recv_sem.at[slot],
+            send_sem=self.send_sem.at[sent],
+            recv_sem=self.recv_sem.at[arrived],
             device_id={"shard": z, "ctx": i},
             device_id_type=MESH,
         )
 
-    def send(self, src, dst, z, i):
-        slot = self.used
-        self.used += 1
-        one = self.copy(src, dst, slot, z, i)
-        one.start()
-        self.sent.append(one)
-        return slot
-
-    def wait(self, slot, dst):
-        self.copy(dst, dst, slot, self.z, self.i).wait_recv()
+    def arrival(self):
+        self.arrivals += 1
+        return self.arrivals - 1
+
+    def send(self, src, dst, arrived, z, i):
+        slot = self.starts % RING
+        self.starts += 1
+        if self.ring[slot]:
+            self.left(self.ring[slot])
+        one = self.ring[slot] = [self.copy(src, dst, slot, arrived, z, i)]
+        one[0].start()
+        return one
+
+    def left(self, one):
+        if one:
+            one.pop().wait_send()
+
+    def wait(self, arrived, dst):
+        self.copy(dst, dst, 0, arrived, self.z, self.i).wait_recv()
 
     def finish(self):
-        for one in self.sent:
-            one.wait_send()
-        self.sent = []
+        for one in self.ring:
+            self.left(one)
 
     def greet(self):
         barrier = pltpu.get_barrier_semaphore()
@@ -116,94 +126,74 @@
 
 
 class Spread:
-    def __init__(self, net, ref):
-        self.net, self.ref = net, ref
-        self.piece = ref.shape[0] // net.group
-        self.half = ref.shape[0] // 2
+    def __init__(self, net, refs, all_of):
+        self.net, self.refs, self.all_of = net, refs, all_of
+        self.piece = refs[0].shape[0] // net.group
+        self.half = refs[0].shape[0] // 2
 
     def part(self, chip):
-        first = (self.net.core * self.net.pairs + chip) * self.piece
-        return self.ref.at[many(first, self.piece, self.piece)]
+        return many((self.net.core * self.net.pairs + chip) * self.piece, self.piece, self.piece)
 
     def block(self, core):
-        return self.ref.at[many(core * self.half, self.half, self.half)]
+        return many(core * self.half, self.half, self.half)
+
+    def give(self, rows, peer):
+        arrived = self.net.arrival()
+        for ref in self.refs:
+            self.net.send(ref.at[rows], ref.at[rows], arrived, self.net.z, peer)
+        return arrived
 
     def begin(self):
         net = self.net
         own = self.part(net.chip)
         if net.dims == 2:
-            self.to_a = net.send(own, own, net.z, net.peer(net.chip_a))
+            self.to_a = self.give(own, net.peer(net.chip_a))
         if net.dims:
-            self.to_b = net.send(own, own, net.z, net.peer(net.chip_b))
+            self.to_b = self.give(own, net.peer(net.chip_b))
 
     def pass_on(self):
         net = self.net
         if net.dims == 2:
             got = self.part(net.chip_a)
-            net.wait(self.to_a, got)
-            self.on = net.send(got, got, net.z, net.peer(net.chip_b))
+            net.wait(self.to_a, self.all_of(got))
+            self.on = self.give(got, net.peer(net.chip_b))
 
     def share(self):
         net = self.net
         if net.dims:
-            net.wait(self.to_b, self.part(net.chip_b))
+            net.wait(self.to_b, self.all_of(self.part(net.chip_b)))
         if net.dims == 2:
-            net.wait(self.on, self.part(net.chip_ab))
-        block = self.block(net.core)
-        self.to_core = net.send(block, block, net.z, net.sibling())
+            net.wait(self.on, self.all_of(self.part(net.chip_ab)))
+        self.cross()
+
+    def cross(self):
+        self.to_core = self.give(self.block(self.net.core), self.net.sibling())
 
     def end(self):
-        self.net.wait(self.to_core, self.block(1 - self.net.core))
+        self.net.wait(self.to_core, self.all_of(self.block(1 - self.net.core)))
 
 
 class Gather:
-    def __init__(self, net, buf):
-        self.net, self.buf = net, buf
-        self.spreads = [Spread(net, buf.at[net.src(k)]) for k in range(1, net.shards)]
+    def __init__(self, net, buf, by_core=False):
+        self.net, self.buf, self.by_core = net, buf, by_core
+        planes = [buf.at[net.src(k)] for k in range(1, net.shards)]
+        self.spread = Spread(net, planes, lambda rows: buf.at[0 : net.shards - 1, rows])
+        self.pass_on, self.share, self.end = self.spread.pass_on, self.spread.share, self.spread.end
+        self.rows = self.spread.block(net.core) if by_core else self.spread.part(net.chip)
 
     def start(self):
         net = self.net
-        own = Spread(net, self.buf.at[net.z]).part(net.chip)
-        self.slots = [net.send(own, own, net.far(k), net.i) for k in range(1, net.shards)]
+        own = self.buf.at[net.z, self.rows]
+        self.far = net.arrival()
+        for k in range(1, net.shards):
+            net.send(own, own, self.far, net.far(k), net.i)
 
     def begin(self):
-        for slot, spread in zip(self.slots, self.spreads):
-            self.net.wait(slot, spread.part(self.net.chip))
-            spread.begin()
-
-    def pass_on(self):
-        for spread in self.spreads:
-            spread.pass_on()
-
-    def share(self):
-        for spread in self.spreads:
-            spread.share()
-
-    def end(self):
-        for spread in self.spreads:
-            spread.end()
-
-
-class CoreGather:
-    def __init__(self, net, buf):
-        self.net, self.buf = net, buf
-        self.spreads = [Spread(net, buf.at[net.src(k)]) for k in range(1, net.shards)]
-
-    def start(self):
-        net = self.net
-        own = Spread(net, self.buf.at[net.z]).block(net.core)
-        self.slots = [net.send(own, own, net.far(k), net.i) for k in range(1, net.shards)]
-
-    def share(self):
-        net = self.net
-        for slot, spread in zip(self.slots, self.spreads):
-            block = spread.block(net.core)
-            net.wait(slot, block)
-            spread.to_core = net.send(block, block, net.z, net.sibling())
-
-    def end(self):
-        for spread in self.spreads:
-            spread.end()
+        self.net.wait(self.far, self.spread.all_of(self.rows))
+        if self.by_core:
+            self.spread.cross()
+        else:
+            self.spread.begin()
 
 
 class Reduce:
@@ -216,7 +206,7 @@
         self.from_group, self.from_far = from_group, from_far
         self.piece = grad.shape[1] // net.group
         self.half = grad.shape[1] // 2
-        self.spread = Spread(net, out)
+        self.spread = Spread(net, [out], lambda rows: out.at[rows])
         near = [self.take_a, self.take_b] if net.dims == 2 else [self.take_b]
         steps = [self.take_far] + near if far_first else near + [self.take_far]
         self.steps = [self.start, self.take_core] + steps
@@ -274,7 +264,8 @@
     def start(self):
         net = self.net
         away = many((1 - net.core) * self.half, self.half, self.half)
-        self.to_core = net.send(self.grad.at[:, away], self.from_core, net.z, net.sibling())
+        self.to_core = net.arrival()
+        net.send(self.grad.at[:, away], self.from_core, self.to_core, net.z, net.sibling())
 
     def take_core(self):
         net = self.net
@@ -289,22 +280,24 @@
     def send_near(self, after_far):
         net = self.net
         if net.dims == 2:
-            self.to_a = [
+            self.to_a = [net.arrival(), net.arrival()]
+            for k, chip in ((1, net.chip_ab), (0, net.chip_a)):
                 net.send(
                     self.cut(self.rows(chip), after_far),
                     self.from_a.at[k],
+                    self.to_a[k],
                     net.z,
                     net.peer(net.chip_a),
                 )
-                for k, chip in enumerate((net.chip_a, net.chip_ab))
-            ]
         elif net.dims == 1:
             self.send_b(after_far)
 
     def send_b(self, after_far):
         net = self.net
-        self.to_b = net.send(
-            self.cut(self.rows(net.chip_b), after_far), self.from_b, net.z, net.peer(net.chip_b)
+        self.to_b = net.arrival()
+        rows = self.rows(net.chip_b)
+        net.send(
+            self.cut(rows, after_far), self.from_b, self.to_b, net.z, net.peer(net.chip_b)
         )
 
     def take_a(self):
@@ -326,9 +319,12 @@
         step, at = 1, 0
         while step < net.groups:
             peer = net.i + net.group * step * (1 - 2 * ((net.grp // step) % 2))
-            slot = net.send(self.cut(own, self.far_first), self.from_group.at[at], net.z, peer)
-            net.wait(slot, self.from_group.at[at])
-            net.sent.pop().wait_send()
+            arrived = net.arrival()
+            one = net.send(
+                self.cut(own, self.far_first), self.from_group.at[at], arrived, net.z, peer
+            )
+            net.wait(arrived, self.from_group.at[at])
+            net.left(one)
             self.add(
                 self.first(net.chip),
                 self.piece,
@@ -344,20 +340,19 @@
     def send_far(self, own):
         net = self.net
         self.own = own
-        self.to_far = [
+        self.to_far = net.arrival()
+        for k in range(1, net.shards):
             net.send(
                 self.grad.at[pl.ds(net.far(k), 1), own],
                 self.from_far.at[pl.ds(k - 1, 1)],
+                self.to_far,
                 net.far(k),
                 net.i,
             )
-            for k in range(1, net.shards)
-        ]
 
     def take_far(self):
         net = self.net
-        for k in range(1, net.shards):
-            net.wait(self.to_far[k - 1], self.from_far.at[pl.ds(k - 1, 1)])
+        net.wait(self.to_far, self.from_far)
         parts = [self.from_far.at[pl.ds(k, 1)] for k in range(net.shards - 1)]
         if self.far_first:
             self.add(net.core * self.half, self.half, self.planes(True), parts)
@@ -367,26 +362,19 @@
             self.out[self.own, :] = self.grad[net.z, self.own]
 
 
-def reduce_scratch(shards, group, rounds, rows, wide, far_first, lead=()):
+def reduce_scratch(shards, group, rounds, rows, wide, far_first):
     pairs = group // 2
     piece, half = rows // group, rows // 2
-    far_rows = half if far_first else piece
     planes = 1 if far_first else shards
-    tiny = (*lead, 1, 16, 128)
+    tiny = (1, 16, 128)
     return [
-        pltpu.VMEM((*lead, shards, rows, wide), BF16),
-        pltpu.VMEM((*lead, shards, half, wide), BF16),
-        pltpu.VMEM((*lead, 2, planes, piece, wide) if pairs == 4 else tiny, BF16),
-        pltpu.VMEM((*lead, planes, piece, wide), BF16),
-        pltpu.VMEM((*lead, rounds, planes, piece, wide) if rounds else tiny, BF16),
-        pltpu.VMEM((*lead, shards - 1, far_rows, wide), BF16),
+        pltpu.VMEM((shards, rows, wide), BF16),
+        pltpu.VMEM((shards, half, wide), BF16),
+        pltpu.VMEM((2, planes, piece, wide) if pairs == 4 else tiny, BF16),
+        pltpu.VMEM((planes, piece, wide), BF16),
+        pltpu.VMEM((rounds, planes, piece, wide) if rounds else tiny, BF16),
+        pltpu.VMEM((shards - 1, half if far_first else piece, wide), BF16),
     ]
-
-
-def reduce_copies(shards, group, rounds):
-    pairs = group // 2
-    near = {1: 0, 2: 1, 4: 3}[pairs]
-    return 2 * (near + 1) + rounds + shards - 1
 
 
 def layer_kernel(
@@ -434,6 +422,7 @@
     wq,
     wo,
     wc,
+    vec_st,
     vecs,
     normed,
     normed_t,
@@ -457,30 +446,10 @@
     gfin_low,
     biases,
     g_t,
-    gc,
-    gc_core,
-    gc_a,
-    gc_b,
-    gc_group,
-    gc_far,
-    go,
-    go_core,
-    go_a,
-    go_b,
-    go_group,
-    go_far,
-    gq,
-    gq_core,
-    gq_a,
-    gq_b,
-    gq_group,
-    gq_far,
-    gk,
-    gk_core,
-    gk_a,
-    gk_b,
-    gk_group,
-    gk_far,
+    sums_c,
+    sums_o,
+    sums_q,
+    sums_k,
     out_ref,
     gin_ref,
     chunk_out,
@@ -507,6 +476,7 @@
     per_panel = PANEL // UNIT
     lanes = TOP * half
     wide = E * HS
+    gc, go, gq, gk = [one[0] for one in sums_c], sums_o[0], sums_q[0], sums_k[0]
     vec_line = E
     bias_line = vec_line + 5
     per_unit = UNIT // ws
@@ -541,22 +511,28 @@
         loads[id(dst)] = local(src, dst, at)
         loads[id(dst)].start()
     loads[id(wkv_st)].wait()
-    loads[id(wr_st)].wait()
-    wk[z, :, 0 : 2 * HS] = wkv_st[...].astype(BF16)
-    padded = jnp.concatenate([wr_st[...], jnp.zeros((128 - E, ws), F32)], axis=0)
-    wk[z, :, 2 * HS :] = padded.T.astype(BF16)
+    wk[z] = wkv_st[...].astype(BF16)
+    vec_st[...] = jnp.zeros(vec_st.shape, F32)
+    for row, ref in enumerate((g1_ref, b1_ref, g2_ref, b2_ref, bo_ref)):
+        loads[id(ref)].wait()
+        vec_st[row : row + 1, 0:ws] = ref[...]
+    loads[id(bi_ref)].wait()
+    for k in range(chunks):
+        vec_st[5 + k : 6 + k, :] = bi_ref[:, k * UNIT : (k + 1) * UNIT]
     own_vec = vecs.at[z]
-    own_vec[...] = jnp.zeros(own_vec.shape, F32)
-    for row, ref in enumerate((g1_ref, b1_ref, g2_ref, b2_ref, bo_ref, bi_ref)):
-        loads[id(ref)].wait()
-        own_vec[row : row + 1, 0 : ref.shape[1]] = ref[...].astype(BF16).astype(F32)
+    own_vec[...] = vec_st[...].astype(BF16)
     net.greeted()
-    gather_k, gather_q, gather_o = CoreGather(net, wk), Gather(net, wq), Gather(net, wo)
+    gather_k, gather_q, gather_o = Gather(net, wk, True), Gather(net, wq), Gather(net, wo)
     gather_c = [Gather(net, wc.at[k]) for k in range(chunks)]
     gather_k.start()
-    vec_slots = [net.send(own_vec, own_vec, net.far(k), net.i) for k in range(1, shards)]
+    vec_slot = net.arrival()
+    for k in range(1, shards):
+        net.send(own_vec, own_vec, vec_slot, net.far(k), net.i)
     loads[id(wq_st)].wait()
-    wq[z] = wq_st[...].astype(BF16)
+    loads[id(wr_st)].wait()
+    wq[z, :, 0:wide] = wq_st[...].astype(BF16)
+    padded = jnp.concatenate([wr_st[...], jnp.zeros((128 - E, ws), F32)], axis=0)
+    wq[z, :, wide:] = padded.T.astype(BF16)
     gather_q.start()
 
     loads[id(x_ref)].wait()
@@ -580,21 +556,19 @@
             wc[k, z, first : first + ws, at : at + UNIT] = wi_st[
                 :, s * fs + k * UNIT : s * fs + (k + 1) * UNIT
             ].astype(BF16)
-    gather_k.share()
-    for k in range(1, shards):
-        net.wait(vec_slots[k - 1], vecs.at[net.src(k)])
+    gather_k.begin()
+    net.wait(vec_slot, vecs.at[0 : shards - 1])
+
+    vec_all = [vecs[s].astype(F32) for s in range(shards)]
 
     def whole(row):
-        return jnp.concatenate([vecs[s, row : row + 1, 0:ws] for s in range(shards)], axis=1)
+        return jnp.concatenate([one[row : row + 1, 0:ws] for one in vec_all], axis=1)
 
     gain1, bias1, gain2, bias2, bias_out = (whole(row) for row in range(5))
     for k in range(chunks):
         for p in range(panels):
             biases[k * panels + p : k * panels + p + 1, :] = jnp.concatenate(
-                [
-                    vecs[s, 5:6, k * UNIT : (k + 1) * UNIT]
-                    for s in range(p * per_panel, (p + 1) * per_panel)
-                ],
+                [one[5 + k : 6 + k] for one in vec_all[p * per_panel : (p + 1) * per_panel]],
                 axis=1,
             )
     norm_value = first_hat() * gain1 + bias1
@@ -602,8 +576,7 @@
     normed_t[...] = norm_value.T.astype(BF16)
     gather_k.end()
 
-    kvr = dot(normed[...], wk[...].reshape(width, 256))
-    kv_own = kvr[:, 0 : 2 * HS].astype(BF16)
+    kv_own = dot(normed[...], wk[...].reshape(width, 2 * HS)).astype(BF16)
 
     def at_block(ref, block):
         return ref.at[block // 2, :, block % 2]
@@ -619,20 +592,42 @@
         for s in range(2):
             first = s * seg + h * half
             kvall[block // 2, s, block % 2] = kv_own[first : first + half]
-    kv_first = len(net.sent)
-    kv_slots = []
+    kv_slot, kv_cross = net.arrival(), net.arrival()
+    kv_sent = []
     for step in range(1, near_steps):
-        kv_slots.append(
-            [
-                net.send(at_block(kvall, block), at_block(kvall, block), z, (c + 2 * step) % ctxs)
-                for block in (c, blocks - 1 - c)
-            ]
-        )
-    kv_sent = net.sent[kv_first:]
-    del net.sent[kv_first:]
+        for block in (c, blocks - 1 - c):
+            ref = at_block(kvall, block)
+            kv_sent.append(net.send(ref, ref, kv_slot, z, (c + 2 * step) % ctxs))
+    gather_o.start()
     gather_q.begin()
-    gather_o.start()
-    logits_t = kvr[:, 2 * HS : 2 * HS + 128].T
+    gather_c[0].start()
+    net.wait(kv_slot, kvall.at[0 : near_steps - 1])
+    for part in core_blocks(kvall, net.core):
+        kv_sent.append(net.send(part, part, kv_cross, z, net.sibling()))
+    gather_q.pass_on()
+    net.wait(kv_cross, kvall.at[0:near_steps])
+
+    def turn(step, carry):
+        for s in range(2):
+            keys = kvall[step, s].reshape(2 * half, 2 * HS)
+            kvt[step, s] = keys.astype(F32).T.astype(BF16)
+            dkv[step, s] = jnp.zeros((2 * half, 2 * HS), F32)
+        return carry
+
+    lax.fori_loop(0, ctxs, turn, 0)
+
+    def serve(*calls):
+        for k, call in calls:
+            if k < chunks:
+                getattr(gather_c[k], call)()
+
+    gather_o.begin()
+    serve((1, "start"))
+    gather_q.share()
+    serve((0, "begin"), (2, "start"))
+    gather_q.end()
+
+    logits_t = dot(normed[...], wq[:, :, wide:].reshape(width, 128)).T
     loads[id(picks_ref)].wait()
     picks = jnp.concatenate([picks_ref[0], picks_ref[1]], axis=1).astype(F32)
     picked = jnp.zeros((TOP, tokens), F32)
@@ -642,31 +637,6 @@
     gexp = jnp.exp(picked - top)
     small[1, 0:TOP, 0:tokens] = gexp / jnp.sum(gexp, axis=0, keepdims=True)
     small[1, TOP : 2 * TOP, 0:tokens] = picks
-    for step in range(1, near_steps):
-        source = (c + ctxs - 2 * step) % ctxs
-        for slot, block in zip(kv_slots[step - 1], (source, blocks - 1 - source)):
-            net.wait(slot, at_block(kvall, block))
-    kv_cross = [net.send(part, part, z, net.sibling()) for part in core_blocks(kvall, net.core)]
-    kv_sent += net.sent[-2:]
-    del net.sent[-2:]
-    gather_q.pass_on()
-    gather_c[0].start()
-    for slot, part in zip(kv_cross, core_blocks(kvall, 1 - net.core)):
-        net.wait(slot, part)
-
-    def turn(step, carry):
-        for s in range(2):
-            keys = kvall[step, s].reshape(2 * half, 2 * HS)
-            kvt[step, s] = keys.astype(F32).T.astype(BF16)
-            dkv[step, s] = jnp.zeros((2 * half, 2 * HS), F32)
-        return carry
-
-    lax.fori_loop(0, ctxs, turn, 0)
-    gather_q.share()
-    gather_o.begin()
-    if chunks > 1:
-        gather_c[1].start()
-    gather_q.end()
 
     def query_tile(n, carry):
         cols = many(n * 256, 256, 256)
@@ -711,13 +681,8 @@
     def store_query(j, value):
         sel_a[j] = value * scale
 
-    def serve(*calls):
-        for k, call in calls:
-            if k < chunks:
-                getattr(gather_c[k], call)()
-
     gather_o.pass_on()
-    serve((0, "begin"), (2, "start"))
+    serve((3, "start"))
     choose(q_t, store_query)
     for s in range(2):
         for pair in range(TOP // 2):
@@ -731,8 +696,8 @@
         pads[sh, HS:, 0:lanes] = jnp.zeros((HS, lanes), BF16)
         pads[sh, 0:HS, lanes:] = jnp.zeros((HS, lanes), BF16)
 
-    gather_o.share()
-    serve((0, "pass_on"), (1, "begin"), (3, "start"))
+    serve((1, "begin"))
+    serve((0, "pass_on"))
 
     offset = lax.broadcasted_iota(jnp.int32, (1, lanes), 1) % half
     key_row = lax.broadcasted_iota(jnp.int32, (2 * half, lanes), 0)
@@ -770,7 +735,8 @@
         tops = lax.fori_loop(0, count, score_step, (start, start))
         tops = [jnp.max(top, axis=0, keepdims=True) for top in tops]
         if h == 1:
-            serve((0, "share"), (1, "pass_on"), (2, "begin"))
+            gather_o.share()
+            serve((2, "begin"))
         for s in range(2):
             hrow[2 * s + h] = jnp.zeros((HS, lanes), F32)
 
@@ -792,9 +758,9 @@
             hrow[2 * s + h] = hrow[2 * s + h] * inverse
 
     attend(1)
-    serve((1, "share"), (2, "pass_on"), (3, "begin"))
+    serve((0, "share"), (1, "pass_on"), (3, "begin"))
     attend(0)
-    serve((2, "share"), (3, "pass_on"))
+    serve((2, "pass_on"), (1, "share"))
 
     for s in range(2):
         for pair in range(TOP // 2):
@@ -812,8 +778,6 @@
 
     spread_back(sel_a, store_mixed)
     gather_o.end()
-    serve((3, "share"))
-
     experts = E // shards
     acc_a[...] = x_ref[...].astype(F32)
 
@@ -871,9 +835,9 @@
                     :, a * UNIT + q * ws : a * UNIT + (q + 1) * ws
                 ]
         grad_outer = dot(act.astype(F32).T.astype(BF16), gfin).astype(BF16)
-        gc[k, planes, 0:UNIT] = grad_outer.reshape(per_panel, UNIT, width)
+        gc[k][planes, 0:UNIT] = grad_outer.reshape(per_panel, UNIT, width)
         grad_inner = dot(n2_t[...], grad_hidden).astype(BF16)
-        gc[k, :, rows_in] = grad_inner.reshape(shards, ws, PANEL)
+        gc[k][:, rows_in] = grad_inner.reshape(shards, ws, PANEL)
         acc_b[...] += dot_t(grad_hidden, w_in)
 
     outs = [local(out_ref, out_hbm, 15), local(gin_ref, gin_hbm, 16)]
@@ -884,22 +848,20 @@
         return Reduce(net, *refs, out, far_first, store)
 
     reduce_c = [
-        reduction(
-            [ref.at[k] for ref in (gc, gc_core, gc_a, gc_b, gc_group, gc_far)],
-            chunk_out.at[k],
-            chunk_hbm.at[k],
-            20 + k,
-            chunk_far[k],
-        )
+        reduction(sums_c[k], chunk_out.at[k], chunk_hbm.at[k], 20 + k, chunk_far[k])
         for k in range(chunks)
     ]
     for k in range(chunks):
+        if k == 0:
+            serve((3, "pass_on"), (2, "share"))
+        if k == 1:
+            serve((3, "share"))
         gather_c[k].end()
         for p in range(panels):
             feed(k, p)
         reduce_c[k].advance()
-        if k:
-            reduce_c[k - 1].advance()
+        if k > 1:
+            reduce_c[k - 2].advance()
     out_ref[...] = (valid * (resid[...] + acc_a[...] + bias_out)).astype(BF16)
     outs[0].start()
     gfin = cot_ref[...].astype(F32) * valid
@@ -913,7 +875,8 @@
     grad_residual = gfin + grad_hat * small[0, :, 1:2]
     resid[...] = grad_residual
     n2[...] = grad_residual.astype(BF16)
-    reduce_c[chunks - 1].advance()
+    if chunks > 1:
+        reduce_c[chunks - 2].advance()
 
     def branch(s, carry):
         part = mixed_t[pl.ds(s * experts, experts)].reshape(wos, tokens)
@@ -923,10 +886,9 @@
         return carry
 
     lax.fori_loop(0, shards, branch, 0)
-    reduce_o = reduction(
-        (go, go_core, go_a, go_b, go_group, go_far), wo_out, wo_hbm_out, 17, False
-    )
+    reduce_o = reduction(sums_o, wo_out, wo_hbm_out, 17, False)
     reduce_o.advance()
+    reduce_c[chunks - 1].advance()
 
     def store_head_grad(j, value):
         sel_a[j] = value * small[1, pl.ds(j, 1), 0:tokens]
@@ -935,18 +897,17 @@
         )
 
     choose(q_t, store_head_grad)
-    reduce_c[0].advance()
     gates = small[1, 0:TOP, 0:tokens]
     grad_gates = small[1, 2 * TOP : 3 * TOP, 0:tokens]
     grad_picked = gates * (grad_gates - jnp.sum(gates * grad_gates, axis=0, keepdims=True))
     picks = small[1, TOP : 2 * TOP, 0:tokens]
-    g_t[wide + 2 * HS :, :] = jnp.zeros((128, tokens), BF16)
+    g_t[wide : wide + 128, :] = jnp.zeros((128, tokens), BF16)
     grad_logits = [
         jnp.sum(jnp.where(picks == float(e), grad_picked, 0.0), axis=0, keepdims=True)
         for e in range(E)
     ]
     grad_logits += [jnp.zeros((1, tokens), F32)] * (32 - E)
-    g_t[wide + 2 * HS : wide + 2 * HS + 32, :] = jnp.concatenate(grad_logits, axis=0).astype(BF16)
+    g_t[wide : wide + 32, :] = jnp.concatenate(grad_logits, axis=0).astype(BF16)
     for s in range(2):
         for pair in range(TOP // 2):
             halves = swap(
@@ -962,7 +923,6 @@
                     grad.astype(F32) * hrow[sh, :, at : at + 128], axis=0, keepdims=True
                 )
     reduce_o.advance()
-    reduce_c[1 % chunks].advance()
 
     def attend_back(h):
         count, base = place(h)
@@ -983,22 +943,19 @@
         lax.fori_loop(0, count, grad_step, 0)
 
     attend_back(1)
-    for k in range(chunks):
-        reduce_c[k].advance()
     attend_back(0)
 
     for one in kv_sent:
-        one.wait_send()
+        net.left(one)
 
     def lower(step, carry):
         kvall[step] = dkv[step].astype(BF16).reshape(2, 2, half, 2 * HS)
         return carry
 
     lax.fori_loop(0, ctxs, lower, 0)
-    dkv_cross = [
-        net.send(part, from_sib.at[k], z, net.sibling())
-        for k, part in enumerate(core_blocks(kvall, 1 - net.core))
-    ]
+    dkv_cross, dkv_near = net.arrival(), net.arrival()
+    for k, part in enumerate(core_blocks(kvall, 1 - net.core)):
+        net.send(part, from_sib.at[k], dkv_cross, z, net.sibling())
     for s in range(2):
         for pair in range(TOP // 2):
             both = swap(
@@ -1013,8 +970,7 @@
 
     spread_back(q_t, store_grad_query)
 
-    for k in range(2):
-        net.wait(dkv_cross[k], from_sib.at[k])
+    net.wait(dkv_cross, from_sib)
 
     def add_sibling(step, carry):
         for k, sub in enumerate((net.core, 1 - net.core)):
@@ -1027,15 +983,10 @@
         return carry
 
     lax.fori_loop(0, near_steps, add_sibling, 0)
-    dkv_slots = []
     for step in range(1, near_steps):
         peer = (c + 2 * step) % ctxs
-        dkv_slots.append(
-            [
-                net.send(at_block(kvall, block), from_kv.at[step - 1, h], z, peer)
-                for h, block in enumerate((peer, blocks - 1 - peer))
-            ]
-        )
+        for h, block in enumerate((peer, blocks - 1 - peer)):
+            net.send(at_block(kvall, block), from_kv.at[step - 1, h], dkv_near, z, peer)
 
     def query_grad(n, carry):
         at = many(n * 256, 256, 256)
@@ -1044,9 +995,8 @@
         return carry
 
     lax.fori_loop(0, wide // 256, query_grad, 0)
-    reduce_q = reduction((gq, gq_core, gq_a, gq_b, gq_group, gq_far), q_out, q_hbm, 18, False)
+    reduce_q = reduction(sums_q, q_out, q_hbm, 18, False)
     reduce_q.advance()
-    reduce_o.advance()
 
     heads_t[...] = jnp.zeros(heads_t.shape, F32)
 
@@ -1057,10 +1007,10 @@
         return carry
 
     lax.fori_loop(0, wide // 256, norm_grad, 0)
+    part = dot(wq[:, :, wide:].reshape(width, 128), g_t[wide : wide + 128, :])
+    heads_t[...] += part.reshape(heads_t.shape)
     reduce_q.advance()
-    for step in range(1, near_steps):
-        for h in range(2):
-            net.wait(dkv_slots[step - 1][h], from_kv.at[step - 1, h])
+    net.wait(dkv_near, from_kv)
     for h in range(2):
         block = my_block(h)
         for s in range(2):
@@ -1069,18 +1019,17 @@
                 value = value + from_kv[step - 1, h, s].astype(F32)
             first = s * seg + h * half
             acc_a[first : first + half, 0:128] = value
-    g_t[wide : wide + 2 * HS, :] = acc_a[:, 0:128].T.astype(BF16)
-    tail = g_t[wide:, :]
-    part = heads_t[...].reshape(width, tokens) + dot(wk[...].reshape(width, 256), tail)
+    grad_kv = acc_a[:, 0:128].T.astype(BF16)
+    part = heads_t[...].reshape(width, tokens) + dot(wk[...].reshape(width, 2 * HS), grad_kv)
     grad_normed = part.T
     hat = first_hat()
     vec_g[vec_line : vec_line + 1, :] = jnp.sum(grad_normed * hat, axis=0, keepdims=True)
     vec_g[vec_line + 1 : vec_line + 2, :] = jnp.sum(grad_normed, axis=0, keepdims=True)
-    tail_grad = dot_t(normed_t[...], tail)
-    gk[:, :, 0 : 2 * HS] = tail_grad[:, 0 : 2 * HS].astype(BF16).reshape(shards, ws, 2 * HS)
-    tail_grad = tail_grad[:, 2 * HS :] + vec_g[...].T
-    gk[:, :, 2 * HS :] = tail_grad.astype(BF16).reshape(shards, ws, 128)
-    reduce_k = reduction((gk, gk_core, gk_a, gk_b, gk_group, gk_far), kv_out, kv_hbm, 19, False)
+    value = dot_t(normed_t[...], grad_kv)
+    gk[:, :, 0 : 2 * HS] = value.astype(BF16).reshape(shards, ws, 2 * HS)
+    value = dot_t(normed_t[...], g_t[wide:, :]) + vec_g[...].T
+    gk[:, :, 2 * HS :] = value.astype(BF16).reshape(shards, ws, 128)
+    reduce_k = reduction(sums_k, kv_out, kv_hbm, 19, False)
     reduce_k.advance()
     grad_hat = grad_normed * gain1
     grad_hat = grad_hat - jnp.mean(grad_hat, axis=1, keepdims=True)
@@ -1190,7 +1139,7 @@
     panels = shards * UNIT // PANEL
     chunk_rows = UNIT + panels * ws
     wide = E * HS
-    chunk_far = [False] * chunks
+    chunk_far = [k < chunks // 2 for k in range(chunks)]
     shapes_mid = (
         jax.ShapeDtypeStruct((count, width), BF16),
         jax.ShapeDtypeStruct((count, width), F32),
@@ -1202,14 +1151,7 @@
 
     smem = pl.BlockSpec(memory_space=pltpu.SMEM)
     anywhere = pl.BlockSpec(memory_space=pl.ANY)
-    spread = {1: 0, 2: 1, 4: 3}[pairs]
-    copies = (
-        (3 + chunks) * (shards - 1) * (spread + 2)
-        + (3 + chunks) * (reduce_copies(shards, group, rounds) + 1)
-        + 4 * (ctxs // 2 - 1)
-        + 4
-        + (shards - 1)
-    )
+    arrivals = 2 + (2 + chunks) * 5 + 1 + 4 + (3 + chunks) * (9 + rounds)
     scratch = [
         pltpu.VMEM((count, width), BF16),
         pltpu.VMEM((count, width), BF16),
@@ -1221,11 +1163,12 @@
         pltpu.VMEM((E, ws), F32),
         pltpu.VMEM(inner_weight.shape, F32),
         pltpu.VMEM((max(wos + fs, 3 * count), width), F32),
-        pltpu.VMEM((shards, ws, 256), BF16),
-        pltpu.VMEM((shards, ws, wide), BF16),
+        pltpu.VMEM((shards, ws, 2 * HS), BF16),
+        pltpu.VMEM((shards, ws, wide + 128), BF16),
         pltpu.VMEM((shards, wos, width), BF16),
         pltpu.VMEM((chunks, shards, chunk_rows, PANEL), BF16),
-        pltpu.VMEM((shards, 8, fs), F32),
+        pltpu.VMEM((16, UNIT), F32),
+        pltpu.VMEM((shards, 16, UNIT), BF16),
         pltpu.VMEM((count, width), BF16),
         pltpu.VMEM((width, count), BF16),
         pltpu.VMEM((E, HS, count), F32),
@@ -1247,16 +1190,19 @@
         pltpu.VMEM((width, count), BF16),
         pltpu.VMEM((count, width), BF16),
         pltpu.VMEM((8, PANEL), F32),
-        pltpu.VMEM((wide + 256, count), BF16),
-        *reduce_scratch(shards, group, rounds, chunk_rows, PANEL, False, (chunks,)),
-        *reduce_scratch(shards, group, rounds, wos, width, False),
-        *reduce_scratch(shards, group, rounds, ws, wide, False),
-        *reduce_scratch(shards, group, rounds, ws, 256, False),
+        pltpu.VMEM((wide + 128, count), BF16),
+        [
+            reduce_scratch(shards, group, rounds, chunk_rows, PANEL, chunk_far[k])
+            for k in range(chunks)
+        ],
+        reduce_scratch(shards, group, rounds, wos, width, False),
+        reduce_scratch(shards, group, rounds, ws, wide, False),
+        reduce_scratch(shards, group, rounds, ws, 256, False),
         *[pltpu.VMEM(one.shape, one.dtype) for one in shapes_mid],
         pltpu.VMEM((128, width), F32),
         pltpu.SemaphoreType.DMA((20 + chunks,)),
-        pltpu.SemaphoreType.DMA((copies,)),
-        pltpu.SemaphoreType.DMA((copies,)),
+        pltpu.SemaphoreType.DMA((RING,)),
+        pltpu.SemaphoreType.DMA((arrivals,)),
     ]
     results = pl.pallas_call(
         functools.partial(layer_kernel, shards, ctxs, group, chunk_far),

time: 120 us -> 109 us (0.908)
  Pallas kernels: 119 us -> 108 us
    pallas_call x1, Pallas kernels: 115 us -> 104 us  [on_device(): pl.pallas_call(functools.partial(layer_kernel, shards, ctxs, group, chunk...]
where the time goes in v3:
time: 109 us
  Pallas kernels  108 us (99%)
    pallas_call x1, Pallas kernels, on_device(): pl.pallas_call(functools.partial(layer_kernel, shards, ctxs, group, chunk...  104 us
    pallas_call x1, Pallas kernels, on_device(): pl.pallas_call(functools.partial(unpack_kernel, shards), out_shape=shapes...  3.63 us

profile of v3, /device:TPU:0, one launch (start us, length us, event | category | flops | bytes accessed | tf_op | source)
XLA Modules:
  0.0 108.6 jit_solution(2188920853235482242)
XLA Ops:
  0.7 104.1 %layer.1 = (bf16[256,512]{1,0:T(8,128)(2,1)}, f32[256,512]{1,0:T(8,128)}, bf16[4,256,512]{2,1,0:T(8,128)(2,1)}, bf16[384,512]{1,0:T(8,128)(2,1)}, bf16[128,1536]{1,0:T(8,128)(2,1)}, /*index=5*/bf16[128,256]{1,0:T(8,128)(2,1)}) custom-call(s32[2]{0:T(128)} %len_ref.1, bf16[256,512]{1,0:T(8,128)(2,1)} %bitcast.19, bf16[256,512]{1,0:T(8,128)(2,1)} %bitcast.20, ...), custom_call_target="tpu_custom_call" | custom-call | tf_op jit(solution)/shard_map/layer/pallas_call | solution.py:1207
  104.8 3.6 %unpack.1 = (bf16[256,512]{1,0:T(8,128)(2,1)}, f32[256,512]{1,0:T(8,128)}, f32[1,128]{1,0:T(1,128)}, f32[1,128]{1,0:T(1,128)}, f32[128,128]{1,0:T(8,128)}, /*ind...) custom-call(bf16[256,512]{1,0:T(8,128)(2,1)} %get-tuple-element.34.r, ...), custom_call_target="tpu_custom_call" | custom-call | tf_op jit(solution)/shard_map/unpack/pallas_call | solution.py:1252

commit v4 on v3

--- a/solution.py
+++ b/solution.py
@@ -419,7 +419,7 @@
     wi_st,
     stage,
     wk,
-    wq,
+    wqs,
     wo,
     wc,
     vec_st,
@@ -435,6 +435,7 @@
     pads,
     hrow,
     linv,
+    sbuf,
     ebuf,
     dkv,
     from_sib,
@@ -476,6 +477,7 @@
     per_panel = PANEL // UNIT
     lanes = TOP * half
     wide = E * HS
+    split = wide // 2
     gc, go, gq, gk = [one[0] for one in sums_c], sums_o[0], sums_q[0], sums_k[0]
     vec_line = E
     bias_line = vec_line + 5
@@ -522,7 +524,8 @@
     own_vec = vecs.at[z]
     own_vec[...] = vec_st[...].astype(BF16)
     net.greeted()
-    gather_k, gather_q, gather_o = Gather(net, wk, True), Gather(net, wq), Gather(net, wo)
+    gather_k, gather_o = Gather(net, wk, True), Gather(net, wo)
+    gather_q = [Gather(net, one) for one in wqs]
     gather_c = [Gather(net, wc.at[k]) for k in range(chunks)]
     gather_k.start()
     vec_slot = net.arrival()
@@ -530,10 +533,12 @@
         net.send(own_vec, own_vec, vec_slot, net.far(k), net.i)
     loads[id(wq_st)].wait()
     loads[id(wr_st)].wait()
-    wq[z, :, 0:wide] = wq_st[...].astype(BF16)
+    for k in range(2):
+        wqs[k][z, :, 0:split] = wq_st[:, k * split : (k + 1) * split].astype(BF16)
     padded = jnp.concatenate([wr_st[...], jnp.zeros((128 - E, ws), F32)], axis=0)
-    wq[z, :, wide:] = padded.T.astype(BF16)
-    gather_q.start()
+    wqs[1][z, :, split:] = padded.T.astype(BF16)
+    for one in gather_q:
+        one.start()
 
     loads[id(x_ref)].wait()
     x = x_ref[...].astype(F32)
@@ -574,6 +579,7 @@
     norm_value = first_hat() * gain1 + bias1
     normed[...] = norm_value.astype(BF16)
     normed_t[...] = norm_value.T.astype(BF16)
+    gather_q[0].begin()
     gather_k.end()
 
     kv_own = dot(normed[...], wk[...].reshape(width, 2 * HS)).astype(BF16)
@@ -598,13 +604,15 @@
         for block in (c, blocks - 1 - c):
             ref = at_block(kvall, block)
             kv_sent.append(net.send(ref, ref, kv_slot, z, (c + 2 * step) % ctxs))
+    gather_q[1].begin()
     gather_o.start()
-    gather_q.begin()
-    gather_c[0].start()
+    gather_q[0].pass_on()
     net.wait(kv_slot, kvall.at[0 : near_steps - 1])
     for part in core_blocks(kvall, net.core):
         kv_sent.append(net.send(part, part, kv_cross, z, net.sibling()))
-    gather_q.pass_on()
+    gather_q[1].pass_on()
+    gather_c[0].start()
+    gather_q[0].share()
     net.wait(kv_cross, kvall.at[0:near_steps])
 
     def turn(step, carry):
@@ -614,7 +622,7 @@
             dkv[step, s] = jnp.zeros((2 * half, 2 * HS), F32)
         return carry
 
-    lax.fori_loop(0, ctxs, turn, 0)
+    lax.fori_loop(0, ctxs, turn, 0, unroll=4)
 
     def serve(*calls):
         for k, call in calls:
@@ -623,11 +631,26 @@
 
     gather_o.begin()
     serve((1, "start"))
-    gather_q.share()
+    gather_q[0].end()
+
+    def project_queries(part):
+        def query_tile(n, carry):
+            cols = many(n * 256, 256, 256)
+            value = dot(normed[...], wqs[part][:, :, cols].reshape(width, 256))
+            value = value.astype(BF16).astype(F32).T
+            for k in range(4):
+                q_t[part * (E // 2) + n * 4 + k] = value[k * HS : (k + 1) * HS]
+            return carry
+
+        lax.fori_loop(0, split // 256, query_tile, 0, unroll=True)
+
+    project_queries(0)
+    gather_q[1].share()
     serve((0, "begin"), (2, "start"))
-    gather_q.end()
-
-    logits_t = dot(normed[...], wq[:, :, wide:].reshape(width, 128)).T
+    gather_q[1].end()
+    project_queries(1)
+
+    logits_t = dot(normed[...], wqs[1][:, :, split:].reshape(width, 128)).T
     loads[id(picks_ref)].wait()
     picks = jnp.concatenate([picks_ref[0], picks_ref[1]], axis=1).astype(F32)
     picked = jnp.zeros((TOP, tokens), F32)
@@ -638,16 +661,6 @@
     small[1, 0:TOP, 0:tokens] = gexp / jnp.sum(gexp, axis=0, keepdims=True)
     small[1, TOP : 2 * TOP, 0:tokens] = picks
 
-    def query_tile(n, carry):
-        cols = many(n * 256, 256, 256)
-        value = dot(normed[...], wq[:, :, cols].reshape(width, 256))
-        value = value.astype(BF16).astype(F32).T
-        for k in range(4):
-            q_t[n * 4 + k] = value[k * HS : (k + 1) * HS]
-        return carry
-
-    lax.fori_loop(0, wide // 256, query_tile, 0)
-
     def choose(src, store):
         def one(j, carry):
             pick = small[1, pl.ds(TOP + j, 1), 0:tokens]
@@ -657,7 +670,7 @@
             store(j, value)
             return carry
 
-        lax.fori_loop(0, TOP, one, 0)
+        lax.fori_loop(0, TOP, one, 0, unroll=2)
 
     def spread_back(src, store):
         def one(e, carry):
@@ -668,7 +681,7 @@
             store(e, value)
             return carry
 
-        lax.fori_loop(0, E, one, 0)
+        lax.fori_loop(0, E, one, 0, unroll=4)
 
     low_lane = lax.broadcasted_iota(jnp.int32, (HS, 2 * half), 1) < half
 
@@ -700,12 +713,14 @@
     serve((0, "pass_on"))
 
     offset = lax.broadcasted_iota(jnp.int32, (1, lanes), 1) % half
-    key_row = lax.broadcasted_iota(jnp.int32, (2 * half, lanes), 0)
+    key_row = lax.broadcasted_iota(jnp.int32, (4 * half, lanes), 0)
+    keep_scores = sbuf.shape[1] > 1
 
     def place(h):
+        last = (blocks - c + 3) // 4
         if h == 1:
-            return (blocks - c + 1) // 2, 0
-        return (c + 2) // 2, (blocks - c + 1) // 2
+            return last, 0
+        return (c + 4) // 4, last
 
     def fold(value, op):
         parts = [value[8 * k : 8 * k + 8] for k in range(value.shape[0] // 8)]
@@ -714,7 +729,10 @@
         return parts[0]
 
     def keys_of(step, s):
-        return kvall[step, s].reshape(2 * half, 2 * HS)
+        return kvall[pl.ds(2 * step, 2), s].reshape(4 * half, 2 * HS)
+
+    def turned(step, s, rows):
+        return jnp.concatenate([kvt[2 * step + k, s, rows] for k in range(2)], axis=1)
 
     def attend(h):
         count, base = place(h)
@@ -724,12 +742,16 @@
 
         def masked(step, s):
             scores = dot(keys_of(step, s), pads[2 * s + h, :, 0:lanes])
-            return jnp.where(key_row <= limits[s] - step * 2 * half, scores, NEG_LARGE)
+            return jnp.where(key_row <= limits[s] - step * 4 * half, scores, NEG_LARGE)
 
         def score_step(step, tops):
-            return tuple(
-                jnp.maximum(tops[s], fold(masked(step, s), jnp.maximum)) for s in range(2)
-            )
+            result = []
+            for s in range(2):
+                scores = masked(step, s)
+                if keep_scores:
+                    sbuf[s, step] = scores
+                result.append(jnp.maximum(tops[s], fold(scores, jnp.maximum)))
+            return tuple(result)
 
         start = jnp.full((8, lanes), NEG_LARGE, F32)
         tops = lax.fori_loop(0, count, score_step, (start, start))
@@ -743,11 +765,16 @@
         def value_step(step, totals):
             result = []
             for s in range(2):
-                expd = jnp.exp(masked(step, s) - tops[s])
-                low = expd.astype(BF16)
-                ebuf[s, base + step] = low
-                hrow[2 * s + h] += dot(kvt[step, s, HS:], low)
-                result.append(totals[s] + fold(expd, jnp.add))
+                total = totals[s]
+                scores = None if keep_scores else masked(step, s)
+                for k in range(2):
+                    rows = slice(2 * half * k, 2 * half * (k + 1))
+                    part = sbuf[s, step, rows] if keep_scores else scores[rows]
+                    expd = jnp.exp(part - tops[s])
+                    ebuf[s, base + step, rows] = expd.astype(BF16)
+                    total = total + fold(expd, jnp.add)
+                hrow[2 * s + h] += dot(turned(step, s, slice(HS, 2 * HS)), ebuf[s, base + step])
+                result.append(total)
             return tuple(result)
 
         start = jnp.zeros((8, lanes), F32)
@@ -786,7 +813,7 @@
         acc_a[...] += dot(part.astype(F32).T.astype(BF16), wo[s])
         return carry
 
-    lax.fori_loop(0, shards, project, 0)
+    lax.fori_loop(0, shards, project, 0, unroll=True)
     residual = acc_a[...]
     resid[...] = residual
     cen = residual - jnp.mean(residual, axis=1, keepdims=True)
@@ -885,7 +912,7 @@
         q_t[pl.ds(s * experts, experts)] = grad.reshape(experts, HS, tokens)
         return carry
 
-    lax.fori_loop(0, shards, branch, 0)
+    lax.fori_loop(0, shards, branch, 0, unroll=2)
     reduce_o = reduction(sums_o, wo_out, wo_hbm_out, 17, False)
     reduce_o.advance()
     reduce_c[chunks - 1].advance()
@@ -933,16 +960,24 @@
         def grad_step(step, carry):
             for s in range(2):
                 sh = 2 * s + h
-                expd = ebuf[s, base + step]
-                grad_prob = dot(keys_of(step, s), pads[sh, :, lanes:])
-                grad_score = (expd.astype(F32) * (grad_prob - deltas[s])).astype(BF16)
-                dkv[step, s] += dot_t(jnp.concatenate([grad_score, expd], axis=1), pads[sh])
-                hrow[sh] += dot(kvt[step, s, 0:HS], grad_score)
+                parts = []
+                for k in range(2):
+                    expd = ebuf[s, base + step, 2 * half * k : 2 * half * (k + 1)]
+                    keys = kvall[2 * step + k, s].reshape(2 * half, 2 * HS)
+                    grad_prob = dot(keys, pads[sh, :, lanes:])
+                    parts.append((expd.astype(F32) * (grad_prob - deltas[s])).astype(BF16))
+                grad_score = jnp.concatenate(parts, axis=0)
+                grad = dot_t(grad_score, pads[sh, :, 0:lanes])
+                grad = grad + dot_t(ebuf[s, base + step], pads[sh, :, lanes:])
+                dkv[pl.ds(2 * step, 2), s] += grad.reshape(2, 2 * half, 2 * HS)
+                hrow[sh] += dot(turned(step, s, slice(0, HS)), grad_score)
             return carry
 
         lax.fori_loop(0, count, grad_step, 0)
 
     attend_back(1)
+    for k in range(chunks // 2, chunks):
+        reduce_c[k].advance()
     attend_back(0)
 
     for one in kv_sent:
@@ -970,6 +1005,16 @@
 
     spread_back(q_t, store_grad_query)
 
+    def query_grad(n, carry):
+        at = many(n * 256, 256, 256)
+        grad = dot_t(normed_t[...], g_t[at, :]).astype(BF16)
+        gq[:, :, at] = grad.reshape(shards, ws, 256)
+        return carry
+
+    lax.fori_loop(0, wide // 256, query_grad, 0, unroll=3)
+    reduce_q = reduction(sums_q, q_out, q_hbm, 18, False)
+    reduce_q.advance()
+
     net.wait(dkv_cross, from_sib)
 
     def add_sibling(step, carry):
@@ -988,28 +1033,13 @@
         for h, block in enumerate((peer, blocks - 1 - peer)):
             net.send(at_block(kvall, block), from_kv.at[step - 1, h], dkv_near, z, peer)
 
-    def query_grad(n, carry):
-        at = many(n * 256, 256, 256)
-        grad = dot_t(normed_t[...], g_t[at, :]).astype(BF16)
-        gq[:, :, at] = grad.reshape(shards, ws, 256)
-        return carry
-
-    lax.fori_loop(0, wide // 256, query_grad, 0)
-    reduce_q = reduction(sums_q, q_out, q_hbm, 18, False)
+    reduce_o.advance()
+    part = dot(wqs[0][...].reshape(width, split), g_t[0:split, :])
+    part = part + dot(wqs[1][...].reshape(width, split + 128), g_t[split:, :])
+    heads_t[...] = part.reshape(heads_t.shape)
     reduce_q.advance()
-
-    heads_t[...] = jnp.zeros(heads_t.shape, F32)
-
-    def norm_grad(n, carry):
-        at = many(n * 256, 256, 256)
-        part = dot(wq[:, :, at].reshape(width, 256), g_t[at, :])
-        heads_t[...] += part.reshape(heads_t.shape)
-        return carry
-
-    lax.fori_loop(0, wide // 256, norm_grad, 0)
-    part = dot(wq[:, :, wide:].reshape(width, 128), g_t[wide : wide + 128, :])
-    heads_t[...] += part.reshape(heads_t.shape)
-    reduce_q.advance()
+    for k in range(chunks // 2, chunks):
+        reduce_c[k].advance()
     net.wait(dkv_near, from_kv)
     for h in range(2):
         block = my_block(h)
@@ -1037,7 +1067,7 @@
     gin_ref[...] = resid[...] + grad_hat * small[0, :, 0:1]
     outs[1].start()
 
-    everything = [*reduce_c, reduce_o, reduce_q, reduce_k]
+    everything = [reduce_k, reduce_q, reduce_o, *reduce_c[chunks // 2 :], *reduce_c[: chunks // 2]]
     while any(one.stage < len(one.steps) for one in everything):
         for one in everything:
             one.advance()
@@ -1140,6 +1170,7 @@
     chunk_rows = UNIT + panels * ws
     wide = E * HS
     chunk_far = [k < chunks // 2 for k in range(chunks)]
+    keep_scores = ctxs * seg * slots * lanes * 4 <= 8 * 1024 * 1024
     shapes_mid = (
         jax.ShapeDtypeStruct((count, width), BF16),
         jax.ShapeDtypeStruct((count, width), F32),
@@ -1151,7 +1182,7 @@
 
     smem = pl.BlockSpec(memory_space=pltpu.SMEM)
     anywhere = pl.BlockSpec(memory_space=pl.ANY)
-    arrivals = 2 + (2 + chunks) * 5 + 1 + 4 + (3 + chunks) * (9 + rounds)
+    arrivals = 2 + (3 + chunks) * 5 + 1 + 4 + (3 + chunks) * (9 + rounds)
     scratch = [
         pltpu.VMEM((count, width), BF16),
         pltpu.VMEM((count, width), BF16),
@@ -1164,7 +1195,7 @@
         pltpu.VMEM(inner_weight.shape, F32),
         pltpu.VMEM((max(wos + fs, 3 * count), width), F32),
         pltpu.VMEM((shards, ws, 2 * HS), BF16),
-        pltpu.VMEM((shards, ws, wide + 128), BF16),
+        [pltpu.VMEM((shards, ws, wide // 2 + 128 * k), BF16) for k in range(2)],
         pltpu.VMEM((shards, wos, width), BF16),
         pltpu.VMEM((chunks, shards, chunk_rows, PANEL), BF16),
         pltpu.VMEM((16, UNIT), F32),
@@ -1180,7 +1211,8 @@
         pltpu.VMEM((4, 2 * HS, 2 * lanes), BF16),
         pltpu.VMEM((4, HS, lanes), F32),
         pltpu.VMEM((4, 8, lanes), F32),
-        pltpu.VMEM((slots, ctxs + 1, 2 * half, lanes), BF16),
+        pltpu.VMEM((slots, ctxs // 2, 4 * half, lanes) if keep_scores else (1, 1, 8, 128), F32),
+        pltpu.VMEM((slots, ctxs // 2 + 1, 4 * half, lanes), BF16),
         pltpu.VMEM((ctxs, slots, 2 * half, 2 * HS), F32),
         pltpu.VMEM((2, ctxs // 2, slots, half, 2 * HS), BF16),
         pltpu.VMEM((ctxs // 2 - 1, 2, slots, half, 2 * HS), BF16),

time: 109 us -> 101 us (0.927)
  Pallas kernels: 108 us -> 99.5 us
    pallas_call x1, Pallas kernels: 104 us -> 95.8 us  [on_device(): pl.pallas_call(functools.partial(layer_kernel, shards, ctxs, group, chunk...]
where the time goes in v4:
time: 101 us; the launch traced here: 100 us
  Pallas kernels  99.5 us (99%)
    pallas_call x1, Pallas kernels, on_device(): pl.pallas_call(functools.partial(layer_kernel, shards, ctxs, group, chunk...  95.8 us
    pallas_call x1, Pallas kernels, on_device(): pl.pallas_call(functools.partial(unpack_kernel, shards), out_shape=shapes...  3.63 us

profile of v4, /device:TPU:0, one launch (start us, length us, event | category | flops | bytes accessed | tf_op | source)
XLA Modules:
  0.0 100.3 jit_solution(18198572038944503325)
XLA Ops:
  0.7 95.8 %layer.1 = (bf16[256,512]{1,0:T(8,128)(2,1)}, f32[256,512]{1,0:T(8,128)}, bf16[4,256,512]{2,1,0:T(8,128)(2,1)}, bf16[384,512]{1,0:T(8,128)(2,1)}, bf16[128,1536]{1,0:T(8,128)(2,1)}, /*index=5*/bf16[128,256]{1,0:T(8,128)(2,1)}) custom-call(s32[2]{0:T(128)} %len_ref.1, bf16[256,512]{1,0:T(8,128)(2,1)} %bitcast.19, bf16[256,512]{1,0:T(8,128)(2,1)} %bitcast.20, ...), custom_call_target="tpu_custom_call" | custom-call | tf_op jit(solution)/shard_map/layer/pallas_call | solution.py:1239
  96.5 3.6 %unpack.1 = (bf16[256,512]{1,0:T(8,128)(2,1)}, f32[256,512]{1,0:T(8,128)}, f32[1,128]{1,0:T(1,128)}, f32[1,128]{1,0:T(1,128)}, f32[128,128]{1,0:T(8,128)}, /*ind...) custom-call(bf16[256,512]{1,0:T(8,128)(2,1)} %get-tuple-element.34.r, ...), custom_call_target="tpu_custom_call" | custom-call | tf_op jit(solution)/shard_map/unpack/pallas_call | solution.py:1284

commit v5 on v4

--- a/solution.py
+++ b/solution.py
@@ -20,6 +20,7 @@
 GELU_A = 0.044715
 MESH = pl.DeviceIdType.MESH
 RING = 40
+START, CORE, NEAR_A, NEAR_B, FAR_0, FAR_1, FAR_2, PASS, SHARE, END = range(10)
 
 
 def dot(left, right):
@@ -126,8 +127,9 @@
 
 
 class Spread:
-    def __init__(self, net, refs, all_of):
-        self.net, self.refs, self.all_of = net, refs, all_of
+    def __init__(self, net, refs, all_of, at_once=False, straight=False):
+        self.net, self.refs, self.all_of, self.at_once = net, refs, all_of, at_once
+        self.straight = straight
         self.piece = refs[0].shape[0] // net.group
         self.half = refs[0].shape[0] // 2
 
@@ -146,14 +148,23 @@
     def begin(self):
         net = self.net
         own = self.part(net.chip)
+        if self.at_once:
+            self.to_all = net.arrival()
+            (ref,) = self.refs
+            for step in range(1, net.group):
+                peer = net.grp * net.group + (net.i + step) % net.group
+                net.send(ref.at[own], ref.at[own], self.to_all, net.z, peer)
+            return
         if net.dims == 2:
             self.to_a = self.give(own, net.peer(net.chip_a))
         if net.dims:
             self.to_b = self.give(own, net.peer(net.chip_b))
+        if net.dims == 2 and self.straight:
+            self.on = self.give(own, net.peer(net.chip_ab))
 
     def pass_on(self):
         net = self.net
-        if net.dims == 2:
+        if net.dims == 2 and not self.straight:
             got = self.part(net.chip_a)
             net.wait(self.to_a, self.all_of(got))
             self.on = self.give(got, net.peer(net.chip_b))
@@ -163,6 +174,8 @@
         if net.dims:
             net.wait(self.to_b, self.all_of(self.part(net.chip_b)))
         if net.dims == 2:
+            if self.straight:
+                net.wait(self.to_a, self.all_of(self.part(net.chip_a)))
             net.wait(self.on, self.all_of(self.part(net.chip_ab)))
         self.cross()
 
@@ -170,7 +183,11 @@
         self.to_core = self.give(self.block(self.net.core), self.net.sibling())
 
     def end(self):
-        self.net.wait(self.to_core, self.all_of(self.block(1 - self.net.core)))
+        if self.at_once:
+            count = self.piece * (self.net.group - 1)
+            self.net.wait(self.to_all, self.all_of(pl.ds(0, count)))
+        else:
+            self.net.wait(self.to_core, self.all_of(self.block(1 - self.net.core)))
 
 
 class Gather:
@@ -178,7 +195,6 @@
         self.net, self.buf, self.by_core = net, buf, by_core
         planes = [buf.at[net.src(k)] for k in range(1, net.shards)]
         self.spread = Spread(net, planes, lambda rows: buf.at[0 : net.shards - 1, rows])
-        self.pass_on, self.share, self.end = self.spread.pass_on, self.spread.share, self.spread.end
         self.rows = self.spread.block(net.core) if by_core else self.spread.part(net.chip)
 
     def start(self):
@@ -195,32 +211,60 @@
         else:
             self.spread.begin()
 
+    def pass_on(self):
+        if not self.by_core:
+            self.spread.pass_on()
+
+    def share(self):
+        if not self.by_core:
+            self.spread.share()
+
+    def end(self):
+        self.spread.end()
+
+
+class Absent:
+    def start(self):
+        pass
+
+    begin = pass_on = share = end = start
+
+    def to(self, name):
+        pass
+
 
 class Reduce:
-    def __init__(
-        self, net, grad, from_core, from_a, from_b, from_group, from_far, out, far_first, store
-    ):
-        self.net, self.grad, self.out, self.far_first = net, grad, out, far_first
-        self.store = store
-        self.from_core, self.from_a, self.from_b = from_core, from_a, from_b
-        self.from_group, self.from_far = from_group, from_far
-        self.piece = grad.shape[1] // net.group
-        self.half = grad.shape[1] // 2
-        self.spread = Spread(net, [out], lambda rows: out.at[rows])
-        near = [self.take_a, self.take_b] if net.dims == 2 else [self.take_b]
-        steps = [self.take_far] + near if far_first else near + [self.take_far]
-        self.steps = [self.start, self.take_core] + steps
-        self.steps[-1] = functools.partial(self.last, self.steps[-1])
+    def __init__(self, net, buffers, out, far_first, halving, at_once, straight, store):
+        self.net, self.out, self.store = net, out, store
+        self.grad, self.from_core, self.from_a, self.from_b = buffers[0:4]
+        self.from_group, self.from_far = buffers[4:6]
+        self.far_first, self.halving = far_first, halving
+        self.piece = self.grad.shape[1] // net.group
+        self.half = self.grad.shape[1] // 2
+        self.spread = Spread(net, [out], lambda rows: out.at[rows], at_once, straight)
+        near = [(NEAR_B, self.take_b)]
         if net.dims == 2:
-            self.steps.append(self.spread.pass_on)
-        self.steps += [self.spread.share, self.finish]
-        self.stage = 0
-
-    def advance(self, times=1):
-        for _ in range(times):
-            if self.stage < len(self.steps):
-                self.steps[self.stage]()
-                self.stage += 1
+            near = [(NEAR_A, self.take_a)] + near
+        if halving:
+            rounds = net.shards.bit_length() - 1
+            far = [(FAR_0 + k, functools.partial(self.take_half, k)) for k in range(rounds)]
+        else:
+            far = [(FAR_0, self.take_far)]
+        steps = far + near if far_first else near + far
+        name, step = steps[-1]
+        steps[-1] = (name, functools.partial(self.last, step))
+        after = [(PASS, self.spread.pass_on), (SHARE, self.spread.share)]
+        after = [] if at_once else after if net.dims == 2 else after[1:]
+        self.steps = [(START, self.start), (CORE, self.take_core), *steps, *after]
+        self.steps.append((END, self.finish))
+        far, near = [FAR_0, FAR_1, FAR_2], [NEAR_A, NEAR_B]
+        order = far + near if far_first else near + far
+        order = [START, CORE, *order, PASS, SHARE, END]
+        self.rank = {name: k for k, name in enumerate(order)}
+
+    def to(self, name):
+        while self.steps and self.rank[self.steps[0][0]] <= self.rank[name]:
+            self.steps.pop(0)[1]()
 
     def last(self, step):
         step()
@@ -340,6 +384,9 @@
     def send_far(self, own):
         net = self.net
         self.own = own
+        if self.halving:
+            self.send_half(0)
+            return
         self.to_far = net.arrival()
         for k in range(1, net.shards):
             net.send(
@@ -350,16 +397,58 @@
                 net.i,
             )
 
+    def half_at(self, turn):
+        step = 1 << turn
+        count = self.net.shards // (2 * step)
+        return step, count, self.net.shards - 2 * count
+
+    def send_half(self, turn):
+        net = self.net
+        step, count, at = self.half_at(turn)
+        partner = net.z + step * (1 - 2 * ((net.z // step) % 2))
+        self.to_far = net.arrival()
+        for k in range(count):
+            plane = partner % (2 * step) + 2 * step * k
+            net.send(
+                self.grad.at[pl.ds(plane, 1), self.own],
+                self.from_far.at[pl.ds(at + k, 1)],
+                self.to_far,
+                partner,
+                net.i,
+            )
+
+    def take_half(self, turn):
+        net = self.net
+        step, count, at = self.half_at(turn)
+        parts = self.from_far.at[pl.ds(at, count)]
+        net.wait(self.to_far, parts)
+        planes = [(net.z % (2 * step) + 2 * step * k, k) for k in range(count)]
+        first, size = (
+            (net.core * self.half, self.half)
+            if self.far_first
+            else (self.first(net.chip), self.piece)
+        )
+        self.add(first, size, planes, [parts])
+        if count > 1:
+            self.send_half(turn + 1)
+        else:
+            self.far_done()
+
     def take_far(self):
         net = self.net
         net.wait(self.to_far, self.from_far)
         parts = [self.from_far.at[pl.ds(k, 1)] for k in range(net.shards - 1)]
         if self.far_first:
             self.add(net.core * self.half, self.half, self.planes(True), parts)
+        else:
+            self.add(self.first(net.chip), self.piece, self.planes(True), parts)
+        self.far_done()
+
+    def far_done(self):
+        if self.far_first:
             self.send_near(True)
         else:
-            self.add(self.first(net.chip), self.piece, self.planes(True), parts)
-            self.out[self.own, :] = self.grad[net.z, self.own]
+            self.out[self.own, :] = self.grad[self.net.z, self.own]
 
 
 def reduce_scratch(shards, group, rounds, rows, wide, far_first):
@@ -478,7 +567,8 @@
     lanes = TOP * half
     wide = E * HS
     split = wide // 2
-    gc, go, gq, gk = [one[0] for one in sums_c], sums_o[0], sums_q[0], sums_k[0]
+    sum_c, sum_q = [one[0] for one in sums_c], [one[0] for one in sums_q]
+    sum_o, sum_k = sums_o[0], sums_k[0]
     vec_line = E
     bias_line = vec_line + 5
     per_unit = UNIT // ws
@@ -526,7 +616,7 @@
     net.greeted()
     gather_k, gather_o = Gather(net, wk, True), Gather(net, wo)
     gather_q = [Gather(net, one) for one in wqs]
-    gather_c = [Gather(net, wc.at[k]) for k in range(chunks)]
+    gather_c = [Gather(net, wc.at[k], k == chunks - 1) for k in range(chunks)]
     gather_k.start()
     vec_slot = net.arrival()
     for k in range(1, shards):
@@ -580,10 +670,6 @@
     normed[...] = norm_value.astype(BF16)
     normed_t[...] = norm_value.T.astype(BF16)
     gather_q[0].begin()
-    gather_k.end()
-
-    kv_own = dot(normed[...], wk[...].reshape(width, 2 * HS)).astype(BF16)
-
     def at_block(ref, block):
         return ref.at[block // 2, :, block % 2]
 
@@ -593,45 +679,39 @@
     def core_blocks(ref, core):
         return ref.at[0:near_steps, :, core], ref.at[near_steps:ctxs, :, 1 - core]
 
-    for h in range(2):
-        block = my_block(h)
-        for s in range(2):
-            first = s * seg + h * half
-            kvall[block // 2, s, block % 2] = kv_own[first : first + half]
-    kv_slot, kv_cross = net.arrival(), net.arrival()
+    kv_slot, kv_cross, dkv_cross, dkv_near = (net.arrival() for _ in range(4))
     kv_sent = []
-    for step in range(1, near_steps):
-        for block in (c, blocks - 1 - c):
-            ref = at_block(kvall, block)
-            kv_sent.append(net.send(ref, ref, kv_slot, z, (c + 2 * step) % ctxs))
-    gather_q[1].begin()
-    gather_o.start()
-    gather_q[0].pass_on()
-    net.wait(kv_slot, kvall.at[0 : near_steps - 1])
-    for part in core_blocks(kvall, net.core):
-        kv_sent.append(net.send(part, part, kv_cross, z, net.sibling()))
-    gather_q[1].pass_on()
-    gather_c[0].start()
-    gather_q[0].share()
-    net.wait(kv_cross, kvall.at[0:near_steps])
-
-    def turn(step, carry):
-        for s in range(2):
-            keys = kvall[step, s].reshape(2 * half, 2 * HS)
-            kvt[step, s] = keys.astype(F32).T.astype(BF16)
-            dkv[step, s] = jnp.zeros((2 * half, 2 * HS), F32)
-        return carry
-
-    lax.fori_loop(0, ctxs, turn, 0, unroll=4)
-
-    def serve(*calls):
-        for k, call in calls:
-            if k < chunks:
-                getattr(gather_c[k], call)()
-
-    gather_o.begin()
-    serve((1, "start"))
-    gather_q[0].end()
+
+    def do_kvproj():
+        kv_own = dot(normed[...], wk[...].reshape(width, 2 * HS)).astype(BF16)
+
+        for h in range(2):
+            block = my_block(h)
+            for s in range(2):
+                first = s * seg + h * half
+                kvall[block // 2, s, block % 2] = kv_own[first : first + half]
+        for step in range(1, near_steps):
+            for block in (c, blocks - 1 - c):
+                ref = at_block(kvall, block)
+                kv_sent.append(net.send(ref, ref, kv_slot, z, (c + 2 * step) % ctxs))
+
+    def do_kvcross():
+        net.wait(kv_slot, kvall.at[0 : near_steps - 1])
+        for part in core_blocks(kvall, net.core):
+            kv_sent.append(net.send(part, part, kv_cross, z, net.sibling()))
+
+    def do_kvwait():
+        net.wait(kv_cross, kvall.at[0:near_steps])
+
+    def do_turn():
+        def turn(step, carry):
+            for s in range(2):
+                keys = kvall[step, s].reshape(2 * half, 2 * HS)
+                kvt[step, s] = keys.astype(F32).T.astype(BF16)
+                dkv[step, s] = jnp.zeros((2 * half, 2 * HS), F32)
+            return carry
+
+        lax.fori_loop(0, ctxs, turn, 0, unroll=4)
 
     def project_queries(part):
         def query_tile(n, carry):
@@ -644,22 +724,17 @@
 
         lax.fori_loop(0, split // 256, query_tile, 0, unroll=True)
 
-    project_queries(0)
-    gather_q[1].share()
-    serve((0, "begin"), (2, "start"))
-    gather_q[1].end()
-    project_queries(1)
-
-    logits_t = dot(normed[...], wqs[1][:, :, split:].reshape(width, 128)).T
-    loads[id(picks_ref)].wait()
-    picks = jnp.concatenate([picks_ref[0], picks_ref[1]], axis=1).astype(F32)
-    picked = jnp.zeros((TOP, tokens), F32)
-    for e in range(E):
-        picked = jnp.where(picks == float(e), logits_t[e : e + 1, :], picked)
-    top = jnp.max(picked, axis=0, keepdims=True)
-    gexp = jnp.exp(picked - top)
-    small[1, 0:TOP, 0:tokens] = gexp / jnp.sum(gexp, axis=0, keepdims=True)
-    small[1, TOP : 2 * TOP, 0:tokens] = picks
+    def do_gates():
+        logits_t = dot(normed[...], wqs[1][:, :, split:].reshape(width, 128)).T
+        loads[id(picks_ref)].wait()
+        picks = jnp.concatenate([picks_ref[0], picks_ref[1]], axis=1).astype(F32)
+        picked = jnp.zeros((TOP, tokens), F32)
+        for e in range(E):
+            picked = jnp.where(picks == float(e), logits_t[e : e + 1, :], picked)
+        top = jnp.max(picked, axis=0, keepdims=True)
+        gexp = jnp.exp(picked - top)
+        small[1, 0:TOP, 0:tokens] = gexp / jnp.sum(gexp, axis=0, keepdims=True)
+        small[1, TOP : 2 * TOP, 0:tokens] = picks
 
     def choose(src, store):
         def one(j, carry):
@@ -694,23 +769,19 @@
     def store_query(j, value):
         sel_a[j] = value * scale
 
-    gather_o.pass_on()
-    serve((3, "start"))
-    choose(q_t, store_query)
-    for s in range(2):
-        for pair in range(TOP // 2):
-            halves = swap(
-                sel_a[2 * pair, :, s * seg : (s + 1) * seg],
-                sel_a[2 * pair + 1, :, s * seg : (s + 1) * seg],
-            )
-            for h in range(2):
-                pads[2 * s + h, 0:HS, pair * 128 : (pair + 1) * 128] = halves[h].astype(BF16)
-    for sh in range(4):
-        pads[sh, HS:, 0:lanes] = jnp.zeros((HS, lanes), BF16)
-        pads[sh, 0:HS, lanes:] = jnp.zeros((HS, lanes), BF16)
-
-    serve((1, "begin"))
-    serve((0, "pass_on"))
+    def do_choose():
+        choose(q_t, store_query)
+        for s in range(2):
+            for pair in range(TOP // 2):
+                halves = swap(
+                    sel_a[2 * pair, :, s * seg : (s + 1) * seg],
+                    sel_a[2 * pair + 1, :, s * seg : (s + 1) * seg],
+                )
+                for h in range(2):
+                    pads[2 * s + h, 0:HS, pair * 128 : (pair + 1) * 128] = halves[h].astype(BF16)
+        for sh in range(4):
+            pads[sh, HS:, 0:lanes] = jnp.zeros((HS, lanes), BF16)
+            pads[sh, 0:HS, lanes:] = jnp.zeros((HS, lanes), BF16)
 
     offset = lax.broadcasted_iota(jnp.int32, (1, lanes), 1) % half
     key_row = lax.broadcasted_iota(jnp.int32, (4 * half, lanes), 0)
@@ -734,31 +805,29 @@
     def turned(step, s, rows):
         return jnp.concatenate([kvt[2 * step + k, s, rows] for k in range(2)], axis=1)
 
-    def attend(h):
-        count, base = place(h)
-        limits = [
-            jnp.minimum(my_block(h) * half + offset, len_ref[s] - 1) for s in range(2)
-        ]
-
-        def masked(step, s):
-            scores = dot(keys_of(step, s), pads[2 * s + h, :, 0:lanes])
-            return jnp.where(key_row <= limits[s] - step * 4 * half, scores, NEG_LARGE)
-
+    tops_of = {}
+
+    def masked(step, s, h):
+        limit = jnp.minimum(my_block(h) * half + offset, len_ref[s] - 1)
+        scores = dot(keys_of(step, s), pads[2 * s + h, :, 0:lanes])
+        return jnp.where(key_row <= limit - step * 4 * half, scores, NEG_LARGE)
+
+    def find_tops(h):
         def score_step(step, tops):
             result = []
             for s in range(2):
-                scores = masked(step, s)
+                scores = masked(step, s, h)
                 if keep_scores:
                     sbuf[s, step] = scores
                 result.append(jnp.maximum(tops[s], fold(scores, jnp.maximum)))
             return tuple(result)
 
         start = jnp.full((8, lanes), NEG_LARGE, F32)
-        tops = lax.fori_loop(0, count, score_step, (start, start))
-        tops = [jnp.max(top, axis=0, keepdims=True) for top in tops]
-        if h == 1:
-            gather_o.share()
-            serve((2, "begin"))
+        tops = lax.fori_loop(0, place(h)[0], score_step, (start, start))
+        tops_of[h] = [jnp.max(top, axis=0, keepdims=True) for top in tops]
+
+    def weigh(h):
+        count, base = place(h)
         for s in range(2):
             hrow[2 * s + h] = jnp.zeros((HS, lanes), F32)
 
@@ -766,11 +835,11 @@
             result = []
             for s in range(2):
                 total = totals[s]
-                scores = None if keep_scores else masked(step, s)
+                scores = None if keep_scores else masked(step, s, h)
                 for k in range(2):
                     rows = slice(2 * half * k, 2 * half * (k + 1))
                     part = sbuf[s, step, rows] if keep_scores else scores[rows]
-                    expd = jnp.exp(part - tops[s])
+                    expd = jnp.exp(part - tops_of[h][s])
                     ebuf[s, base + step, rows] = expd.astype(BF16)
                     total = total + fold(expd, jnp.add)
                 hrow[2 * s + h] += dot(turned(step, s, slice(HS, 2 * HS)), ebuf[s, base + step])
@@ -784,58 +853,56 @@
             linv[2 * s + h] = jnp.broadcast_to(inverse, (8, lanes))
             hrow[2 * s + h] = hrow[2 * s + h] * inverse
 
-    attend(1)
-    serve((0, "share"), (1, "pass_on"), (3, "begin"))
-    attend(0)
-    serve((2, "pass_on"), (1, "share"))
-
-    for s in range(2):
-        for pair in range(TOP // 2):
-            both = swap(
-                hrow[2 * s, :, pair * 128 : (pair + 1) * 128],
-                hrow[2 * s + 1, :, pair * 128 : (pair + 1) * 128],
-            )
-            for k in range(2):
-                heads_t[2 * pair + k, :, s * seg : (s + 1) * seg] = both[k]
-    for j in range(TOP):
-        sel_a[j] = heads_t[j] * small[1, j : j + 1, 0:tokens]
-
-    def store_mixed(e, value):
-        mixed_t[e] = value.astype(BF16)
-
-    spread_back(sel_a, store_mixed)
-    gather_o.end()
+    def do_mix():
+        for s in range(2):
+            for pair in range(TOP // 2):
+                both = swap(
+                    hrow[2 * s, :, pair * 128 : (pair + 1) * 128],
+                    hrow[2 * s + 1, :, pair * 128 : (pair + 1) * 128],
+                )
+                for k in range(2):
+                    heads_t[2 * pair + k, :, s * seg : (s + 1) * seg] = both[k]
+        for j in range(TOP):
+            sel_a[j] = heads_t[j] * small[1, j : j + 1, 0:tokens]
+
+        def store_mixed(e, value):
+            mixed_t[e] = value.astype(BF16)
+
+        spread_back(sel_a, store_mixed)
+
     experts = E // shards
-    acc_a[...] = x_ref[...].astype(F32)
-
-    def project(s, carry):
-        part = mixed_t[pl.ds(s * experts, experts)].reshape(wos, tokens)
-        acc_a[...] += dot(part.astype(F32).T.astype(BF16), wo[s])
-        return carry
-
-    lax.fori_loop(0, shards, project, 0, unroll=True)
-    residual = acc_a[...]
-    resid[...] = residual
-    cen = residual - jnp.mean(residual, axis=1, keepdims=True)
-    rstd2 = lax.rsqrt(jnp.mean(cen * cen, axis=1, keepdims=True) + NORM_EPS)
-    small[0, :, 1:2] = rstd2
-    cen = cen * rstd2
-    xhat2[...] = cen
-    cen = cen * gain2 + bias2
-    n2[...] = cen.astype(BF16)
-    n2_t[...] = cen.T.astype(BF16)
-
     row = lax.broadcasted_iota(jnp.int32, (tokens, 1), 0)
     inner_row = row % seg
     pos = jnp.where(
         inner_row < half, c * half + inner_row, blocks * half - (c + 2) * half + inner_row
     )
     valid = (pos < jnp.where(row < seg, len_ref[0], len_ref[1])).astype(F32)
-    loads[id(cot_ref)].wait()
-    gfin_low[...] = (cot_ref[...].astype(F32) * valid).astype(BF16)
-    acc_a[...] = jnp.zeros((tokens, width), F32)
-    acc_b[...] = jnp.zeros((tokens, width), F32)
-    vec_g[...] = jnp.zeros(vec_g.shape, F32)
+
+    def do_project():
+        acc_a[...] = x_ref[...].astype(F32)
+
+        def project(s, carry):
+            part = mixed_t[pl.ds(s * experts, experts)].reshape(wos, tokens)
+            acc_a[...] += dot(part.astype(F32).T.astype(BF16), wo[s])
+            return carry
+
+        lax.fori_loop(0, shards, project, 0, unroll=True)
+        residual = acc_a[...]
+        resid[...] = residual
+        cen = residual - jnp.mean(residual, axis=1, keepdims=True)
+        rstd2 = lax.rsqrt(jnp.mean(cen * cen, axis=1, keepdims=True) + NORM_EPS)
+        small[0, :, 1:2] = rstd2
+        cen = cen * rstd2
+        xhat2[...] = cen
+        cen = cen * gain2 + bias2
+        n2[...] = cen.astype(BF16)
+        n2_t[...] = cen.T.astype(BF16)
+
+        loads[id(cot_ref)].wait()
+        gfin_low[...] = (cot_ref[...].astype(F32) * valid).astype(BF16)
+        acc_a[...] = jnp.zeros((tokens, width), F32)
+        acc_b[...] = jnp.zeros((tokens, width), F32)
+        vec_g[...] = jnp.zeros(vec_g.shape, F32)
 
     def feed(k, p):
         rows_in = slice(UNIT + p * ws, UNIT + (p + 1) * ws)
@@ -862,94 +929,95 @@
                     :, a * UNIT + q * ws : a * UNIT + (q + 1) * ws
                 ]
         grad_outer = dot(act.astype(F32).T.astype(BF16), gfin).astype(BF16)
-        gc[k][planes, 0:UNIT] = grad_outer.reshape(per_panel, UNIT, width)
+        sum_c[k][planes, 0:UNIT] = grad_outer.reshape(per_panel, UNIT, width)
         grad_inner = dot(n2_t[...], grad_hidden).astype(BF16)
-        gc[k][:, rows_in] = grad_inner.reshape(shards, ws, PANEL)
+        sum_c[k][:, rows_in] = grad_inner.reshape(shards, ws, PANEL)
         acc_b[...] += dot_t(grad_hidden, w_in)
 
     outs = [local(out_ref, out_hbm, 15), local(gin_ref, gin_hbm, 16)]
 
-    def reduction(refs, out, hbm, at, far_first):
+    def reduction(
+        refs, out, hbm, at, far_first=False, halving=False, at_once=False, straight=False
+    ):
         store = local(out, hbm, at)
         outs.append(store)
-        return Reduce(net, *refs, out, far_first, store)
+        return Reduce(net, refs, out, far_first, halving, at_once, straight, store)
 
     reduce_c = [
-        reduction(sums_c[k], chunk_out.at[k], chunk_hbm.at[k], 20 + k, chunk_far[k])
+        reduction(sums_c[k], chunk_out.at[k], chunk_hbm.at[k], 20 + k, chunk_far[k], True)
         for k in range(chunks)
     ]
-    for k in range(chunks):
-        if k == 0:
-            serve((3, "pass_on"), (2, "share"))
-        if k == 1:
-            serve((3, "share"))
-        gather_c[k].end()
-        for p in range(panels):
-            feed(k, p)
-        reduce_c[k].advance()
-        if k > 1:
-            reduce_c[k - 2].advance()
-    out_ref[...] = (valid * (resid[...] + acc_a[...] + bias_out)).astype(BF16)
-    outs[0].start()
-    gfin = cot_ref[...].astype(F32) * valid
-    vec_g[vec_line + 4 : vec_line + 5, :] = jnp.sum(gfin, axis=0, keepdims=True)
-    grad_n2 = acc_b[...]
-    vec_g[vec_line + 3 : vec_line + 4, :] = jnp.sum(grad_n2, axis=0, keepdims=True)
-    vec_g[vec_line + 2 : vec_line + 3, :] = jnp.sum(grad_n2 * xhat2[...], axis=0, keepdims=True)
-    grad_hat = grad_n2 * gain2
-    grad_hat = grad_hat - jnp.mean(grad_hat, axis=1, keepdims=True)
-    grad_hat = grad_hat - xhat2[...] * jnp.mean(grad_hat * xhat2[...], axis=1, keepdims=True)
-    grad_residual = gfin + grad_hat * small[0, :, 1:2]
-    resid[...] = grad_residual
-    n2[...] = grad_residual.astype(BF16)
-    if chunks > 1:
-        reduce_c[chunks - 2].advance()
-
-    def branch(s, carry):
-        part = mixed_t[pl.ds(s * experts, experts)].reshape(wos, tokens)
-        go[s] = dot(part, n2[...]).astype(BF16)
-        grad = dot_t(wo[s], n2[...])
-        q_t[pl.ds(s * experts, experts)] = grad.reshape(experts, HS, tokens)
-        return carry
-
-    lax.fori_loop(0, shards, branch, 0, unroll=2)
-    reduce_o = reduction(sums_o, wo_out, wo_hbm_out, 17, False)
-    reduce_o.advance()
-    reduce_c[chunks - 1].advance()
-
-    def store_head_grad(j, value):
-        sel_a[j] = value * small[1, pl.ds(j, 1), 0:tokens]
-        small[1, pl.ds(2 * TOP + j, 1), 0:tokens] = jnp.sum(
-            value * heads_t[j], axis=0, keepdims=True
+    reduce_o = reduction(sums_o, wo_out, wo_hbm_out, 17, straight=False)
+    reduce_q = [
+        reduction(
+            sums_q[k],
+            q_out[k],
+            q_hbm.at[:, k * split : (k + 1) * split],
+            20 + chunks + k,
+            straight=True,
         )
-
-    choose(q_t, store_head_grad)
-    gates = small[1, 0:TOP, 0:tokens]
-    grad_gates = small[1, 2 * TOP : 3 * TOP, 0:tokens]
-    grad_picked = gates * (grad_gates - jnp.sum(gates * grad_gates, axis=0, keepdims=True))
-    picks = small[1, TOP : 2 * TOP, 0:tokens]
-    g_t[wide : wide + 128, :] = jnp.zeros((128, tokens), BF16)
-    grad_logits = [
-        jnp.sum(jnp.where(picks == float(e), grad_picked, 0.0), axis=0, keepdims=True)
-        for e in range(E)
+        for k in range(2)
     ]
-    grad_logits += [jnp.zeros((1, tokens), F32)] * (32 - E)
-    g_t[wide : wide + 32, :] = jnp.concatenate(grad_logits, axis=0).astype(BF16)
-    for s in range(2):
-        for pair in range(TOP // 2):
-            halves = swap(
-                sel_a[2 * pair, :, s * seg : (s + 1) * seg],
-                sel_a[2 * pair + 1, :, s * seg : (s + 1) * seg],
+    reduce_k = reduction(sums_k, kv_out, kv_hbm, 19, at_once=True)
+
+    def do_norm2():
+        out_ref[...] = (valid * (resid[...] + acc_a[...] + bias_out)).astype(BF16)
+        outs[0].start()
+        gfin = cot_ref[...].astype(F32) * valid
+        vec_g[vec_line + 4 : vec_line + 5, :] = jnp.sum(gfin, axis=0, keepdims=True)
+        grad_n2 = acc_b[...]
+        vec_g[vec_line + 3 : vec_line + 4, :] = jnp.sum(grad_n2, axis=0, keepdims=True)
+        vec_g[vec_line + 2 : vec_line + 3, :] = jnp.sum(grad_n2 * xhat2[...], axis=0, keepdims=True)
+        grad_hat = grad_n2 * gain2
+        grad_hat = grad_hat - jnp.mean(grad_hat, axis=1, keepdims=True)
+        grad_hat = grad_hat - xhat2[...] * jnp.mean(grad_hat * xhat2[...], axis=1, keepdims=True)
+        grad_residual = gfin + grad_hat * small[0, :, 1:2]
+        resid[...] = grad_residual
+        n2[...] = grad_residual.astype(BF16)
+
+    def do_branch():
+        def branch(s, carry):
+            part = mixed_t[pl.ds(s * experts, experts)].reshape(wos, tokens)
+            sum_o[s] = dot(part, n2[...]).astype(BF16)
+            grad = dot_t(wo[s], n2[...])
+            q_t[pl.ds(s * experts, experts)] = grad.reshape(experts, HS, tokens)
+            return carry
+
+        lax.fori_loop(0, shards, branch, 0, unroll=2)
+
+    def do_heads():
+        def store_head_grad(j, value):
+            sel_a[j] = value * small[1, pl.ds(j, 1), 0:tokens]
+            small[1, pl.ds(2 * TOP + j, 1), 0:tokens] = jnp.sum(
+                value * heads_t[j], axis=0, keepdims=True
             )
-            at = pair * 128
-            for h in range(2):
-                sh = 2 * s + h
-                grad = (halves[h] * linv[sh, 0:1, at : at + 128]).astype(BF16)
-                pads[sh, HS:, lanes + at : lanes + at + 128] = grad
-                linv[sh, 1:2, at : at + 128] = jnp.sum(
-                    grad.astype(F32) * hrow[sh, :, at : at + 128], axis=0, keepdims=True
+
+        choose(q_t, store_head_grad)
+        gates = small[1, 0:TOP, 0:tokens]
+        grad_gates = small[1, 2 * TOP : 3 * TOP, 0:tokens]
+        grad_picked = gates * (grad_gates - jnp.sum(gates * grad_gates, axis=0, keepdims=True))
+        picks = small[1, TOP : 2 * TOP, 0:tokens]
+        g_t[wide : wide + 128, :] = jnp.zeros((128, tokens), BF16)
+        grad_logits = [
+            jnp.sum(jnp.where(picks == float(e), grad_picked, 0.0), axis=0, keepdims=True)
+            for e in range(E)
+        ]
+        grad_logits += [jnp.zeros((1, tokens), F32)] * (32 - E)
+        g_t[wide : wide + 32, :] = jnp.concatenate(grad_logits, axis=0).astype(BF16)
+        for s in range(2):
+            for pair in range(TOP // 2):
+                halves = swap(
+                    sel_a[2 * pair, :, s * seg : (s + 1) * seg],
+                    sel_a[2 * pair + 1, :, s * seg : (s + 1) * seg],
                 )
-    reduce_o.advance()
+                at = pair * 128
+                for h in range(2):
+                    sh = 2 * s + h
+                    grad = (halves[h] * linv[sh, 0:1, at : at + 128]).astype(BF16)
+                    pads[sh, HS:, lanes + at : lanes + at + 128] = grad
+                    linv[sh, 1:2, at : at + 128] = jnp.sum(
+                        grad.astype(F32) * hrow[sh, :, at : at + 128], axis=0, keepdims=True
+                    )
 
     def attend_back(h):
         count, base = place(h)
@@ -975,102 +1043,242 @@
 
         lax.fori_loop(0, count, grad_step, 0)
 
+    def do_dsend():
+        for one in kv_sent:
+            net.left(one)
+
+        def lower(step, carry):
+            kvall[step] = dkv[step].astype(BF16).reshape(2, 2, half, 2 * HS)
+            return carry
+
+        lax.fori_loop(0, ctxs, lower, 0)
+        for k, part in enumerate(core_blocks(kvall, 1 - net.core)):
+            net.send(part, from_sib.at[k], dkv_cross, z, net.sibling())
+
+    def do_gradq():
+        for s in range(2):
+            for pair in range(TOP // 2):
+                both = swap(
+                    hrow[2 * s, :, pair * 128 : (pair + 1) * 128],
+                    hrow[2 * s + 1, :, pair * 128 : (pair + 1) * 128],
+                )
+                for k in range(2):
+                    q_t[2 * pair + k, :, s * seg : (s + 1) * seg] = both[k] * scale
+
+        def store_grad_query(e, value):
+            g_t[many(e * HS, HS, HS), :] = value.astype(BF16)
+
+        spread_back(q_t, store_grad_query)
+
+    def query_grads(part):
+        def query_grad(n, carry):
+            rows = many(part * split + n * 256, 256, 256)
+            grad = dot_t(normed_t[...], g_t[rows, :]).astype(BF16)
+            sum_q[part][:, :, many(n * 256, 256, 256)] = grad.reshape(shards, ws, 256)
+            return carry
+
+        lax.fori_loop(0, split // 256, query_grad, 0, unroll=True)
+
+    def do_dnear():
+        net.wait(dkv_cross, from_sib)
+
+        def add_sibling(step, carry):
+            for k, sub in enumerate((net.core, 1 - net.core)):
+                at = step + k * near_steps
+                rows = many(sub * half, half, half)
+                for s in range(2):
+                    value = dkv[at, s, rows] + from_sib[k, step, s].astype(F32)
+                    dkv[at, s, rows] = value
+                    kvall[at, s, sub] = value.astype(BF16)
+            return carry
+
+        lax.fori_loop(0, near_steps, add_sibling, 0)
+        for step in range(1, near_steps):
+            peer = (c + 2 * step) % ctxs
+            for h, block in enumerate((peer, blocks - 1 - peer)):
+                net.send(at_block(kvall, block), from_kv.at[step - 1, h], dkv_near, z, peer)
+
+    def do_ngrad():
+        part = dot(wqs[0][...].reshape(width, split), g_t[0:split, :])
+        part = part + dot(wqs[1][...].reshape(width, split + 128), g_t[split:, :])
+        heads_t[...] = part.reshape(heads_t.shape)
+
+    def do_dwait():
+        net.wait(dkv_near, from_kv)
+
+    def do_kvgrad():
+        for h in range(2):
+            block = my_block(h)
+            for s in range(2):
+                value = dkv[block // 2, s, many((block % 2) * half, half, half)]
+                for step in range(1, near_steps):
+                    value = value + from_kv[step - 1, h, s].astype(F32)
+                first = s * seg + h * half
+                acc_a[first : first + half, 0:128] = value
+        grad_kv = acc_a[:, 0:128].T.astype(BF16)
+        part = heads_t[...].reshape(width, tokens) + dot(wk[...].reshape(width, 2 * HS), grad_kv)
+        grad_normed = part.T
+        hat = first_hat()
+        vec_g[vec_line : vec_line + 1, :] = jnp.sum(grad_normed * hat, axis=0, keepdims=True)
+        vec_g[vec_line + 1 : vec_line + 2, :] = jnp.sum(grad_normed, axis=0, keepdims=True)
+        value = dot_t(normed_t[...], grad_kv)
+        sum_k[:, :, 0 : 2 * HS] = value.astype(BF16).reshape(shards, ws, 2 * HS)
+        value = dot_t(normed_t[...], g_t[wide:, :]) + vec_g[...].T
+        sum_k[:, :, 2 * HS :] = value.astype(BF16).reshape(shards, ws, 128)
+        acc_b[...] = grad_normed
+
+    def do_gin():
+        hat = first_hat()
+        grad_normed = acc_b[...]
+        grad_hat = grad_normed * gain1
+        grad_hat = grad_hat - jnp.mean(grad_hat, axis=1, keepdims=True)
+        grad_hat = grad_hat - hat * jnp.mean(grad_hat * hat, axis=1, keepdims=True)
+        gin_ref[...] = resid[...] + grad_hat * small[0, :, 0:1]
+        outs[1].start()
+
+    def feed_all(k):
+        if k < chunks:
+            for p in range(panels):
+                feed(k, p)
+
+    absent = [Absent()] * 4
+    gc0, gc1, gc2, gc3 = (gather_c + absent)[0:4]
+    rc0, rc1, rc2, rc3 = (reduce_c + absent)[0:4]
+    (gq0, gq1), (rq0, rq1) = gather_q, reduce_q
+    go, gk, ro, rk = gather_o, gather_k, reduce_o, reduce_k
+    gk.end()
+    do_kvproj()
+    go.start()
+    gq1.begin()
+    gq0.pass_on()
+    gc0.start()
+    do_kvcross()
+    gq1.pass_on()
+    gc1.start()
+    go.begin()
+    gc2.start()
+    gq0.share()
+    do_kvwait()
+    do_turn()
+    gc0.begin()
+    gq0.end()
+    project_queries(0)
+    gq1.share()
+    gc1.begin()
+    gq1.end()
+    gc3.start()
+    project_queries(1)
+    do_gates()
+    go.pass_on()
+    gc2.begin()
+    do_choose()
+    gc0.pass_on()
+    find_tops(1)
+    go.share()
+    gc1.pass_on()
+    weigh(1)
+    gc0.share()
+    gc2.pass_on()
+    find_tops(0)
+    weigh(0)
+    gc1.share()
+    do_mix()
+    go.end()
+    do_project()
+    gc2.share()
+    gc0.end()
+    feed_all(0)
+    rc0.to(START)
+    gc3.begin()
+    gc3.pass_on()
+    gc3.share()
+    gc1.end()
+    feed_all(1)
+    rc1.to(START)
+    gc2.end()
+    feed_all(2)
+    rc2.to(START)
+    rc0.to(CORE)
+    gc3.end()
+    feed_all(3)
+    rc3.to(START)
+    rc1.to(CORE)
+    do_norm2()
+    rc2.to(CORE)
+    do_branch()
+    ro.to(START)
+    rc3.to(CORE)
+    do_heads()
     attend_back(1)
-    for k in range(chunks // 2, chunks):
-        reduce_c[k].advance()
     attend_back(0)
-
-    for one in kv_sent:
-        net.left(one)
-
-    def lower(step, carry):
-        kvall[step] = dkv[step].astype(BF16).reshape(2, 2, half, 2 * HS)
-        return carry
-
-    lax.fori_loop(0, ctxs, lower, 0)
-    dkv_cross, dkv_near = net.arrival(), net.arrival()
-    for k, part in enumerate(core_blocks(kvall, 1 - net.core)):
-        net.send(part, from_sib.at[k], dkv_cross, z, net.sibling())
-    for s in range(2):
-        for pair in range(TOP // 2):
-            both = swap(
-                hrow[2 * s, :, pair * 128 : (pair + 1) * 128],
-                hrow[2 * s + 1, :, pair * 128 : (pair + 1) * 128],
-            )
-            for k in range(2):
-                q_t[2 * pair + k, :, s * seg : (s + 1) * seg] = both[k] * scale
-
-    def store_grad_query(e, value):
-        g_t[many(e * HS, HS, HS), :] = value.astype(BF16)
-
-    spread_back(q_t, store_grad_query)
-
-    def query_grad(n, carry):
-        at = many(n * 256, 256, 256)
-        grad = dot_t(normed_t[...], g_t[at, :]).astype(BF16)
-        gq[:, :, at] = grad.reshape(shards, ws, 256)
-        return carry
-
-    lax.fori_loop(0, wide // 256, query_grad, 0, unroll=3)
-    reduce_q = reduction(sums_q, q_out, q_hbm, 18, False)
-    reduce_q.advance()
-
-    net.wait(dkv_cross, from_sib)
-
-    def add_sibling(step, carry):
-        for k, sub in enumerate((net.core, 1 - net.core)):
-            at = step + k * near_steps
-            rows = many(sub * half, half, half)
-            for s in range(2):
-                value = dkv[at, s, rows] + from_sib[k, step, s].astype(F32)
-                dkv[at, s, rows] = value
-                kvall[at, s, sub] = value.astype(BF16)
-        return carry
-
-    lax.fori_loop(0, near_steps, add_sibling, 0)
-    for step in range(1, near_steps):
-        peer = (c + 2 * step) % ctxs
-        for h, block in enumerate((peer, blocks - 1 - peer)):
-            net.send(at_block(kvall, block), from_kv.at[step - 1, h], dkv_near, z, peer)
-
-    reduce_o.advance()
-    part = dot(wqs[0][...].reshape(width, split), g_t[0:split, :])
-    part = part + dot(wqs[1][...].reshape(width, split + 128), g_t[split:, :])
-    heads_t[...] = part.reshape(heads_t.shape)
-    reduce_q.advance()
-    for k in range(chunks // 2, chunks):
-        reduce_c[k].advance()
-    net.wait(dkv_near, from_kv)
-    for h in range(2):
-        block = my_block(h)
-        for s in range(2):
-            value = dkv[block // 2, s, many((block % 2) * half, half, half)]
-            for step in range(1, near_steps):
-                value = value + from_kv[step - 1, h, s].astype(F32)
-            first = s * seg + h * half
-            acc_a[first : first + half, 0:128] = value
-    grad_kv = acc_a[:, 0:128].T.astype(BF16)
-    part = heads_t[...].reshape(width, tokens) + dot(wk[...].reshape(width, 2 * HS), grad_kv)
-    grad_normed = part.T
-    hat = first_hat()
-    vec_g[vec_line : vec_line + 1, :] = jnp.sum(grad_normed * hat, axis=0, keepdims=True)
-    vec_g[vec_line + 1 : vec_line + 2, :] = jnp.sum(grad_normed, axis=0, keepdims=True)
-    value = dot_t(normed_t[...], grad_kv)
-    gk[:, :, 0 : 2 * HS] = value.astype(BF16).reshape(shards, ws, 2 * HS)
-    value = dot_t(normed_t[...], g_t[wide:, :]) + vec_g[...].T
-    gk[:, :, 2 * HS :] = value.astype(BF16).reshape(shards, ws, 128)
-    reduce_k = reduction(sums_k, kv_out, kv_hbm, 19, False)
-    reduce_k.advance()
-    grad_hat = grad_normed * gain1
-    grad_hat = grad_hat - jnp.mean(grad_hat, axis=1, keepdims=True)
-    grad_hat = grad_hat - hat * jnp.mean(grad_hat * hat, axis=1, keepdims=True)
-    gin_ref[...] = resid[...] + grad_hat * small[0, :, 0:1]
-    outs[1].start()
-
-    everything = [reduce_k, reduce_q, reduce_o, *reduce_c[chunks // 2 :], *reduce_c[: chunks // 2]]
-    while any(one.stage < len(one.steps) for one in everything):
-        for one in everything:
-            one.advance()
+    ro.to(CORE)
+    do_dsend()
+    do_gradq()
+    query_grads(0)
+    rq0.to(START)
+    query_grads(1)
+    rq1.to(START)
+    rc2.to(NEAR_A)
+    rc3.to(NEAR_A)
+    do_dnear()
+    do_ngrad()
+    rc0.to(FAR_0)
+    rc1.to(FAR_0)
+    ro.to(NEAR_A)
+    rc2.to(NEAR_B)
+    rc3.to(NEAR_B)
+    rq0.to(CORE)
+    rq1.to(CORE)
+    do_dwait()
+    do_kvgrad()
+    rk.to(START)
+    do_gin()
+    rk.to(CORE)
+    rc0.to(FAR_1)
+    rc1.to(FAR_1)
+    ro.to(NEAR_B)
+    rq0.to(NEAR_A)
+    rq1.to(NEAR_A)
+    rc2.to(FAR_0)
+    rc3.to(FAR_0)
+    rc0.to(NEAR_A)
+    rc1.to(NEAR_A)
+    rk.to(NEAR_A)
+    rq0.to(NEAR_B)
+    rq1.to(NEAR_B)
+    ro.to(FAR_0)
+    rc0.to(NEAR_B)
+    rc1.to(NEAR_B)
+    rc2.to(FAR_1)
+    rc3.to(FAR_1)
+    rk.to(NEAR_B)
+    ro.to(PASS)
+    rc0.to(PASS)
+    rc1.to(PASS)
+    rc2.to(PASS)
+    rc3.to(PASS)
+    rq0.to(FAR_0)
+    rq1.to(FAR_0)
+    rk.to(FAR_0)
+    ro.to(SHARE)
+    rc0.to(SHARE)
+    rc1.to(SHARE)
+    rc2.to(SHARE)
+    rc3.to(SHARE)
+    rq0.to(PASS)
+    rq1.to(PASS)
+    rc1.to(END)
+    rc2.to(END)
+    rc0.to(END)
+    rc3.to(END)
+    rq0.to(SHARE)
+    rq1.to(SHARE)
+    rk.to(END)
+    ro.to(END)
+    rq0.to(END)
+    rq1.to(END)
+    for one in (*reduce_c, ro, *reduce_q, rk):
+        one.to(END)
     net.finish()
     for one in outs:
         one.wait()
@@ -1079,23 +1287,33 @@
 def unpack_kernel(shards, *refs):
     ins, outs = refs[0:6], refs[6:20]
     in_st, out_st, sem = refs[20:26], refs[26:40], refs[40]
-    loads = [pltpu.make_async_copy(a, b, sem.at[k]) for k, (a, b) in enumerate(zip(ins, in_st))]
-    stores = [
-        pltpu.make_async_copy(in_st[k] if k < 2 else out_st[k], outs[k], sem.at[6 + k])
+    chunks = ins[2].shape[0]
+    copy = pltpu.make_async_copy
+    loads = [copy(a, b, sem.at[k]) for k, (a, b) in enumerate(zip(ins, in_st)) if k != 2]
+    loads.insert(2, None)
+    stores = {
+        k: copy(in_st[k] if k < 2 else out_st[k], outs[k], sem.at[6 + k])
         for k in range(14)
-    ]
-    for k in (2, 3, 4, 5, 1, 0):
-        loads[k].start()
+        if k != 12
+    }
     chunk_in, wo_in, q_in, kv_in = in_st[2:]
     g1_ref, b1_ref, kv_ref, q_ref, r_ref, wo_ref, g2_ref, b2_ref = out_st[2:10]
     wi_ref, bi_ref, wout_ref, bo_ref = out_st[10:]
     ws, fs = q_ref.shape[0], wout_ref.shape[0]
     per_panel = PANEL // UNIT
-    loads[2].wait()
-    for k in range(chunk_in.shape[0]):
-        wout_ref[k * UNIT : (k + 1) * UNIT, :] = chunk_in[k, 0:UNIT].astype(F32)
-    stores[12].start()
-    for k in range(chunk_in.shape[0]):
+    chunk_loads = [
+        copy(ins[2].at[k], chunk_in.at[k], sem.at[20 + k]) for k in range(chunks)
+    ]
+    for one in chunk_loads:
+        one.start()
+    for k in (3, 4, 5, 1, 0):
+        loads[k].start()
+    for k in range(chunks):
+        chunk_loads[k].wait()
+        rows = slice(k * UNIT, (k + 1) * UNIT)
+        wout_ref[rows, :] = chunk_in[k, 0:UNIT].astype(F32)
+        stores[20 + k] = copy(wout_ref.at[rows], outs[12].at[rows], sem.at[20 + chunks + k])
+        stores[20 + k].start()
         for s in range(shards):
             first = UNIT + (s // per_panel) * ws
             at = (s % per_panel) * UNIT
@@ -1131,7 +1349,7 @@
     stores[1].start()
     loads[0].wait()
     stores[0].start()
-    for one in stores:
+    for one in stores.values():
         one.wait()
 
 
@@ -1169,7 +1387,7 @@
     panels = shards * UNIT // PANEL
     chunk_rows = UNIT + panels * ws
     wide = E * HS
-    chunk_far = [k < chunks // 2 for k in range(chunks)]
+    chunk_far = [k < 2 for k in range(chunks)]
     keep_scores = ctxs * seg * slots * lanes * 4 <= 8 * 1024 * 1024
     shapes_mid = (
         jax.ShapeDtypeStruct((count, width), BF16),
@@ -1182,7 +1400,7 @@
 
     smem = pl.BlockSpec(memory_space=pltpu.SMEM)
     anywhere = pl.BlockSpec(memory_space=pl.ANY)
-    arrivals = 2 + (3 + chunks) * 5 + 1 + 4 + (3 + chunks) * (9 + rounds)
+    arrivals = 2 + (3 + chunks) * 5 + 1 + 4 + (4 + chunks) * (8 + rounds + shards.bit_length() - 1)
     scratch = [
         pltpu.VMEM((count, width), BF16),
         pltpu.VMEM((count, width), BF16),
@@ -1228,11 +1446,13 @@
             for k in range(chunks)
         ],
         reduce_scratch(shards, group, rounds, wos, width, False),
-        reduce_scratch(shards, group, rounds, ws, wide, False),
+        [reduce_scratch(shards, group, rounds, ws, wide // 2, False) for _ in range(2)],
         reduce_scratch(shards, group, rounds, ws, 256, False),
-        *[pltpu.VMEM(one.shape, one.dtype) for one in shapes_mid],
+        *[pltpu.VMEM(one.shape, one.dtype) for one in shapes_mid[0:4]],
+        [pltpu.VMEM((ws, wide // 2), BF16) for _ in range(2)],
+        pltpu.VMEM((ws, 256), BF16),
         pltpu.VMEM((128, width), F32),
-        pltpu.SemaphoreType.DMA((20 + chunks,)),
+        pltpu.SemaphoreType.DMA((22 + chunks,)),
         pltpu.SemaphoreType.DMA((RING,)),
         pltpu.SemaphoreType.DMA((arrivals,)),
     ]
@@ -1287,7 +1507,7 @@
         in_specs=[anywhere] * 6,
         out_specs=tuple([anywhere] * 14),
         scratch_shapes=[pltpu.VMEM(one.shape, one.dtype) for one in (*shapes_mid, *shapes_out)]
-        + [pltpu.SemaphoreType.DMA((20,))],
+        + [pltpu.SemaphoreType.DMA((20 + 2 * chunks,))],
         name="unpack",
     )(*results)
     final = list(final)

time: 101 us -> 91.5 us (0.906)
  Pallas kernels: 99.5 us -> 90.5 us
    pallas_call x1, Pallas kernels: 95.8 us -> 87.1 us  [on_device(): pl.pallas_call(functools.partial(layer_kernel, shards, ctxs, group, chunk...]
where the time goes in v5:
time: 91.5 us; the launch traced here: 91.3 us
  Pallas kernels  90.5 us (99%)
    pallas_call x1, Pallas kernels, on_device(): pl.pallas_call(functools.partial(layer_kernel, shards, ctxs, group, chunk...  87.1 us
    pallas_call x1, Pallas kernels, on_device(): pl.pallas_call(functools.partial(unpack_kernel, shards), out_shape=shapes...  3.38 us

profile of v5, /device:TPU:0, one launch (start us, length us, event | category | flops | bytes accessed | tf_op | source)
XLA Modules:
  0.0 91.3 jit_solution(6762263946049825165)
XLA Ops:
  0.7 87.1 %layer.1 = (bf16[256,512]{1,0:T(8,128)(2,1)}, f32[256,512]{1,0:T(8,128)}, bf16[4,256,512]{2,1,0:T(8,128)(2,1)}, bf16[384,512]{1,0:T(8,128)(2,1)}, bf16[128,1536]{1,0:T(8,128)(2,1)}, /*index=5*/bf16[128,256]{1,0:T(8,128)(2,1)}) custom-call(s32[2]{0:T(128)} %len_ref.1, bf16[256,512]{1,0:T(8,128)(2,1)} %bitcast.19, bf16[256,512]{1,0:T(8,128)(2,1)} %bitcast.20, ...), custom_call_target="tpu_custom_call" | custom-call | tf_op jit(solution)/shard_map/layer/pallas_call | solution.py:1459
  87.8 3.4 %unpack.1 = (bf16[256,512]{1,0:T(8,128)(2,1)}, f32[256,512]{1,0:T(8,128)}, f32[1,128]{1,0:T(1,128)}, f32[1,128]{1,0:T(1,128)}, f32[128,128]{1,0:T(8,128)}, /*ind...) custom-call(bf16[256,512]{1,0:T(8,128)(2,1)} %get-tuple-element.34.r, ...), custom_call_target="tpu_custom_call" | custom-call | tf_op jit(solution)/shard_map/unpack/pallas_call | solution.py:1504

commit v6 on v5

--- a/solution.py
+++ b/solution.py
@@ -627,8 +627,6 @@
         wqs[k][z, :, 0:split] = wq_st[:, k * split : (k + 1) * split].astype(BF16)
     padded = jnp.concatenate([wr_st[...], jnp.zeros((128 - E, ws), F32)], axis=0)
     wqs[1][z, :, split:] = padded.T.astype(BF16)
-    for one in gather_q:
-        one.start()
 
     loads[id(x_ref)].wait()
     x = x_ref[...].astype(F32)
@@ -651,6 +649,8 @@
             wc[k, z, first : first + ws, at : at + UNIT] = wi_st[
                 :, s * fs + k * UNIT : s * fs + (k + 1) * UNIT
             ].astype(BF16)
+    for one in gather_q:
+        one.start()
     gather_k.begin()
     net.wait(vec_slot, vecs.at[0 : shards - 1])
 
@@ -1174,20 +1174,20 @@
     do_choose()
     gc0.pass_on()
     find_tops(1)
-    go.share()
     gc1.pass_on()
     weigh(1)
-    gc0.share()
+    go.share()
     gc2.pass_on()
     find_tops(0)
     weigh(0)
-    gc1.share()
+    gc0.share()
     do_mix()
     go.end()
     do_project()
-    gc2.share()
+    gc1.share()
     gc0.end()
     feed_all(0)
+    gc2.share()
     rc0.to(START)
     gc3.begin()
     gc3.pass_on()

time: 91.5 us -> 90.6 us (level)
  no operation moved by 1% of the time
where the time goes in v6:
time: 90.6 us; the launch traced here: 90.5 us
  Pallas kernels  89.7 us (99%)
    pallas_call x1, Pallas kernels, on_device(): pl.pallas_call(functools.partial(layer_kernel, shards, ctxs, group, chunk...  86.3 us
    pallas_call x1, Pallas kernels, on_device(): pl.pallas_call(functools.partial(unpack_kernel, shards), out_shape=shapes...  3.38 us

profile of v6, /device:TPU:0, one launch (start us, length us, event | category | flops | bytes accessed | tf_op | source)
XLA Modules:
  0.0 90.5 jit_solution(14501743200164348374)
XLA Ops:
  0.7 86.3 %layer.1 = (bf16[256,512]{1,0:T(8,128)(2,1)}, f32[256,512]{1,0:T(8,128)}, bf16[4,256,512]{2,1,0:T(8,128)(2,1)}, bf16[384,512]{1,0:T(8,128)(2,1)}, bf16[128,1536]{1,0:T(8,128)(2,1)}, /*index=5*/bf16[128,256]{1,0:T(8,128)(2,1)}) custom-call(s32[2]{0:T(128)} %len_ref.1, bf16[256,512]{1,0:T(8,128)(2,1)} %bitcast.19, bf16[256,512]{1,0:T(8,128)(2,1)} %bitcast.20, ...), custom_call_target="tpu_custom_call" | custom-call | tf_op jit(solution)/shard_map/layer/pallas_call | solution.py:1459
  86.9 3.4 %unpack.1 = (bf16[256,512]{1,0:T(8,128)(2,1)}, f32[256,512]{1,0:T(8,128)}, f32[1,128]{1,0:T(1,128)}, f32[1,128]{1,0:T(1,128)}, f32[128,128]{1,0:T(8,128)}, /*ind...) custom-call(bf16[256,512]{1,0:T(8,128)(2,1)} %get-tuple-element.34.r, ...), custom_call_target="tpu_custom_call" | custom-call | tf_op jit(solution)/shard_map/unpack/pallas_call | solution.py:1504

commit v7 on v6

--- a/solution.py
+++ b/solution.py
@@ -471,7 +471,7 @@
     ctxs,
     group,
     chunk_far,
-    len_ref,
+    len_hbm,
     x_hbm,
     cot_hbm,
     picks_hbm,
@@ -493,6 +493,7 @@
     wo_hbm_out,
     q_hbm,
     kv_hbm,
+    len_ref,
     x_ref,
     cot_ref,
     picks_ref,
@@ -584,14 +585,14 @@
     for at, (src, dst) in enumerate(
         (
             (wkv_hbm, wkv_st),
-            (wr_hbm, wr_st),
-            (wq_hbm, wq_st),
             (g1_hbm, g1_ref),
             (b1_hbm, b1_ref),
             (g2_hbm, g2_ref),
             (b2_hbm, b2_ref),
             (bo_hbm, bo_ref),
             (bi_hbm, bi_ref),
+            (wr_hbm, wr_st),
+            (wq_hbm, wq_st),
             (x_hbm, x_ref),
             (picks_hbm, picks_ref),
             (wo_hbm, wo_st),
@@ -602,6 +603,8 @@
     ):
         loads[id(dst)] = local(src, dst, at)
         loads[id(dst)].start()
+    load_len = local(len_hbm, len_ref, 22 + chunks)
+    load_len.start()
     loads[id(wkv_st)].wait()
     wk[z] = wkv_st[...].astype(BF16)
     vec_st[...] = jnp.zeros(vec_st.shape, F32)
@@ -652,6 +655,7 @@
     for one in gather_q:
         one.start()
     gather_k.begin()
+    load_len.wait()
     net.wait(vec_slot, vecs.at[0 : shards - 1])
 
     vec_all = [vecs[s].astype(F32) for s in range(shards)]
@@ -1398,10 +1402,10 @@
         jax.ShapeDtypeStruct((ws, 256), BF16),
     )
 
-    smem = pl.BlockSpec(memory_space=pltpu.SMEM)
     anywhere = pl.BlockSpec(memory_space=pl.ANY)
     arrivals = 2 + (3 + chunks) * 5 + 1 + 4 + (4 + chunks) * (8 + rounds + shards.bit_length() - 1)
     scratch = [
+        pltpu.SMEM(lengths.shape, jnp.int32),
         pltpu.VMEM((count, width), BF16),
         pltpu.VMEM((count, width), BF16),
         pltpu.VMEM((slots, TOP, seg), jnp.int32),
@@ -1452,14 +1456,14 @@
         [pltpu.VMEM((ws, wide // 2), BF16) for _ in range(2)],
         pltpu.VMEM((ws, 256), BF16),
         pltpu.VMEM((128, width), F32),
-        pltpu.SemaphoreType.DMA((22 + chunks,)),
+        pltpu.SemaphoreType.DMA((23 + chunks,)),
         pltpu.SemaphoreType.DMA((RING,)),
         pltpu.SemaphoreType.DMA((arrivals,)),
     ]
     results = pl.pallas_call(
         functools.partial(layer_kernel, shards, ctxs, group, chunk_far),
         out_shape=shapes_mid,
-        in_specs=[smem] + [anywhere] * 15,
+        in_specs=[anywhere] * 16,
         out_specs=tuple([anywhere] * 6),
         scratch_shapes=scratch,
         compiler_params=pltpu.CompilerParams(

time: 90.6 us -> 90 us (level)
  no operation moved by 1% of the time
where the time goes in v7:
time: 90 us; the launch traced here: 89.6 us
  Pallas kernels  88.8 us (99%)
    pallas_call x1, Pallas kernels, on_device(): pl.pallas_call(functools.partial(layer_kernel, shards, ctxs, group, chunk...  85.4 us
    pallas_call x1, Pallas kernels, on_device(): pl.pallas_call(functools.partial(unpack_kernel, shards), out_shape=shapes...  3.38 us

profile of v7, /device:TPU:0, one launch (start us, length us, event | category | flops | bytes accessed | tf_op | source)
XLA Modules:
  0.0 89.6 jit_solution(13822717391840202240)
XLA Ops:
  0.7 85.4 %layer.1 = (bf16[256,512]{1,0:T(8,128)(2,1)}, f32[256,512]{1,0:T(8,128)}, bf16[4,256,512]{2,1,0:T(8,128)(2,1)}, bf16[384,512]{1,0:T(8,128)(2,1)}, bf16[128,1536]{1,0:T(8,128)(2,1)}, /*index=5*/bf16[128,256]{1,0:T(8,128)(2,1)}) custom-call(s32[2]{0:T(128)} %len_hbm.1, bf16[256,512]{1,0:T(8,128)(2,1)} %bitcast.19, bf16[256,512]{1,0:T(8,128)(2,1)} %bitcast.20, ...), custom_call_target="tpu_custom_call" | custom-call | tf_op jit(solution)/shard_map/layer/pallas_call | solution.py:1463
  86.1 3.4 %unpack.1 = (bf16[256,512]{1,0:T(8,128)(2,1)}, f32[256,512]{1,0:T(8,128)}, f32[1,128]{1,0:T(1,128)}, f32[1,128]{1,0:T(1,128)}, f32[128,128]{1,0:T(8,128)}, /*ind...) custom-call(bf16[256,512]{1,0:T(8,128)(2,1)} %get-tuple-element.34.r, ...), custom_call_target="tpu_custom_call" | custom-call | tf_op jit(solution)/shard_map/unpack/pallas_call | solution.py:1508

commit v8 on v7

--- a/solution.py
+++ b/solution.py
@@ -1238,9 +1238,9 @@
     rk.to(START)
     do_gin()
     rk.to(CORE)
+    ro.to(NEAR_B)
     rc0.to(FAR_1)
     rc1.to(FAR_1)
-    ro.to(NEAR_B)
     rq0.to(NEAR_A)
     rq1.to(NEAR_A)
     rc2.to(FAR_0)

time: 90 us -> 89.7 us (level)
  no operation moved by 1% of the time
where the time goes in v8:
time: 89.7 us; the launch traced here: 89.5 us
  Pallas kernels  88.7 us (99%)
    pallas_call x1, Pallas kernels, on_device(): pl.pallas_call(functools.partial(layer_kernel, shards, ctxs, group, chunk...  85.3 us
    pallas_call x1, Pallas kernels, on_device(): pl.pallas_call(functools.partial(unpack_kernel, shards), out_shape=shapes...  3.38 us

profile of v8, /device:TPU:0, one launch (start us, length us, event | category | flops | bytes accessed | tf_op | source)
XLA Modules:
  0.0 89.5 jit_solution(9325910928682468346)
XLA Ops:
  0.7 85.3 %layer.1 = (bf16[256,512]{1,0:T(8,128)(2,1)}, f32[256,512]{1,0:T(8,128)}, bf16[4,256,512]{2,1,0:T(8,128)(2,1)}, bf16[384,512]{1,0:T(8,128)(2,1)}, bf16[128,1536]{1,0:T(8,128)(2,1)}, /*index=5*/bf16[128,256]{1,0:T(8,128)(2,1)}) custom-call(s32[2]{0:T(128)} %len_hbm.1, bf16[256,512]{1,0:T(8,128)(2,1)} %bitcast.19, bf16[256,512]{1,0:T(8,128)(2,1)} %bitcast.20, ...), custom_call_target="tpu_custom_call" | custom-call | tf_op jit(solution)/shard_map/layer/pallas_call | solution.py:1463
  86.0 3.4 %unpack.1 = (bf16[256,512]{1,0:T(8,128)(2,1)}, f32[256,512]{1,0:T(8,128)}, f32[1,128]{1,0:T(1,128)}, f32[1,128]{1,0:T(1,128)}, f32[128,128]{1,0:T(8,128)}, /*ind...) custom-call(bf16[256,512]{1,0:T(8,128)(2,1)} %get-tuple-element.34.r, ...), custom_call_target="tpu_custom_call" | custom-call | tf_op jit(solution)/shard_map/unpack/pallas_call | solution.py:1508

commit v9 on v8

--- a/solution.py
+++ b/solution.py
@@ -191,10 +191,12 @@
 
 
 class Gather:
-    def __init__(self, net, buf, by_core=False):
+    def __init__(self, net, buf, by_core=False, straight=False):
         self.net, self.buf, self.by_core = net, buf, by_core
         planes = [buf.at[net.src(k)] for k in range(1, net.shards)]
-        self.spread = Spread(net, planes, lambda rows: buf.at[0 : net.shards - 1, rows])
+        self.spread = Spread(
+            net, planes, lambda rows: buf.at[0 : net.shards - 1, rows], False, straight
+        )
         self.rows = self.spread.block(net.core) if by_core else self.spread.part(net.chip)
 
     def start(self):
@@ -618,7 +620,7 @@
     own_vec[...] = vec_st[...].astype(BF16)
     net.greeted()
     gather_k, gather_o = Gather(net, wk, True), Gather(net, wo)
-    gather_q = [Gather(net, one) for one in wqs]
+    gather_q = [Gather(net, one, False, k == 1) for k, one in enumerate(wqs)]
     gather_c = [Gather(net, wc.at[k], k == chunks - 1) for k in range(chunks)]
     gather_k.start()
     vec_slot = net.arrival()

time: 89.7 us -> 89.6 us (level)
  no operation moved by 1% of the time
where the time goes in v9:
time: 89.6 us; the launch traced here: 89.4 us
  Pallas kernels  88.6 us (99%)
    pallas_call x1, Pallas kernels, on_device(): pl.pallas_call(functools.partial(layer_kernel, shards, ctxs, group, chunk...  85.2 us
    pallas_call x1, Pallas kernels, on_device(): pl.pallas_call(functools.partial(unpack_kernel, shards), out_shape=shapes...  3.38 us

profile of v9, /device:TPU:0, one launch (start us, length us, event | category | flops | bytes accessed | tf_op | source)
XLA Modules:
  0.0 89.4 jit_solution(13343863193757897740)
XLA Ops:
  0.7 85.2 %layer.1 = (bf16[256,512]{1,0:T(8,128)(2,1)}, f32[256,512]{1,0:T(8,128)}, bf16[4,256,512]{2,1,0:T(8,128)(2,1)}, bf16[384,512]{1,0:T(8,128)(2,1)}, bf16[128,1536]{1,0:T(8,128)(2,1)}, /*index=5*/bf16[128,256]{1,0:T(8,128)(2,1)}) custom-call(s32[2]{0:T(128)} %len_hbm.1, bf16[256,512]{1,0:T(8,128)(2,1)} %bitcast.19, bf16[256,512]{1,0:T(8,128)(2,1)} %bitcast.20, ...), custom_call_target="tpu_custom_call" | custom-call | tf_op jit(solution)/shard_map/layer/pallas_call | solution.py:1465
  85.9 3.4 %unpack.1 = (bf16[256,512]{1,0:T(8,128)(2,1)}, f32[256,512]{1,0:T(8,128)}, f32[1,128]{1,0:T(1,128)}, f32[1,128]{1,0:T(1,128)}, f32[128,128]{1,0:T(8,128)}, /*ind...) custom-call(bf16[256,512]{1,0:T(8,128)(2,1)} %get-tuple-element.34.r, ...), custom_call_target="tpu_custom_call" | custom-call | tf_op jit(solution)/shard_map/unpack/pallas_call | solution.py:1510
